TPU v7x, 256 devices: a whole 4x4x8 slice. The times are simulated.
256 devices in a mesh: seq: 32 (over x, z), ch: 8 (over y, core).
Axes of the slice: x: 4, y: 4, z: 8, core: 2. Of those that a mesh axis runs over, the one named last changes fastest.
Arguments:
- features: bfloat16 [32768, 1024], P('seq', 'ch'), may hold values from -6 to 6
- w_qkv: bfloat16 [1024, 3072], P('ch'), may hold values from -0.1875 to 0.1875
- log_gate: float32 [8, 32768], P(None, ('seq', 'ch')), may hold values from -1 to 0
- norm_gain: float32 [1024], replicated, may hold values from 0.1 to 1.9
- w_pred: bfloat16 [4, 1024, 1024], replicated, may hold values from -0.1875 to 0.1875
- patch_mask: int32 [32768], P(('seq', 'ch')), may hold values 0 or 1
- neg_index: int32 [4, 256], P(None, ('seq', 'ch')), may hold values from 0 to 32767, as said below
Outputs:
- context: bfloat16 [32768, 1024], P(('seq', 'ch'))
- nce_loss: float32 [4, 32768], P(None, ('seq', 'ch'))
Inputs may be any that keep to these rules, and one draw needn't show every extreme that they name: `neg_index`: negative n of every offset lies among the 128 patches of block n, blocks of 128 consecutive patches.
All inputs are finite; a program needn't handle non-finite values. No bound on the sum of `patch_mask` on one device may be relied on, other than what follows from the above.
Results may differ from a plain program's by a relative error of at most 0.0061.
Values may be sent and summed in bfloat16 or wider, within the bound.
No kernel may reach another device: no remote copies, remote signals or barrier semaphores. Data moves between devices by JAX's collectives and lax.ppermute only.
A program may use at most 320 MiB of HBM per device.

v0:
```python
import jax
import jax.numpy as jnp
from jax import lax
from jax.sharding import PartitionSpec as P

CIN = 1024
HEADS = 8
HEAD_DIM = 128
K = 4


norm_eps = 1e-06


def prefix(part, axis, combine, identity):
    place = lax.axis_index(axis)
    gathered = jax.tree.map(lambda a: lax.all_gather(a, axis), part)
    state = jax.tree.map(lambda a, e: jnp.zeros_like(a) + jnp.asarray(e, a.dtype), part, identity)

    def one(turn, state):
        return combine(
            state, jax.tree.map(lambda a: lax.dynamic_index_in_dim(a, turn, 0, False), gathered)
        )

    return lax.fori_loop(0, place, one, state)


def shifted(x, axis, by):
    length = lax.axis_size(axis)
    pairs = [(i, i + by) for i in range(length) if 0 <= i + by < length]
    return lax.ppermute(x, axis, pairs)


def combine_states(earlier, later):
    return (earlier[0] * later[0], later[0][:, None, None] * earlier[1] + later[1])


def shards(features, w_qkv, log_gate, norm_gain, w_pred, patch_mask, neg_index):
    groups = lax.axis_size("ch")
    length = features.shape[0] // groups
    row_width = length // 2
    inner = HEADS * HEAD_DIM
    highest = lax.Precision.HIGHEST
    score_scale = 4.0 * CIN ** (-0.5)
    encoded = lax.all_to_all(features, "ch", split_axis=0, concat_axis=1, tiled=True)
    projected = jnp.dot(
        encoded, lax.all_gather(w_qkv, "ch", axis=0, tiled=True), preferred_element_type=jnp.float32
    )
    projected = projected.astype(jnp.bfloat16)
    mask_wire = patch_mask.astype(jnp.bfloat16)
    maskf = patch_mask.astype(jnp.float32)
    queries = projected[:, :inner].astype(jnp.float32).reshape(length, HEADS, HEAD_DIM)
    keys_local = (
        projected[:, inner : 2 * inner].astype(jnp.float32).reshape(length, HEADS, HEAD_DIM)
    )
    values = (
        (projected[:, 2 * inner :] * mask_wire[:, None])
        .astype(jnp.float32)
        .reshape(length, HEADS, HEAD_DIM)
    )
    cumul = jnp.cumsum(log_gate, axis=1)
    lower = jnp.arange(length)[:, None] >= jnp.arange(length)[None, :]
    scores = jnp.einsum("thd,shd->hts", queries, keys_local, precision=highest)
    diff = cumul[:, :, None] - cumul[:, None, :]
    decay = jnp.where(lower[None], jnp.exp(jnp.where(lower[None], diff, 0.0)), 0.0)
    intra = jnp.einsum("hts,shd->thd", scores * decay, values, precision=highest)
    tail = jnp.exp(cumul[:, -1:] - cumul)
    summary = jnp.einsum("shd,she->hde", keys_local * tail.T[:, :, None], values, precision=highest)
    block_decay = jnp.exp(cumul[:, -1])
    identity = (
        jnp.ones((HEADS,), jnp.float32),
        jnp.zeros((HEADS, HEAD_DIM, HEAD_DIM), jnp.float32),
    )
    incoming = prefix((block_decay, summary), ("seq", "ch"), combine_states, identity)
    inter = (
        jnp.einsum("thd,hde->the", queries, incoming[1], precision=highest)
        * jnp.exp(cumul).T[:, :, None]
    )
    mixed = (intra + inter) * HEAD_DIM ** (-0.5)
    squares = jnp.mean(mixed * mixed, axis=-1, keepdims=True)
    normed = (mixed / jnp.sqrt(squares + norm_eps)).reshape(length, inner)
    context = (normed * norm_gain).astype(jnp.bfloat16)
    predicted = jnp.einsum(
        "td,kdc->ktc", context, w_pred, preferred_element_type=jnp.float32
    ).astype(jnp.bfloat16)
    base_row = lax.axis_index(("seq", "ch")) * length
    local_index = neg_index - base_row
    owned = jnp.take(encoded, local_index, axis=0)
    logits = (
        jnp.einsum(
            "ktc,kjc->ktj",
            predicted,
            lax.all_gather(owned, ("seq", "ch"), axis=1, tiled=True),
            preferred_element_type=jnp.float32,
        )
        * score_scale
    )
    negsum = jnp.sum(jnp.exp(logits), axis=2)
    ahead_rows = [encoded]
    ahead_mask = [mask_wire]
    for distance in (1, 2):
        target_rows, target_flags = shifted((encoded, mask_wire), ("seq", "ch"), -distance)
        ahead_rows.append(target_rows)
        ahead_mask.append(target_flags)
    ahead_rows = jnp.concatenate(ahead_rows, axis=0)
    ahead_mask = jnp.concatenate(ahead_mask, axis=0)
    losses = []
    for offset in range(1, K + 1):
        begin = offset * row_width
        target = ahead_rows[begin : begin + length]
        target_mask = ahead_mask[begin : begin + length]
        positive = (
            jnp.einsum(
                "tc,tc->t", predicted[offset - 1], target, preferred_element_type=jnp.float32
            )
            * score_scale
        )
        valid = maskf * target_mask.astype(jnp.float32)
        losses.append(valid * (jnp.log(jnp.exp(positive) + negsum[offset - 1]) - positive))
    return (context, jnp.stack(losses, axis=0))


def solution(mesh):
    placed = (
        P("seq", "ch"),
        P("ch", None),
        P(None, ("seq", "ch")),
        P(),
        P(),
        P(("seq", "ch")),
        P(None, ("seq", "ch")),
    )
    return jax.shard_map(
        shards,
        mesh=mesh,
        in_specs=placed,
        out_specs=(P(("seq", "ch"), None), P(None, ("seq", "ch"))),
        check_vma=False,
    )
```

profile of v0, /device:TPU:255, one launch (start us, length us, event | category | flops | bytes accessed | tf_op | source)
XLA Modules:
  0.0 740.3 jit_solution(8675403109615047747)
XLA Ops:
  7.9 5.0 all-to-all-start
  14.8 2.9 all-to-all-done
  17.7 34.2 %all-gather.6.cloned.1.call-done = bf16[1024,3072]{1,0:T(8,128)(2,1)} async-done(((bf16[128,3072]{1,0:T(8,128)(2,1)}), bf16[1024,3072]{1,0:T(8,128)(2,1)}) %all-gather.6.cloned.1.call-update) | async-done | bytes 6291472 | tf_op jit(solution)/shard_map/all_gather | solution.py:47
  51.8 3.8 convolution_convert_fusion
  56.0 1.2 fusion.19
  58.6 2.2 collective-permute-start
  60.8 3.2 collective-permute-start.2
  64.2 76.9 %all-reduce = f32[2048]{0:T(1024)S(1)} all-reduce(f32[2048]{0:T(1024)S(1)} %dynamic-update-slice), channel_id=2, replica_groups=mesh['seq'=32,'ch'=8] {'seq','ch'}, use_global_device_ids=true, to_apply=%add | all-reduce | flops 2048 | bytes 16384
  141.3 3.1 collective-permute-start.1
  144.4 2.4 collective-permute-start.3
  147.1 260.4 %all-gather.10.cloned.1.call-done = f32[2048,128,128]{2,1,0:T(8,128)} async-done(((f32[8,128,128]{2,1,0:T(8,128)}), f32[2048,128,128]{2,1,0:T(8,128)}) %all-gather.10.cloned.1.call-update) | async-done | bytes 134217744 | tf_op jit(solution)/shard_map/all_gather | solution.py:17
  407.5 316.1 %while.12 = (s32[]{:T(128)}, f32[8,128,128]{2,1,0:T(8,128)S(1)}, s32[]{:T(128)}, f32[256,8]{1,0:T(8,128)S(1)}, f32[256,8,128,128]{3,2,1,0:T(8,128)}, /*index=5*/s32[]{:T(128)}, s32[]{:T(128)}, s32[]{:T(128)}) while((s32[]{:T(128)}, f32[8,128,128]{2,1,0:T(8,128)S(1)}, s32[]{:T(128)}, f32[256,8]{1,0:T(8,128)S(1)}, ...), condition=%wide.region_2.3_spmd, body=%wide.region_1.2_spmd.sunk | while | flops 262149 | bytes 1573087 | solution.py:25
  408.8 1.2 bitcast_add_fusion.6
  418.7 1.2 bitcast_add_fusion.6
  422.4 1.2 bitcast_add_fusion.6
  423.7 1.2 bitcast_add_fusion.6
  424.9 1.2 bitcast_add_fusion.6
  426.2 1.2 bitcast_add_fusion.6
  436.1 1.2 bitcast_add_fusion.6
  439.8 1.2 bitcast_add_fusion.6
  446.0 1.2 bitcast_add_fusion.6
  449.7 1.2 bitcast_add_fusion.6
  457.1 1.2 bitcast_add_fusion.6
  459.6 1.2 bitcast_add_fusion.6
  462.1 1.2 bitcast_add_fusion.6
  464.6 1.2 bitcast_add_fusion.6
  465.8 1.2 bitcast_add_fusion.6
  469.5 1.2 bitcast_add_fusion.6
  479.5 1.2 bitcast_add_fusion.6
  483.2 1.2 bitcast_add_fusion.6
  489.4 1.2 bitcast_add_fusion.6
  498.1 1.3 bitcast_add_fusion.6
  500.6 1.2 bitcast_add_fusion.6
  509.3 1.2 bitcast_add_fusion.6
  513.0 1.2 bitcast_add_fusion.6
  519.2 1.2 bitcast_add_fusion.6
  522.9 1.2 bitcast_add_fusion.6
  532.8 1.2 bitcast_add_fusion.6
  536.6 1.2 bitcast_add_fusion.6
  542.8 1.2 bitcast_add_fusion.6
  546.5 1.2 bitcast_add_fusion.6
  556.4 1.2 bitcast_add_fusion.6
  560.1 1.2 bitcast_add_fusion.6
  566.3 1.2 bitcast_add_fusion.6
  570.0 1.2 bitcast_add_fusion.6
  579.9 1.2 bitcast_add_fusion.6
  725.3 4.8 fusion.2
  730.1 2.6 fusion.12
  (522 shorter events, 273.9 us)
Async XLA Ops:
  7.2 44.7 %all-gather.6.cloned.1.call-start = ((), (), s32[]{:S(2)}) async-start(), calls=%async_computation.1 | async-start | bytes 7077888 | tf_op jit(solution)/shard_map/all_gather | solution.py:47
  7.9 9.8 %all-to-all-start = ((bf16[8,128,128]{2,1,0:T(8,128)(2,1)}), bf16[8,128,128]{2,1,0:T(8,128)(2,1)S(1)}, u32[]{:S(2)}, u32[]{:S(2)}) async-start(bf16[8,128,128]{2,1,0:T(8,128)(2,1)} %bitcast.135), calls=%async_computation | async-start | bytes 524288 | tf_op jit(solution)/shard_map/all_to_all | solution.py:45
  12.9 394.6 %all-gather.10.cloned.1.call-start = ((), (), s32[]{:S(2)}) async-start(), calls=%async_computation.3 | async-start | bytes 134742016 | tf_op jit(solution)/shard_map/all_gather | solution.py:17
  14.8 42.5 %copy-start.3 = (s32[4,1]{0,1:T(1,128)S(1)}, s32[4,1]{0,1:T(1,128)}, u32[]{:S(2)}) copy-start(s32[4,1]{0,1:T(1,128)} %param.15) | copy-start | bytes 52
  57.2 672.9 %all-gather.8.cloned.1.call-start = ((), (), s32[]{:S(2)}) async-start(), calls=%async_computation.2 | async-start | bytes 2105344 | tf_op jit(solution)/shard_map/all_gather | solution.py:93
  58.6 82.7 %collective-permute-start = (bf16[128]{0:T(256)(128)(2,1)S(1)}, bf16[128]{0:T(256)(128)(2,1)S(1)}, u32[]{:S(2)}, u32[]{:S(2)}) collective-permute-start(bf16[128]{0:T(256)(128)(2,1)S(1)} %convert_element_type.34), channel_id=1, source_target_pairs={{1,0},{2,1},{3,2},{4,3},{5,4},{6,5},{7,6},{8,7},{9,8},{10,9},{11,1... | collective-permute-start | bytes 776 | tf_op jit(solution)/shard_map/ppermute | solution.py:31
  60.8 80.5 %collective-permute-start.2 = (bf16[128]{0:T(256)(128)(2,1)S(1)}, bf16[128]{0:T(256)(128)(2,1)S(1)}, u32[]{:S(2)}, u32[]{:S(2)}) collective-permute-start(bf16[128]{0:T(256)(128)(2,1)S(1)} %convert_element_type.34), channel_id=1, source_target_pairs={{2,0},{3,1},{4,2},{5,3},{6,4},{7,5},{8,6},{9,7},{10,8},{11,9},{12,... | collective-permute-start | bytes 776 | tf_op jit(solution)/shard_map/ppermute | solution.py:31
  141.3 591.4 %collective-permute-start.1 = (bf16[128,1024]{1,0:T(8,128)(2,1)S(1)}, bf16[128,1024]{1,0:T(8,128)(2,1)S(1)}, u32[]{:S(2)}, u32[]{:S(2)}) collective-permute-start(bf16[128,1024]{1,0:T(8,128)(2,1)S(1)} %copy_bitcast_fusion), channel_id=1, source_target_pairs={{1,0},{2,1},{3,2},{4,3},{5,4},{6,5},{7,6},{8,7},{9,8},{10,9},{11,1... | collective-permute-start | bytes 786440 | tf_op jit(solution)/shard_map/ppermute | solution.py:31
  144.4 588.3 %collective-permute-start.3 = (bf16[128,1024]{1,0:T(8,128)(2,1)S(1)}, bf16[128,1024]{1,0:T(8,128)(2,1)S(1)}, u32[]{:S(2)}, u32[]{:S(2)}) collective-permute-start(bf16[128,1024]{1,0:T(8,128)(2,1)S(1)} %copy_bitcast_fusion), channel_id=1, source_target_pairs={{2,0},{3,1},{4,2},{5,3},{6,4},{7,5},{8,6},{9,7},{10,8},{11,9},{12,... | collective-permute-start | bytes 786440 | tf_op jit(solution)/shard_map/ppermute | solution.py:31
  407.5 317.7 %copy-start.1 = (f32[1024]{0:T(1024)S(1)}, f32[1024]{0:T(1024)}, u32[]{:S(2)}) copy-start(f32[1024]{0:T(1024)} %param.12) | copy-start | bytes 12292
  725.3 7.4 %copy-start = (bf16[128,1024]{1,0:T(8,128)(2,1)}, bf16[128,1024]{1,0:T(8,128)(2,1)S(1)}, u32[]{:S(2)}) copy-start(bf16[128,1024]{1,0:T(8,128)(2,1)S(1)} %multiply_convert_fusion) | copy-start | bytes 786436
  725.3 7.8 %copy-start.2 = (s32[128]{0:T(128)S(1)}, s32[128]{0:T(128)}, u32[]{:S(2)}) copy-start(s32[128]{0:T(128)} %param.14) | copy-start | bytes 1540
Sparse Core Ops, SparseCore 0:
  9.8 42.0 all-gather.5
  57.3 350.1 all-gather.9
  411.2 104.2 all-gather.7
where the time goes:
time: 753 us; the launch traced here: 740 us
  other arithmetic  308 us (41%)
  waiting for transfers between devices  298 us (40%)
  blocking collectives  76.9 us (10%)
  starting transfers between devices  15.9 us (2%)
  matrix products  14 us (2%)
  between operations  14 us (2%)
  loops' own time  9 us (1%)
    add x255, other arithmetic, combine_states(): later[0][:, None, None] * earlier[1] + later[1]  305 us
    all_gather x1, waiting for transfers between devices, prefix(): gathered = jax.tree.map(lambda a: lax.all_gather(a, axis), part)  260 us
    unnamed x1, blocking collectives  76.9 us
    all_gather x1, waiting for transfers between devices, shards(): lax.all_gather(w_qkv, 'ch', axis=0, tiled=True)  34.2 us
  transfers between devices with their start and end apart: 8, of which 3 were waited for; matrix products, arithmetic and copies ran while one was open for 43% of the time, Pallas kernels for 0%

commit v1 on v0

v1 whole, which is shorter than its diff:
```python
import jax
import jax.numpy as jnp
from jax import lax
from jax.sharding import PartitionSpec as P

CIN = 1024
HEADS = 8
HEAD_DIM = 128
K = 4
ROW = 64
NORM_EPS = 1e-06
F32 = jnp.float32
BF16 = jnp.bfloat16
BOTH = ("seq", "ch")


def exchange(x, axis, groups=None):
    return lax.all_to_all(x, axis, split_axis=0, concat_axis=0, axis_index_groups=groups)


def collect(x, axis, size, groups=None):
    return exchange(jnp.broadcast_to(x[None], (size,) + x.shape), axis, groups)


def shards(features, w_qkv, log_gate, norm_gain, w_pred, patch_mask, neg_index):
    nseq, nch = lax.axis_size("seq"), lax.axis_size("ch")
    block = features.shape[0]
    length = block // nch
    xs, zs = 4, nseq // 4
    along_z = [[x * zs + z for z in range(zs)] for x in range(xs)]
    along_x = [[x * zs + z for x in range(xs)] for z in range(zs)]
    seq_at, ch_at = lax.axis_index("seq"), lax.axis_index("ch")
    x_at, z_at = seq_at // zs, seq_at % zs
    score_scale = 4.0 * CIN ** (-0.5)

    place = neg_index[:, 0] - seq_at * block
    small = jnp.concatenate(
        [
            log_gate[:, None, :],
            jnp.broadcast_to(patch_mask.astype(F32)[None, None], (nch, 1, length)),
            jnp.broadcast_to(jnp.pad(place.astype(F32), (0, length - K))[None, None], (nch, 1, length)),
        ],
        axis=1,
    )
    small = exchange(small, "ch")
    gate = small[:, 0].reshape(block)
    mask = small[:, 1].reshape(block)
    rows = small[:, 2, :K].astype(jnp.int32)

    encoded = collect(features, "ch", nch)
    w_mine = exchange(
        w_qkv.reshape(w_qkv.shape[0], 3, nch, HEAD_DIM).transpose(2, 0, 1, 3).reshape(nch, w_qkv.shape[0], 3 * HEAD_DIM),
        "ch",
    )

    picked = jnp.take(features, rows.T.reshape(-1), axis=0).reshape(K, nch, -1)
    bank = collect(picked, "seq", nseq)
    bank = bank.transpose(1, 0, 2, 3).reshape(K, nseq * nch, -1)
    bank = collect(bank, "ch", nch)

    projected = jnp.einsum("ctk,ckn->tn", encoded, w_mine, preferred_element_type=F32).astype(BF16)
    queries = projected[:, :HEAD_DIM]
    keys = projected[:, HEAD_DIM : 2 * HEAD_DIM]
    values = projected[:, 2 * HEAD_DIM :] * mask.astype(BF16)[:, None]
    cumul = jnp.cumsum(gate)
    total = cumul[-1]
    tail = jnp.exp(total - cumul)
    summary = jnp.einsum(
        "sd,se->de", (keys.astype(F32) * tail[:, None]).astype(BF16), values, preferred_element_type=F32
    )
    totals = lax.all_to_all(
        jnp.broadcast_to(total, (nseq, 1, 128)), "seq", split_axis=0, concat_axis=0
    )[:, 0, 0].reshape(xs, zs)
    in_z = collect(summary.astype(BF16), "seq", zs, along_z)
    mine = lax.dynamic_index_in_dim(totals, x_at, 0, False)
    zi = jnp.arange(zs)
    below = zi[None, :] < zi[:, None]
    acc = jnp.cumsum(mine)
    before = jnp.concatenate([jnp.zeros((1,), F32), acc[:-1]])
    w_row = jnp.exp(acc[-1] - acc)
    w_here = jnp.where(zi < z_at, jnp.exp(jnp.where(zi < z_at, before[z_at] - acc, 0.0)), 0.0)
    both = jnp.einsum("wz,zde->wde", jnp.stack([w_row, w_here]), in_z.astype(F32), precision=lax.Precision.HIGHEST)
    in_x = collect(both[0].astype(BF16), "seq", xs, along_x)
    xi = jnp.arange(xs)
    row_acc = jnp.cumsum(jnp.sum(totals, axis=1))
    row_before = jnp.concatenate([jnp.zeros((1,), F32), row_acc[:-1]])
    w_x = jnp.where(
        xi < x_at, jnp.exp(jnp.where(xi < x_at, row_before[x_at] - row_acc, 0.0) + before[z_at]), 0.0
    )
    incoming = both[1] + jnp.einsum("x,xde->de", w_x, in_x.astype(F32), precision=lax.Precision.HIGHEST)

    lower = jnp.arange(block)[:, None] >= jnp.arange(block)[None, :]
    decay = jnp.where(lower, jnp.exp(jnp.where(lower, cumul[:, None] - cumul[None, :], 0.0)), 0.0)
    scores = jnp.einsum("td,sd->ts", queries, keys, preferred_element_type=F32)
    intra = jnp.einsum("ts,se->te", (scores * decay).astype(BF16), values, preferred_element_type=F32)
    inter = jnp.einsum("td,de->te", queries, incoming.astype(BF16), preferred_element_type=F32)
    mixed = (intra + inter * jnp.exp(cumul)[:, None]) * HEAD_DIM ** (-0.5)
    squares = jnp.mean(mixed * mixed, axis=-1, keepdims=True)
    gain = lax.dynamic_slice_in_dim(norm_gain, ch_at * HEAD_DIM, HEAD_DIM, 0)
    context = (mixed / jnp.sqrt(squares + NORM_EPS) * gain).astype(BF16)
    context = exchange(context.reshape(nch, length, HEAD_DIM), "ch")
    context = context.transpose(1, 0, 2).reshape(length, HEADS * HEAD_DIM)

    ahead = encoded[:, : K * ROW]
    ahead = jnp.concatenate(
        [ahead, jnp.broadcast_to(mask[: K * ROW].astype(BF16)[None, None], (nch, 1, K * ROW))[:, :, :128],
         jnp.broadcast_to(mask[: K * ROW].astype(BF16)[None, None], (nch, 1, K * ROW))[:, :, 128:]], axis=1)
    last = nch - 2
    pairs = [((s + 1) * nch + c, s * nch + c) for s in range(nseq - 1) for c in range(last, nch)]
    ahead = lax.ppermute(ahead, BOTH, pairs)
    mask_next = jnp.concatenate([ahead[0, K * ROW], ahead[0, K * ROW + 1]]).astype(F32)
    window = jnp.concatenate([encoded, ahead[:, : K * ROW]], axis=1)
    window = lax.dynamic_slice_in_dim(window, ch_at * length, length + K * ROW, 1)
    flags = lax.dynamic_slice_in_dim(
        jnp.concatenate([mask, mask_next]), ch_at * length, length + K * ROW, 0
    )

    losses = []
    for j in range(K):
        predicted = jnp.dot(context, w_pred[j], preferred_element_type=F32).astype(BF16)
        parts = predicted.reshape(length, nch, 128)
        logits = jnp.einsum("tck,cnk->tn", parts, bank[:, j], preferred_element_type=F32) * score_scale
        negsum = jnp.sum(jnp.exp(logits), axis=1)
        target = window[:, (j + 1) * ROW : (j + 1) * ROW + length]
        positive = (
            jnp.einsum("tck,ctk->t", parts.astype(F32), target.astype(F32)) * score_scale
        )
        valid = flags[:length] * flags[(j + 1) * ROW : (j + 1) * ROW + length]
        losses.append(valid * (jnp.log(jnp.exp(positive) + negsum) - positive))
    return (context, jnp.stack(losses, axis=0))


def solution(mesh):
    placed = (
        P("seq", "ch"),
        P("ch", None),
        P(None, BOTH),
        P(),
        P(),
        P(BOTH),
        P(None, BOTH),
    )
    return jax.shard_map(
        shards,
        mesh=mesh,
        in_specs=placed,
        out_specs=(P(BOTH, None), P(None, BOTH)),
        check_vma=False,
    )
```

time: 753 us -> 185 us (0.25)
  the two profiles are of different devices: /device:TPU:255 before, /device:TPU:1 now
where the time goes in v1:
time: 185 us; the launch traced here: 183 us
  waiting for transfers between devices  74.1 us (40%)
  starting transfers between devices  48.2 us (26%)
  matrix products  25.4 us (14%)
  local copies, waits for them, and re-layouts  16.5 us (9%)
  blocking collectives  10.4 us (6%)
  other arithmetic  7.79 us (4%)
    all_to_all x7, waiting for transfers between devices, exchange(): lax.all_to_all(x, axis, split_axis=0, concat_axis=0, axis_index_groups=gr...  69.2 us
    all_to_all x7, starting transfers between devices, exchange(): lax.all_to_all(x, axis, split_axis=0, concat_axis=0, axis_index_groups=gr...  35.7 us
    all_to_all x1, starting transfers between devices, shards(): lax.all_to_all(jnp.broadcast_to(total, (nseq, 1, 128)), 'seq', split_axis...  11 us
    all_to_all x1, blocking collectives, exchange(): lax.all_to_all(x, axis, split_axis=0, concat_axis=0, axis_index_groups=gr...  10.4 us
    dot_general x4, matrix products, shards(): jnp.dot(context, w_pred[j], preferred_element_type=F32).astype(BF16)  8.25 us
    dot_general x4, matrix products, shards(): jnp.einsum('tck,cnk->tn', parts, bank[:, j], preferred_element_type=F32)  5.75 us
    broadcast_in_dim x5, local copies, waits for them, and re-layouts, collect(): return exchange(jnp.broadcast_to(x[None], (size,) + x.shape), axis, groups)  5.54 us
    all_to_all x1, waiting for transfers between devices, shards(): lax.all_to_all(jnp.broadcast_to(total, (nseq, 1, 128)), 'seq', split_axis...  4.95 us
  transfers between devices with their start and end apart: 9, of which 8 were waited for; matrix products, arithmetic and copies ran while one was open for 16% of the time, Pallas kernels for 0%

profile of v1, /device:TPU:1, one launch (start us, length us, event | category | flops | bytes accessed | tf_op | source)
XLA Modules:
  0.0 183.4 jit_solution(2382345199942611162)
XLA Ops:
  0.6 0.7 convert_element_type.85
  1.3 0.7 convert_bitcast_fusion.1
  2.0 0.7 pad_maximum_fusion.1
  2.7 10.4 %all_to_all.45 = f32[8,3,128]{2,1,0:T(4,128)S(1)} all-to-all(f32[8,3,128]{2,1,0:T(4,128)S(1)} %pad_maximum_fusion.1), channel_id=1, replica_groups=mesh['seq'=32,'ch'=8] {'ch'}, dimensions={0} | all-to-all | bytes 24576 | tf_op jit(solution)/shard_map/all_to_all | solution.py:18
  14.3 1.3 broadcast_in_dim.56
  15.5 11.0 %all-to-all-start.3 = ((f32[32,1,128]{2,1,0:T(1,128)}), f32[32,1,128]{2,1,0:T(1,128)S(1)}, u32[]{:S(2)}, u32[]{:S(2)}) async-start(f32[32,1,128]{2,1,0:T(1,128)} %broadcast_in_dim.56), calls=%async_computation.3 | async-start | bytes 32768 | tf_op jit(solution)/shard_map/all_to_all | solution.py:71
  26.6 1.5 copy.65
  28.2 1.2 copy.67
  29.4 0.8 dynamic_slice.23
  30.2 4.9 %all-to-all-done.3 = f32[32,1,128]{2,1,0:T(1,128)S(1)} async-done(((f32[32,1,128]{2,1,0:T(1,128)}), f32[32,1,128]{2,1,0:T(1,128)S(1)}, u32[]{:S(2)}, u32[]{:S(2)}) %all-to-all-start.3) | async-done | bytes 16416 | tf_op jit(solution)/shard_map/all_to_all | solution.py:71
  35.2 5.6 %all-to-all-start.1 = ((bf16[8,128,384]{2,1,0:T(8,128)(2,1)}), bf16[8,128,384]{2,1,0:T(8,128)(2,1)S(1)}, u32[]{:S(2)}, u32[]{:S(2)}) async-start(bf16[8,128,384]{2,1,0:T(8,128)(2,1)} %copy.67), calls=%async_computation.1 | async-start | bytes 1572864 | tf_op jit(solution)/shard_map/all_to_all | solution.py:18
  41.5 11.5 %all-to-all-done.1 = bf16[8,128,384]{2,1,0:T(8,128)(2,1)S(1)} async-done(((bf16[8,128,384]{2,1,0:T(8,128)(2,1)}), bf16[8,128,384]{2,1,0:T(8,128)(2,1)S(1)}, u32[]{:S(2)}, u32[]{:S(2)}) %all-to-all-start.1) | async-done | bytes 786464 | tf_op jit(solution)/shard_map/all_to_all | solution.py:18
  52.9 1.6 broadcast_in_dim.51
  54.6 4.5 %all-to-all-start = ((bf16[8,1024,128]{2,1,0:T(8,128)(2,1)}), bf16[8,1024,128]{2,1,0:T(8,128)(2,1)S(1)}, u32[]{:S(2)}, u32[]{:S(2)}) async-start(bf16[8,1024,128]{2,1,0:T(8,128)(2,1)} %broadcast_in_dim.51), calls=%async_computation | async-start | bytes 4194304 | tf_op jit(solution)/shard_map/all_to_all | solution.py:18
  59.0 0.7 subtract_exponential_fusion
  61.9 0.7 compare_select_fusion.4
  62.6 22.7 %all-to-all-done = bf16[8,1024,128]{2,1,0:T(8,128)(2,1)S(1)} async-done(((bf16[8,1024,128]{2,1,0:T(8,128)(2,1)}), bf16[8,1024,128]{2,1,0:T(8,128)(2,1)S(1)}, u32[]{:S(2)}, u32[]{:S(2)}) %all-to-all-start) | async-done | bytes 2097184 | tf_op jit(solution)/shard_map/all_to_all | solution.py:18
  85.3 0.7 broadcast_in_dim.111
  86.0 3.9 %all-to-all-start.7 = ((bf16[32,4,8,128]{3,2,1,0:T(8,128)(2,1)}), bf16[32,4,8,128]{3,2,1,0:T(8,128)(2,1)S(1)}, u32[]{:S(2)}, u32[]{:S(2)}) async-start(bf16[32,4,8,128]{3,2,1,0:T(8,128)(2,1)} %broadcast_in_dim.111), calls=%async_computation.7 | async-start | bytes 524288 | tf_op jit(solution)/shard_map/all_to_all | solution.py:18
  89.9 2.1 %bitcast_convert_fusion = bf16[1024,384]{1,0:T(8,128)(2,1)} fusion(bf16[8,1024,128]{2,1,0:T(8,128)(2,1)S(1)} %all-to-all-done, bf16[8,128,384]{2,1,0:T(8,128)(2,1)S(1)} %all-to-all-done.1), kind=kOutput, calls=%fused_computation.17 | convolution fusion | flops 805699584 | bytes 3670016 | tf_op jit(solution)/shard_map/ctk,ckn->tn/dot_general | solution.py:61
  92.0 1.6 convolution_convert_fusion
  93.6 5.9 %all-to-all-done.7 = bf16[32,4,8,128]{3,2,1,0:T(8,128)(2,1)S(1)} async-done(((bf16[32,4,8,128]{3,2,1,0:T(8,128)(2,1)}), bf16[32,4,8,128]{3,2,1,0:T(8,128)(2,1)S(1)}, u32[]{:S(2)}, u32[]{:S(2)}) %all-to-all-start.7) | async-done | bytes 262176 | tf_op jit(solution)/shard_map/all_to_all | solution.py:18
  99.6 0.7 broadcast_in_dim.103
  100.3 4.7 %all-to-all-start.4 = ((bf16[8,128,128]{2,1,0:T(8,128)(2,1)}), bf16[8,128,128]{2,1,0:T(8,128)(2,1)S(1)}, u32[]{:S(2)}, u32[]{:S(2)}) async-start(bf16[8,128,128]{2,1,0:T(8,128)(2,1)} %broadcast_in_dim.103), calls=%async_computation.4 | async-start | bytes 524288 | tf_op jit(solution)/shard_map/all_to_all | solution.py:18
  105.0 0.6 dynamic_slice.22
  106.6 1.5 collective-permute-start
  108.0 6.4 %all-to-all-done.4 = bf16[8,128,128]{2,1,0:T(8,128)(2,1)S(1)} async-done(((bf16[8,128,128]{2,1,0:T(8,128)(2,1)}), bf16[8,128,128]{2,1,0:T(8,128)(2,1)S(1)}, u32[]{:S(2)}, u32[]{:S(2)}) %all-to-all-start.4) | async-done | bytes 262176 | tf_op jit(solution)/shard_map/all_to_all | solution.py:18
  114.9 0.7 broadcast_in_dim.106
  115.6 4.0 %all-to-all-start.5 = ((bf16[4,128,128]{2,1,0:T(8,128)(2,1)}), bf16[4,128,128]{2,1,0:T(8,128)(2,1)}, u32[]{:S(2)}, u32[]{:S(2)}) async-start(bf16[4,128,128]{2,1,0:T(8,128)(2,1)} %broadcast_in_dim.106), calls=%async_computation.5 | async-start | bytes 262144 | tf_op jit(solution)/shard_map/all_to_all | solution.py:18
  119.5 3.3 %fusion.12 = f32[1024,128]{1,0:T(8,128)} fusion(f32[1024]{0:T(1024)S(1)} %get-tuple-element.7, bf16[1024,384]{1,0:T(8,128)(2,1)} %bitcast_convert_fusion, bf16[1024]{0:T(1024)(128)(2,1)S(1)} %convert_element_type.89), kind=kOutput, calls=%fused_computation.18 | convolution fusion | flops 543293440 | bytes 1320960 | tf_op jit(solution)/shard_map/ts,se->te/dot_general | solution.py:95
  122.9 1.1 slice.201
  124.4 2.5 %fusion.59 = f32[1,128,128]{2,0,1:T(1,128)S(1)} fusion(bf16[4,128,128]{2,1,0:T(8,128)(2,1)} %all-to-all-done.5, f32[4,1]{0,1:T(1,128)S(1)} %reduce-window.24, f32[]{:T(128)} %bitcast.18, f32[]{:T(128)} %bitcast.24, s32[]{:T(128)S(6)} %select_n.89), kind=kOutput, calls=%fused_computation.80 | convolution fusion | flops 786452 | bytes 196636 | tf_op jit(solution)/shard_map/x,xde->de/dot_general | solution.py:90
  126.9 1.3 multiply_reduce_fusion.4
  128.3 0.9 multiply_convert_fusion.1
  129.2 7.9 %all-to-all-start.6 = ((bf16[8,128,128]{2,1,0:T(8,128)(2,1)}), bf16[8,128,128]{2,1,0:T(8,128)(2,1)S(1)}, u32[]{:S(2)}, u32[]{:S(2)}) async-start(bf16[8,128,128]{2,1,0:T(8,128)(2,1)} %bitcast.29), calls=%async_computation.6 | async-start | bytes 524288 | tf_op jit(solution)/shard_map/all_to_all | solution.py:18
  137.1 0.7 slice_bitcast_fusion.13
  137.8 5.8 %all-to-all-done.6 = bf16[8,128,128]{2,1,0:T(8,128)(2,1)S(1)} async-done(((bf16[8,128,128]{2,1,0:T(8,128)(2,1)}), bf16[8,128,128]{2,1,0:T(8,128)(2,1)S(1)}, u32[]{:S(2)}, u32[]{:S(2)}) %all-to-all-start.6) | async-done | bytes 262176 | tf_op jit(solution)/shard_map/all_to_all | solution.py:18
  143.6 1.8 broadcast_in_dim.113
  145.4 5.3 %all-to-all-start.8 = ((bf16[8,4,256,128]{3,2,1,0:T(8,128)(2,1)}), bf16[8,4,256,128]{3,2,1,0:T(8,128)(2,1)}, u32[]{:S(2)}, u32[]{:S(2)}) async-start(bf16[8,4,256,128]{3,2,1,0:T(8,128)(2,1)} %broadcast_in_dim.113), calls=%async_computation.8 | async-start | bytes 4194304 | tf_op jit(solution)/shard_map/all_to_all | solution.py:18
  151.1 2.1 %fusion.15 = bf16[128,1024]{1,0:T(8,128)(2,1)S(1)} fusion(bf16[128,1024]{1,0:T(8,128)(2,1)S(1)} %copy_bitcast_fusion, bf16[4,1024,1024]{2,1,0:T(8,128)(2,1)} %param.11), kind=kOutput, calls=%fused_computation.22 | convolution fusion | flops 268566528 | bytes 2621440 | tf_op jit(solution)/shard_map/dot_general | solution.py:120
  153.4 2.0 %fusion.21 = bf16[128,1024]{1,0:T(8,128)(2,1)S(1)} fusion(bf16[128,1024]{1,0:T(8,128)(2,1)S(1)} %copy_bitcast_fusion, bf16[4,1024,1024]{2,1,0:T(8,128)(2,1)} %param.11), kind=kOutput, calls=%fused_computation.24 | convolution fusion | flops 268566528 | bytes 2621440 | tf_op jit(solution)/shard_map/dot_general | solution.py:120
  155.5 2.0 %fusion.18 = bf16[128,1024]{1,0:T(8,128)(2,1)S(1)} fusion(bf16[128,1024]{1,0:T(8,128)(2,1)S(1)} %copy_bitcast_fusion, bf16[4,1024,1024]{2,1,0:T(8,128)(2,1)} %param.11), kind=kOutput, calls=%fused_computation.23 | convolution fusion | flops 268566528 | bytes 2621440 | tf_op jit(solution)/shard_map/dot_general | solution.py:120
  157.7 2.0 %fusion.24 = bf16[128,1024]{1,0:T(8,128)(2,1)S(1)} fusion(bf16[128,1024]{1,0:T(8,128)(2,1)S(1)} %copy_bitcast_fusion, bf16[4,1024,1024]{2,1,0:T(8,128)(2,1)} %param.11), kind=kOutput, calls=%fused_computation.25 | convolution fusion | flops 268566528 | bytes 2621440 | tf_op jit(solution)/shard_map/dot_general | solution.py:120
  160.3 16.7 %all-to-all-done.8 = bf16[8,4,256,128]{3,2,1,0:T(8,128)(2,1)} async-done(((bf16[8,4,256,128]{3,2,1,0:T(8,128)(2,1)}), bf16[8,4,256,128]{3,2,1,0:T(8,128)(2,1)}, u32[]{:S(2)}, u32[]{:S(2)}) %all-to-all-start.8) | async-done | bytes 2097184 | tf_op jit(solution)/shard_map/all_to_all | solution.py:18
  177.0 1.4 fusion.38
  178.4 1.4 fusion.37
  179.9 1.4 fusion.36
  181.3 1.4 fusion.35
  (71 shorter events, 8.1 us)
Async XLA Ops:
  15.5 19.6 %all-to-all-start.3 = ((f32[32,1,128]{2,1,0:T(1,128)}), f32[32,1,128]{2,1,0:T(1,128)S(1)}, u32[]{:S(2)}, u32[]{:S(2)}) async-start(f32[32,1,128]{2,1,0:T(1,128)} %broadcast_in_dim.56), calls=%async_computation.3 | async-start | bytes 32768 | tf_op jit(solution)/shard_map/all_to_all | solution.py:71
  28.1 12.8 %copy-start.1 = (bf16[1024,128]{1,0:T(8,128)(2,1)S(1)}, bf16[1024,128]{1,0:T(8,128)(2,1)}, u32[]{:S(2)}) copy-start(bf16[1024,128]{1,0:T(8,128)(2,1)} %param.7) | copy-start | bytes 786436
  35.2 17.8 %all-to-all-start.1 = ((bf16[8,128,384]{2,1,0:T(8,128)(2,1)}), bf16[8,128,384]{2,1,0:T(8,128)(2,1)S(1)}, u32[]{:S(2)}, u32[]{:S(2)}) async-start(bf16[8,128,384]{2,1,0:T(8,128)(2,1)} %copy.67), calls=%async_computation.1 | async-start | bytes 1572864 | tf_op jit(solution)/shard_map/all_to_all | solution.py:18
  54.6 30.7 %all-to-all-start = ((bf16[8,1024,128]{2,1,0:T(8,128)(2,1)}), bf16[8,1024,128]{2,1,0:T(8,128)(2,1)S(1)}, u32[]{:S(2)}, u32[]{:S(2)}) async-start(bf16[8,1024,128]{2,1,0:T(8,128)(2,1)} %broadcast_in_dim.51), calls=%async_computation | async-start | bytes 4194304 | tf_op jit(solution)/shard_map/all_to_all | solution.py:18
  86.0 13.6 %all-to-all-start.7 = ((bf16[32,4,8,128]{3,2,1,0:T(8,128)(2,1)}), bf16[32,4,8,128]{3,2,1,0:T(8,128)(2,1)S(1)}, u32[]{:S(2)}, u32[]{:S(2)}) async-start(bf16[32,4,8,128]{3,2,1,0:T(8,128)(2,1)} %broadcast_in_dim.111), calls=%async_computation.7 | async-start | bytes 524288 | tf_op jit(solution)/shard_map/all_to_all | solution.py:18
  100.3 14.1 %all-to-all-start.4 = ((bf16[8,128,128]{2,1,0:T(8,128)(2,1)}), bf16[8,128,128]{2,1,0:T(8,128)(2,1)S(1)}, u32[]{:S(2)}, u32[]{:S(2)}) async-start(bf16[8,128,128]{2,1,0:T(8,128)(2,1)} %broadcast_in_dim.103), calls=%async_computation.4 | async-start | bytes 524288 | tf_op jit(solution)/shard_map/all_to_all | solution.py:18
  106.6 16.4 %collective-permute-start = (bf16[8,258,128]{2,0,1:T(8,128)(2,1)S(1)}, bf16[8,258,128]{2,0,1:T(8,128)(2,1)}, u32[]{:S(2)}, u32[]{:S(2)}) collective-permute-start(bf16[8,258,128]{2,0,1:T(8,128)(2,1)S(1)} %copy.70), channel_id=1, source_target_pairs={{14,6},{15,7},{22,14},{23,15},{30,22},{31,23},{38,30},{39,31},{46,... | collective-permute-start | bytes 1585160 | tf_op jit(solution)/shard_map/ppermute | solution.py:110
  115.6 8.8 %all-to-all-start.5 = ((bf16[4,128,128]{2,1,0:T(8,128)(2,1)}), bf16[4,128,128]{2,1,0:T(8,128)(2,1)}, u32[]{:S(2)}, u32[]{:S(2)}) async-start(bf16[4,128,128]{2,1,0:T(8,128)(2,1)} %broadcast_in_dim.106), calls=%async_computation.5 | async-start | bytes 262144 | tf_op jit(solution)/shard_map/all_to_all | solution.py:18
  122.9 4.0 %copy-start = (f32[1024,128]{1,0:T(8,128)S(1)}, f32[1024,128]{1,0:T(8,128)}, u32[]{:S(2)}) copy-start(f32[1024,128]{1,0:T(8,128)} %fusion.12) | copy-start | bytes 1572868
  129.2 14.4 %all-to-all-start.6 = ((bf16[8,128,128]{2,1,0:T(8,128)(2,1)}), bf16[8,128,128]{2,1,0:T(8,128)(2,1)S(1)}, u32[]{:S(2)}, u32[]{:S(2)}) async-start(bf16[8,128,128]{2,1,0:T(8,128)(2,1)} %bitcast.29), calls=%async_computation.6 | async-start | bytes 524288 | tf_op jit(solution)/shard_map/all_to_all | solution.py:18
  145.4 31.6 %all-to-all-start.8 = ((bf16[8,4,256,128]{3,2,1,0:T(8,128)(2,1)}), bf16[8,4,256,128]{3,2,1,0:T(8,128)(2,1)}, u32[]{:S(2)}, u32[]{:S(2)}) async-start(bf16[8,4,256,128]{3,2,1,0:T(8,128)(2,1)} %broadcast_in_dim.113), calls=%async_computation.8 | async-start | bytes 4194304 | tf_op jit(solution)/shard_map/all_to_all | solution.py:18
  151.1 6.5 %copy-start.2 = (bf16[128,1024]{1,0:T(8,128)(2,1)}, bf16[128,1024]{1,0:T(8,128)(2,1)S(1)}, u32[]{:S(2)}) copy-start(bf16[128,1024]{1,0:T(8,128)(2,1)S(1)} %copy_bitcast_fusion) | copy-start | bytes 786436

commit v2 on v1

v2 whole, which is shorter than its diff:
```python
import jax
import jax.numpy as jnp
from jax import lax
from jax.experimental import pallas as pl
from jax.experimental.pallas import tpu as pltpu
from jax.sharding import PartitionSpec as P


CIN = 1024
HEADS = 8
D = 128
K = 4
ROW = 64
NORM_EPS = 1e-06
XS, ZS, YS = 4, 8, 4
NSEQ, NCH = XS * ZS, 2 * YS
LEN = 128
BLOCK = NCH * LEN
F32 = jnp.float32
BF16 = jnp.bfloat16
BOTH = ("seq", "ch")
ALONG_Z = [[x * ZS + z for z in range(ZS)] for x in range(XS)]
ALONG_X = [[x * ZS + z for x in range(XS)] for z in range(ZS)]
SCORE_SCALE = 4.0 * CIN ** (-0.5)

VMEM = pl.BlockSpec(memory_space=pltpu.VMEM)


def call(body, out, ins, flops=0, scratch=(), after=()):
    n = len(ins)

    def kernel(*refs):
        body(*refs[:n], *refs[n + len(after) :])

    moved = sum(a.size * a.dtype.itemsize for a in ins) + sum(o.size * o.dtype.itemsize for o in out)
    return pl.pallas_call(
        kernel,
        out_shape=out,
        in_specs=[VMEM] * n + [pl.BlockSpec(memory_space=pl.ANY)] * len(after),
        out_specs=[VMEM] * len(out),
        scratch_shapes=list(scratch),
        cost_estimate=pl.CostEstimate(flops=flops, bytes_accessed=moved, transcendentals=0),
    )(*ins, *after)


def place():
    s, c = lax.axis_index("seq"), lax.axis_index("ch")
    return s >> 3, s & (ZS - 1), c >> 1, c & 1


def shape(dims, dtype):
    return jax.ShapeDtypeStruct(dims, dtype)


def exchange(x, axis, groups=None):
    return lax.all_to_all(x, axis, split_axis=0, concat_axis=0, axis_index_groups=groups)


def hop(x, dy, swap=False):
    pairs = []
    for c in range(NCH):
        y, k = c // 2, c % 2
        pairs.append((c, ((y + dy) % YS) * 2 + ((1 - k) if swap else k)))
    return lax.ppermute(x, "ch", pairs)


def spread(x):
    half = x.shape[0] // 2
    up, dn = hop(x, 1), hop(x, -1)
    other = hop(x, 0, True)
    far_a, far_b = hop(up[:half], 1), hop(dn[half:], -1)
    return [x, up, dn, far_a, far_b], [other] + [hop(a, 0, True) for a in (up, dn, far_a, far_b)]


def split3(x):
    hi = x.astype(BF16).astype(F32)
    mid = (x - hi).astype(BF16).astype(F32)
    return hi, mid, x - hi - mid


PART = LEN


def pack_kernel(w, gate, mask, neg, out):
    hi, mid, lo = split3(gate[...])
    m = mask[...].astype(F32)
    spot = neg[...] - lax.axis_index("seq") * BLOCK
    p_hi, p_lo = (spot >> 5).astype(F32), (spot & 31).astype(F32)
    row = lax.broadcasted_iota(jnp.int32, (16, LEN), 0)
    mine = w[...]
    for h in range(HEADS):
        for part in range(3):
            out[h, 0:PART, part * D : (part + 1) * D] = mine[:, (part * HEADS + h) * D : (part * HEADS + h + 1) * D]
        a = jnp.where(row == 0, hi[h : h + 1], 0.0) + jnp.where(row == 1, m, 0.0)
        b = jnp.where(row == 0, mid[h : h + 1], 0.0)
        c = jnp.where(row == 0, lo[h : h + 1], 0.0)
        for j in range(K):
            a = a + jnp.where(row == 2 + j, p_hi[:, j : j + 1], 0.0)
            b = b + jnp.where(row == 2 + j, p_lo[:, j : j + 1], 0.0)
        out[h, PART : PART + 16, 0:D] = a.astype(BF16)
        out[h, PART : PART + 16, D : 2 * D] = b.astype(BF16)
        out[h, PART : PART + 16, 2 * D : 3 * D] = c.astype(BF16)


def homes(y):
    return [y, (y + 3) % YS, (y + 1) % YS, (y + 2) % YS]


def column(a, r):
    return jnp.concatenate([a[:, 2 * r : 2 * r + 1], a[:, 2 * r + 1 : 2 * r + 2]], axis=0)


def paired(w, first, last):
    _, _, y_at, core = place()
    return [
        jnp.concatenate([w[2 * y + core, 0:LEN, first:last], w[2 * y + 1 - core, 0:LEN, first:last]], axis=0)
        for y in homes(y_at)
    ]


def encoded_dot(mine, theirs, pairs, lo, size):
    acc = None
    for i in range(4):
        k, at = (i, lo) if i < 3 else (3, lo) if lo < BLOCK // 2 else (4, lo - BLOCK // 2)
        both = jnp.concatenate([mine[k][at : at + size], theirs[k][at : at + size]], axis=1)
        term = jnp.dot(both, pairs[i], preferred_element_type=F32)
        acc = term if acc is None else acc + term
    return acc


def project_kernel(part, *refs):
    mine, theirs = refs[0:5], refs[5:10]
    k_out, v_out, packet, cum_out, mask_out = refs[10:15]
    gates, places = refs[15:17]
    for c in range(NCH):
        info = part[c, PART : PART + 16, :].astype(F32)
        for p in range(3):
            gates[p, c : c + 1, :] = info[0:1, p * D : (p + 1) * D]
        mask_out[c : c + 1, :] = info[1:2, 0:D]
        for j in range(K):
            places[j * NCH + c : j * NCH + c + 1, :] = info[2 + j : 3 + j, 0:D] * 32.0 + info[2 + j : 3 + j, D : 2 * D]
    tri = (
        lax.broadcasted_iota(jnp.int32, (LEN, LEN), 0) <= lax.broadcasted_iota(jnp.int32, (LEN, LEN), 1)
    ).astype(BF16)
    cum = sum(jnp.dot(gates[p].astype(BF16), tri, preferred_element_type=F32) for p in range(3))
    rows, offset = [], jnp.zeros((1, 1), F32)
    for c in range(NCH):
        rows.append(cum[c : c + 1] + offset)
        offset = rows[-1][:, LEN - 1 : LEN]
    cum = jnp.concatenate(rows, axis=0)
    total = offset
    cum_out[...] = cum
    tail_t = jnp.exp(total - cum).T
    mask_t = mask_out[...].T
    pairs = paired(part, D, 3 * D)
    state = jnp.zeros((D, D), F32)
    size = 256
    for r in range(BLOCK // size):
        lo = r * size
        acc = encoded_dot(mine, theirs, pairs, lo, size)
        keys = acc[:, 0:D].astype(BF16)
        k_out[lo : lo + size] = keys
        values = (acc[:, D:].astype(BF16).astype(F32) * column(mask_t, r)).astype(BF16)
        v_out[lo : lo + size] = values
        scaled = (keys.astype(F32) * column(tail_t, r)).astype(BF16)
        state += lax.dot_general(scaled, values, (((0,), (0,)), ((), ())), preferred_element_type=F32)
    hot = (places[:, 0:1].astype(jnp.int32) == lax.broadcasted_iota(jnp.int32, (K * NCH, BLOCK), 1)).astype(F32)
    picked = jnp.dot(hot.astype(BF16), mine[0][...], preferred_element_type=F32).astype(BF16)
    row = lax.broadcasted_iota(jnp.int32, (16, D), 0)
    hi, mid, low = split3(total)
    info = (jnp.where(row == 0, hi, 0.0) + jnp.where(row == 1, mid, 0.0) + jnp.where(row == 2, low, 0.0)).astype(BF16)
    state = state.astype(BF16)
    for z in range(ZS):
        packet[z, 0:D, :] = state
        packet[z, D : D + 16, :] = info
        packet[z, D + 16 : D + 16 + K * NCH, :] = picked


FAR = K * ROW


def intra_kernel(part, *refs):
    mine, theirs = refs[0:5], refs[5:10]
    k, v, cum, masks = refs[10:14]
    q, out, window, halo = refs[14:18]
    pairs = paired(part, 0, D)
    size = 256
    cum_rows = cum[...]
    cum_t = cum_rows.T
    lower = lax.broadcasted_iota(jnp.int32, (size, size), 0) >= lax.broadcasted_iota(jnp.int32, (size, size), 1)
    for r in range(BLOCK // size):
        here = column(cum_t, r)
        queries = encoded_dot(mine, theirs, pairs, r * size, size).astype(BF16)
        q[r * size : (r + 1) * size] = queries
        acc = jnp.zeros((size, D), F32)
        for s in range(r + 1):
            diff = here - jnp.concatenate([cum_rows[2 * s : 2 * s + 1], cum_rows[2 * s + 1 : 2 * s + 2]], axis=1)
            if s == r:
                diff = jnp.where(lower, diff, -jnp.inf)
            scores = lax.dot_general(
                queries, k[s * size : (s + 1) * size], (((1,), (1,)), ((), ())), preferred_element_type=F32
            )
            acc += jnp.dot((scores * jnp.exp(diff)).astype(BF16), v[s * size : (s + 1) * size], preferred_element_type=F32)
        out[r * size : (r + 1) * size] = acc
    _, _, y_at, core = place()
    ys = homes(y_at)
    for b in range(3):
        at_row = 2 * y_at + core + b
        inside = jnp.minimum(at_row, NCH - 1)
        low = pl.ds(pl.multiple_of(jnp.minimum(inside, 3) * LEN, LEN), LEN)
        high = pl.ds(pl.multiple_of(jnp.maximum(inside - 4, 0) * LEN, LEN), LEN)
        rows = pl.ds(pl.multiple_of(inside * LEN, LEN), LEN)
        for i, y in enumerate(ys):
            for who, group in ((core, mine), (1 - core, theirs)):
                lanes = pl.ds(pl.multiple_of((2 * y + who) * D, D), D)
                if i < 3:
                    window[b * LEN : (b + 1) * LEN, lanes] = group[i][rows, :]
                else:
                    window[b * LEN : (b + 1) * LEN, lanes] = jnp.where(inside < 4, group[3][low, :], group[4][high, :])
    for i, y in enumerate(ys):
        for who, group in ((core, mine), (1 - core, theirs)):
            halo[pl.ds(pl.multiple_of((2 * y + who) * FAR, FAR), FAR), :] = group[i][0:FAR, :]
    row = lax.broadcasted_iota(jnp.int32, (16, D), 0)
    halo[NCH * FAR : NCH * FAR + 16, :] = (
        jnp.where(row == 0, masks[0:1], 0.0) + jnp.where(row == 1, masks[1:2], 0.0)
    ).astype(BF16)


def log_of(block):
    info = block.astype(F32)
    return info[0:1] + info[1:2] + info[2:3]


def row_kernel(z_in, packet, here_out, before_out):
    z_at = place()[1]
    row_state, here = jnp.zeros((D, D), F32), jnp.zeros((D, D), F32)
    row_log, before = jnp.zeros((1, D), F32), jnp.zeros((1, D), F32)
    for z in range(ZS):
        log = log_of(z_in[z, D : D + 16, :])
        factor, state = jnp.exp(log), z_in[z, 0:D, :].astype(F32)
        row_state = row_state * factor + state
        row_log = row_log + log
        here = jnp.where(z < z_at, here * factor + state, here)
        before = jnp.where(z < z_at, before + log, before)
    here_out[...] = here
    before_out[...] = jnp.broadcast_to(before, (8, D))
    row = lax.broadcasted_iota(jnp.int32, (16, D), 0)
    hi, mid, low = split3(row_log)
    info = (jnp.where(row == 0, hi, 0.0) + jnp.where(row == 1, mid, 0.0) + jnp.where(row == 2, low, 0.0)).astype(BF16)
    row_state = row_state.astype(BF16)
    n = K * NCH
    for x in range(XS):
        packet[x, 0:D, :] = row_state
        packet[x, D : D + 16, :] = info
        for z in range(ZS):
            packet[x, D + 16 + z * n : D + 16 + (z + 1) * n, :] = z_in[z, D + 16 : D + 16 + n, :]


def finish_kernel(x_in, here, before, q, intra, cum, gain, out):
    x_at = place()[0]
    state = jnp.zeros((D, D), F32)
    for x in range(XS):
        log = log_of(x_in[x, D : D + 16, :])
        state = jnp.where(x < x_at, state * jnp.exp(log) + x_in[x, 0:D, :].astype(F32), state)
    incoming = (state * jnp.exp(before[0:1]) + here[...]).astype(BF16)
    grow_t = jnp.exp(cum[...]).T
    scale = gain[:, pl.ds(pl.multiple_of(lax.axis_index("ch") * D, D), D)]
    size = 256
    for r in range(BLOCK // size):
        grow = jnp.concatenate([grow_t[:, 2 * r : 2 * r + 1], grow_t[:, 2 * r + 1 : 2 * r + 2]], axis=0)
        inter = jnp.dot(q[r * size : (r + 1) * size], incoming, preferred_element_type=F32)
        mixed = (intra[r * size : (r + 1) * size] + inter * grow) * D ** (-0.5)
        squares = jnp.mean(mixed * mixed, axis=-1, keepdims=True)
        context = (mixed / jnp.sqrt(squares + NORM_EPS) * scale).astype(BF16)
        out[2 * r] = context[0:LEN]
        out[2 * r + 1] = context[LEN:]


def predict_kernel(ctx, w, context, predicted):
    j = pl.program_id(0)
    whole = jnp.concatenate([ctx[h] for h in range(HEADS)], axis=1)

    @pl.when(j == 0)
    def _():
        context[...] = whole

    predicted[0] = jnp.dot(whole, w[0], preferred_element_type=F32).astype(BF16)


def predict(ctx, w_pred):
    return pl.pallas_call(
        predict_kernel,
        grid=(K,),
        out_shape=[shape((LEN, CIN), BF16), shape((K, LEN, CIN), BF16)],
        in_specs=[pl.BlockSpec((HEADS, LEN, D), lambda j: (0, 0, 0)), pl.BlockSpec((1, CIN, CIN), lambda j: (j, 0, 0))],
        out_specs=[pl.BlockSpec((LEN, CIN), lambda j: (0, 0)), pl.BlockSpec((1, LEN, CIN), lambda j: (j, 0, 0))],
        name="predict",
        cost_estimate=pl.CostEstimate(flops=K * 2 * LEN * CIN * CIN, bytes_accessed=K * 2 * CIN * CIN, transcendentals=0),
    )(ctx, w_pred)


def loss_kernel(predicted, window, halo, masks, *refs):
    mine, theirs = refs[0:5], refs[5:10]
    loss, bank, ahead = refs[10:13]
    _, _, y_at, core = place()
    half = BLOCK // 2
    for i, y in enumerate(homes(y_at)):
        for who, group in ((core, mine), (1 - core, theirs)):
            lanes = pl.ds(pl.multiple_of((2 * y + who) * D, D), D)
            if i < 3:
                bank[:, lanes] = group[i][...]
            else:
                bank[0:half, lanes] = group[3][...]
                bank[half:, lanes] = group[4][...]
    me = 2 * y_at + core
    next_rows = halo[NCH * FAR : NCH * FAR + 16, :].astype(F32)
    ahead[0:LEN, :] = window[0:LEN, :]
    flags = [masks[pl.ds(me, 1), :]]
    for b in (1, 2):
        beyond = jnp.maximum(me + b - NCH, 0)

        @pl.when(me + b < NCH)
        def _():
            ahead[b * LEN : (b + 1) * LEN, :] = window[b * LEN : (b + 1) * LEN, :]

        @pl.when(me + b >= NCH)
        def _():
            for c in range(NCH):
                rows = pl.ds(pl.multiple_of(c * FAR + beyond * LEN, LEN), LEN)
                ahead[b * LEN : (b + 1) * LEN, c * D : (c + 1) * D] = halo[rows, :]

        outer = jnp.where(beyond == 0, next_rows[0:1], next_rows[1:2])
        flags.append(jnp.where(me + b < NCH, masks[pl.ds(jnp.minimum(me + b, NCH - 1), 1), :], outer))
    m0, m1, m2 = flags
    valid = [
        m0 * jnp.concatenate([m0[:, ROW:], m1[:, :ROW]], axis=1),
        m0 * m1,
        m0 * jnp.concatenate([m1[:, ROW:], m2[:, :ROW]], axis=1),
        m0 * m2,
    ]
    n = NSEQ * NCH
    for j in range(K):
        part = predicted[j]
        logits = (
            lax.dot_general(bank[j * n : (j + 1) * n, :], part, (((1,), (1,)), ((), ())), preferred_element_type=F32)
            * SCORE_SCALE
        )
        negsum = jnp.sum(jnp.exp(logits), axis=0, keepdims=True)
        acc = jnp.zeros((LEN, D), F32)
        for c in range(NCH):
            target = ahead[(j + 1) * ROW : (j + 1) * ROW + LEN, c * D : (c + 1) * D]
            acc += part[:, c * D : (c + 1) * D].astype(F32) * target.astype(F32)
        positive = jnp.sum(acc.T, axis=0, keepdims=True) * SCORE_SCALE
        loss[j : j + 1, :] = valid[j] * (jnp.log(jnp.exp(positive) + negsum) - positive)


def step(features, w_qkv, log_gate, norm_gain, w_pred, patch_mask, neg_index):
    mine, theirs = spread(features)
    (packed,) = call(
        pack_kernel, [shape((HEADS, PART + 16, 3 * D), BF16)],
        [w_qkv, log_gate, patch_mask.reshape(1, -1), neg_index.T],
    )
    w_part = exchange(packed, "ch")
    pieces = [w_part, *mine, *theirs]
    whole = shape((BLOCK, D), BF16)
    n = K * NCH
    keys, values, packet, cumul, masks = call(
        project_kernel,
        [whole, whole, shape((ZS, D + 16 + n, D), BF16), shape((NCH, LEN), F32), shape((NCH, LEN), F32)],
        pieces,
        flops=2 * BLOCK * CIN * 2 * D,
        scratch=[pltpu.VMEM((3, NCH, LEN), F32), pltpu.VMEM((n, D), F32)],
    )
    z_in = exchange(packet, "seq", ALONG_Z)
    queries, intra, window, halo = call(
        intra_kernel,
        [whole, shape((BLOCK, D), F32), shape((LEN + FAR, CIN), BF16), shape((NCH * FAR + 16, D), BF16)],
        [*pieces, keys, values, cumul, masks],
        flops=2 * BLOCK * (BLOCK + CIN) * D,
    )
    x_packet, here, before = call(
        row_kernel, [shape((XS, D + 16 + ZS * n, D), BF16), shape((D, D), F32), shape((8, D), F32)], [z_in],
        after=[intra],
    )
    x_packet, halo = lax.optimization_barrier((x_packet, halo))
    x_in = exchange(x_packet, "seq", ALONG_X)
    pairs = [((s + 1) * NCH + c, s * NCH + c) for s in range(NSEQ - 1) for c in (NCH - 2, NCH - 1)]
    halo = lax.ppermute(halo, BOTH, pairs)
    (context,) = call(
        finish_kernel, [shape((NCH, LEN, D), BF16)],
        [x_in, here, before, queries, intra, cumul, norm_gain.reshape(1, -1)], flops=2 * BLOCK * D * D,
    )
    bank = x_in[:, D + 16 :].reshape(XS * ZS, K, NCH, D).transpose(1, 0, 2, 3).reshape(K * NSEQ * NCH, D)
    context = exchange(context, "ch")
    bank_mine, bank_theirs = spread(bank)
    context, predicted = predict(context, w_pred)
    (loss,) = call(
        loss_kernel, [shape((K, LEN), F32)], [predicted, window, halo, masks, *bank_mine, *bank_theirs],
        flops=K * 2 * LEN * CIN * 256,
        scratch=[pltpu.VMEM((K * NSEQ * NCH, CIN), BF16), pltpu.VMEM((LEN + FAR, CIN), BF16)],
    )
    return context, loss


def solution(mesh):
    placed = (
        P("seq", "ch"),
        P("ch", None),
        P(None, BOTH),
        P(),
        P(),
        P(BOTH),
        P(None, BOTH),
    )
    return jax.shard_map(
        lambda *a: tuple(step(*a)),
        mesh=mesh,
        in_specs=placed,
        out_specs=(P(BOTH, None), P(None, BOTH)),
        check_vma=False,
    )
```

time: 185 us -> 114 us (0.62)
  waiting for transfers between devices: 74.1 us -> 38.7 us
  Pallas kernels: 0 us -> 27.2 us
  matrix products: 25.4 us -> 0 us
  local copies, waits for them, and re-layouts: 16.5 us -> 3.94 us
  blocking collectives: 10.4 us -> 0 us
  other arithmetic: 7.79 us -> 0 us
  starting transfers between devices: 48.2 us -> 42.3 us
    all_to_all x7 -> x4, waiting for transfers between devices: 69.2 us -> 15.3 us  [exchange(): lax.all_to_all(x, axis, split_axis=0, concat_axis=0, axis_index_groups=gr...]
    pallas_call x0 -> x7, Pallas kernels: none -> 27.2 us  [the longest x6 21.4 us: call(): pl.pallas_call(kernel, out_shape=out, in_specs=[VMEM] * n + [pl.BlockSpec...]
    dot_general x14 -> x0, matrix products: 25.4 us -> none  [the longest x4 8.25 us: shards(): jnp.dot(context, w_pred[j], preferred_element_type=F32).astype(BF16)]
    ppermute x1 -> x19, waiting for transfers between devices: 0.01 us -> 23.4 us  [the longest x18 23.4 us: hop(): return lax.ppermute(x, 'ch', pairs)]
    ppermute x1 -> x19, starting transfers between devices: 1.47 us -> 18.6 us  [the longest x18 17.9 us: hop(): return lax.ppermute(x, 'ch', pairs)]
    all_to_all x7 -> x4, starting transfers between devices: 35.7 us -> 23.7 us  [exchange(): lax.all_to_all(x, axis, split_axis=0, concat_axis=0, axis_index_groups=gr...]
    all_to_all x1 -> x0, starting transfers between devices: 11 us -> none  [shards(): lax.all_to_all(jnp.broadcast_to(total, (nseq, 1, 128)), 'seq', split_axis...]
    all_to_all x1 -> x0, blocking collectives: 10.4 us -> none  [exchange(): lax.all_to_all(x, axis, split_axis=0, concat_axis=0, axis_index_groups=gr...]
  transfers between devices with their start and end apart: 9 -> 23, of which waited for: 8 -> 7; matrix products, arithmetic and copies ran while one was open for 16% -> 0% of each run, Pallas kernels for 0% -> 13%
where the time goes in v2:
time: 114 us; the launch traced here: 113 us
  starting transfers between devices  42.3 us (37%)
  waiting for transfers between devices  38.7 us (34%)
  Pallas kernels  27.2 us (24%)
  local copies, waits for them, and re-layouts  3.94 us (3%)
    all_to_all x4, starting transfers between devices, exchange(): lax.all_to_all(x, axis, split_axis=0, concat_axis=0, axis_index_groups=gr...  23.7 us
    ppermute x18, waiting for transfers between devices, hop(): return lax.ppermute(x, 'ch', pairs)  23.4 us
    pallas_call x6, Pallas kernels, call(): pl.pallas_call(kernel, out_shape=out, in_specs=[VMEM] * n + [pl.BlockSpec...  21.4 us
    ppermute x18, starting transfers between devices, hop(): return lax.ppermute(x, 'ch', pairs)  17.9 us
    all_to_all x4, waiting for transfers between devices, exchange(): lax.all_to_all(x, axis, split_axis=0, concat_axis=0, axis_index_groups=gr...  15.3 us
    pallas_call x1, Pallas kernels, predict(): pl.pallas_call(predict_kernel, grid=(K,), out_shape=[shape((LEN, CIN), BF...  5.81 us
    unnamed x48, local copies, waits for them, and re-layouts  3.84 us
  transfers between devices with their start and end apart: 23, of which 7 were waited for; matrix products, arithmetic and copies ran while one was open for 0% of the time, Pallas kernels for 13%

profile of v2, /device:TPU:1, one launch (start us, length us, event | category | flops | bytes accessed | tf_op | source)
XLA Modules:
  0.0 113.0 jit_solution(17218574127386390564)
XLA Ops:
  0.6 2.2 %shard_map.86 = bf16[8,144,384]{2,1,0:T(8,128)(2,1)} custom-call(bf16[128,3072]{1,0:T(8,128)(2,1)} %refs_0_.1, f32[8,128]{1,0:T(8,128)} %refs_1_.3, s32[1,128]{1,0:T(1,128)} %bitcast.13, s32[1,4]{1,0:T(1,128)} %bitcast.14), custom_call_target="tpu_custom_call" | custom-call | bytes 1675792 | tf_op jit(solution)/shard_map/pallas_call | solution.py:36
  2.8 6.7 %all-to-all-start = ((bf16[8,144,384]{2,1,0:T(8,128)(2,1)}), bf16[8,144,384]{2,1,0:T(8,128)(2,1)S(1)}, u32[]{:S(2)}, u32[]{:S(2)}) async-start(bf16[8,144,384]{2,1,0:T(8,128)(2,1)} %shard_map.86), calls=%async_computation | async-start | bytes 1769472 | tf_op jit(solution)/shard_map/all_to_all | solution.py:56
  9.5 1.4 %collective-permute-start = (bf16[1024,128]{1,0:T(8,128)(2,1)}, bf16[1024,128]{1,0:T(8,128)(2,1)S(1)}, u32[]{:S(2)}, u32[]{:S(2)}) collective-permute-start(bf16[1024,128]{1,0:T(8,128)(2,1)} %refs_1_.5), channel_id=1, source_target_pairs={{0,2},{1,3},{2,4},{3,5},{4,6},{5,7},{6,0},{7,1},{8,10},{9,11},{10,... | collective-permute-start | bytes 786440 | tf_op jit(solution)/shard_map/ppermute | solution.py:64
  10.9 1.3 %collective-permute-start.1 = (bf16[1024,128]{1,0:T(8,128)(2,1)}, bf16[1024,128]{1,0:T(8,128)(2,1)S(1)}, u32[]{:S(2)}, u32[]{:S(2)}) collective-permute-start(bf16[1024,128]{1,0:T(8,128)(2,1)} %refs_1_.5), channel_id=1, source_target_pairs={{0,6},{1,7},{2,0},{3,1},{4,2},{5,3},{6,4},{7,5},{8,14},{9,15},{10,... | collective-permute-start | bytes 786440 | tf_op jit(solution)/shard_map/ppermute | solution.py:64
  12.2 0.7 collective-permute-start.4
  12.9 15.4 %collective-permute-done.refs_2_ = bf16[1024,128]{1,0:T(8,128)(2,1)S(1)} collective-permute-done((bf16[1024,128]{1,0:T(8,128)(2,1)}, bf16[1024,128]{1,0:T(8,128)(2,1)S(1)}, u32[]{:S(2)}, u32[]{:S(2)}) %collective-permute-start) | collective-permute-done | bytes 262176 | tf_op jit(solution)/shard_map/ppermute | solution.py:64
  28.3 0.1 collective-permute-start.2
  28.4 0.9 collective-permute-start.5
  29.2 0.0 collective-permute-done.1.refs_3_
  29.3 0.1 collective-permute-start.6
  29.4 2.9 %collective-permute-start.3 = (bf16[512,128]{1,0:T(8,128)(2,1)S(1)}, bf16[512,128]{1,0:T(8,128)(2,1)S(1)}, u32[]{:S(2)}, u32[]{:S(2)}) collective-permute-start(bf16[512,128]{1,0:T(8,128)(2,1)S(1)} %slice.21), channel_id=1, source_target_pairs={{0,6},{1,7},{2,0},{3,1},{4,2},{5,3},{6,4},{7,5},{8,14},{9,15},{10,... | collective-permute-start | bytes 393224 | tf_op jit(solution)/shard_map/ppermute | solution.py:64
  32.3 1.6 %collective-permute-done.2.refs_4_ = bf16[512,128]{1,0:T(8,128)(2,1)S(1)} collective-permute-done((bf16[512,128]{1,0:T(8,128)(2,1)S(1)}, bf16[512,128]{1,0:T(8,128)(2,1)S(1)}, u32[]{:S(2)}, u32[]{:S(2)}) %collective-permute-start.2) | collective-permute-done | bytes 131104 | tf_op jit(solution)/shard_map/ppermute | solution.py:64
  33.9 1.6 %collective-permute-start.7 = (bf16[512,128]{1,0:T(8,128)(2,1)S(1)}, bf16[512,128]{1,0:T(8,128)(2,1)S(1)}, u32[]{:S(2)}, u32[]{:S(2)}) collective-permute-start(bf16[512,128]{1,0:T(8,128)(2,1)S(1)} %collective-permute-done.2.refs_4_), channel_id=1, source_target_pairs={{0,1},{1,0},{2,3},{3,2},{4,5},{5,4},{6,7},{7,6},{8,9},{9,8},{10,11... | collective-permute-start | bytes 393224 | tf_op jit(solution)/shard_map/ppermute | solution.py:64
  35.5 0.5 collective-permute-start.8
  36.0 0.4 collective-permute-done.7.refs_9_
  36.5 0.5 collective-permute-done.8.refs_10_
  37.1 0.1 copy-done.15
  37.1 0.5 copy-done.16
  37.6 0.9 copy-done
  38.6 4.5 %shard_map.87 = (bf16[1024,128]{1,0:T(8,128)(2,1)}, bf16[1024,128]{1,0:T(8,128)(2,1)}, bf16[8,176,128]{2,1,0:T(8,128)(2,1)}, f32[8,128]{1,0:T(8,128)}, f32[8,128]{1,0:T(8,128)}) custom-call(bf16[8,144,384]{2,1,0:T(8,128)(2,1)} %copy-done, bf16[1024,128]{1,0:T(8,128)(2,1)} %refs_1_.5, bf16[1024,128]{1,0:T(8,128)(2,1)} %copy-done.2, ...), custom_call_target="tpu_custom_call" | custom-call | flops 536870912 | bytes 3874816 | tf_op jit(solution)/shard_map/pallas_call | solution.py:36
  43.1 7.5 %all-to-all-start.1 = ((bf16[8,176,128]{2,1,0:T(8,128)(2,1)}), bf16[8,176,128]{2,1,0:T(8,128)(2,1)S(1)}, u32[]{:S(2)}, u32[]{:S(2)}) async-start(bf16[8,176,128]{2,1,0:T(8,128)(2,1)} %get-tuple-element.18), calls=%async_computation.1 | async-start | bytes 720896 | tf_op jit(solution)/shard_map/all_to_all | solution.py:56
  50.6 5.7 %shard_map.88 = (bf16[1024,128]{1,0:T(8,128)(2,1)}, f32[1024,128]{1,0:T(8,128)}, bf16[384,1024]{1,0:T(8,128)(2,1)}, bf16[2064,128]{1,0:T(8,128)(2,1)}) custom-call(bf16[8,144,384]{2,1,0:T(8,128)(2,1)} %copy-done, bf16[1024,128]{1,0:T(8,128)(2,1)} %refs_1_.5, bf16[1024,128]{1,0:T(8,128)(2,1)} %copy-done.2, bf16[1024,128]{1,0:T(8,128)(2,1)} %copy-done.3, ...), custom_call_target="tpu_custom_call" | custom-call | flops 536870912 | bytes 5615616 | tf_op jit(solution)/shard_map/pallas_call | solution.py:36
  56.3 8.7 %all-to-all-done.1.refs_0_ = bf16[8,176,128]{2,1,0:T(8,128)(2,1)S(1)} async-done(((bf16[8,176,128]{2,1,0:T(8,128)(2,1)}), bf16[8,176,128]{2,1,0:T(8,128)(2,1)S(1)}, u32[]{:S(2)}, u32[]{:S(2)}) %all-to-all-start.1) | async-done | bytes 360480 | tf_op jit(solution)/shard_map/all_to_all | solution.py:56
  65.0 0.7 copy-done.4
  65.7 1.9 %shard_map.89 = (bf16[4,400,128]{2,1,0:T(8,128)(2,1)}, f32[128,128]{1,0:T(8,128)}, f32[8,128]{1,0:T(8,128)}) custom-call(bf16[8,176,128]{2,1,0:T(8,128)(2,1)} %copy-done.4, f32[1024,128]{1,0:T(8,128)} %get-tuple-element.23.refs_1_.refs_4_), custom_call_target="tpu_custom_call" | custom-call | bytes 839680 | tf_op jit(solution)/shard_map/pallas_call | solution.py:36
  67.6 4.0 %all-to-all-start.2 = ((bf16[4,400,128]{2,1,0:T(8,128)(2,1)}), bf16[4,400,128]{2,1,0:T(8,128)(2,1)S(1)}, u32[]{:S(2)}, u32[]{:S(2)}) async-start(bf16[4,400,128]{2,1,0:T(8,128)(2,1)} %get-tuple-element.26), calls=%async_computation.2 | async-start | bytes 819200 | tf_op jit(solution)/shard_map/all_to_all | solution.py:56
  71.6 0.7 collective-permute-start.9
  72.3 6.6 %all-to-all-done.2.refs_0_ = bf16[4,400,128]{2,1,0:T(8,128)(2,1)S(1)} async-done(((bf16[4,400,128]{2,1,0:T(8,128)(2,1)}), bf16[4,400,128]{2,1,0:T(8,128)(2,1)S(1)}, u32[]{:S(2)}, u32[]{:S(2)}) %all-to-all-start.2) | async-done | bytes 409632 | tf_op jit(solution)/shard_map/all_to_all | solution.py:56
  79.0 0.1 collective-permute-start.10
  79.1 3.7 %collective-permute-start.11 = (bf16[1024,128]{1,0:T(8,128)(2,1)S(1)}, bf16[1024,128]{1,0:T(8,128)(2,1)S(1)}, u32[]{:S(2)}, u32[]{:S(2)}) collective-permute-start(bf16[1024,128]{1,0:T(8,128)(2,1)S(1)} %bitcast.8), channel_id=1, source_target_pairs={{0,6},{1,7},{2,0},{3,1},{4,2},{5,3},{6,4},{7,5},{8,14},{9,15},{10,... | collective-permute-start | bytes 786440 | tf_op jit(solution)/shard_map/ppermute | solution.py:64
  82.7 2.8 %shard_map.90 = bf16[8,128,128]{2,1,0:T(8,128)(2,1)} custom-call(bf16[4,400,128]{2,1,0:T(8,128)(2,1)} %copy-done.1, f32[128,128]{1,0:T(8,128)} %get-tuple-element.27.refs_1_, f32[8,128]{1,0:T(8,128)} %get-tuple-element.28.refs_2_, bf16[1024,128]{1,0:T(8,128)(2,1)} %get-tuple-element.29.refs_3_, f32[1024,128]{1,0:T(8,128)} %get-tuple-element.23.refs_1_.refs_4_, ...), custom_call_target="tpu_custom_call" | custom-call | flops 33554432 | bytes 1536000 | tf_op jit(solution)/shard_map/pallas_call | solution.py:36
  85.5 5.5 %all-to-all-start.3 = ((bf16[8,128,128]{2,1,0:T(8,128)(2,1)}), bf16[8,128,128]{2,1,0:T(8,128)(2,1)S(1)}, u32[]{:S(2)}, u32[]{:S(2)}) async-start(bf16[8,128,128]{2,1,0:T(8,128)(2,1)} %shard_map.90), calls=%async_computation.3 | async-start | bytes 524288 | tf_op jit(solution)/shard_map/all_to_all | solution.py:56
  91.1 0.2 collective-permute-start.14
  91.3 1.6 %collective-permute-start.12 = (bf16[512,128]{1,0:T(8,128)(2,1)S(1)}, bf16[512,128]{1,0:T(8,128)(2,1)S(1)}, u32[]{:S(2)}, u32[]{:S(2)}) collective-permute-start(bf16[512,128]{1,0:T(8,128)(2,1)S(1)} %slice.23), channel_id=1, source_target_pairs={{0,2},{1,3},{2,4},{3,5},{4,6},{5,7},{6,0},{7,1},{8,10},{9,11},{10,... | collective-permute-start | bytes 393224 | tf_op jit(solution)/shard_map/ppermute | solution.py:64
  92.9 0.4 collective-permute-start.15
  93.3 0.2 collective-permute-start.16
  93.5 1.3 %collective-permute-start.13 = (bf16[512,128]{1,0:T(8,128)(2,1)S(1)}, bf16[512,128]{1,0:T(8,128)(2,1)S(1)}, u32[]{:S(2)}, u32[]{:S(2)}) collective-permute-start(bf16[512,128]{1,0:T(8,128)(2,1)S(1)} %slice.24), channel_id=1, source_target_pairs={{0,6},{1,7},{2,0},{3,1},{4,2},{5,3},{6,4},{7,5},{8,14},{9,15},{10,... | collective-permute-start | bytes 393224 | tf_op jit(solution)/shard_map/ppermute | solution.py:64
  94.9 5.5 %collective-permute-done.12.refs_7_ = bf16[512,128]{1,0:T(8,128)(2,1)S(1)} collective-permute-done((bf16[512,128]{1,0:T(8,128)(2,1)S(1)}, bf16[512,128]{1,0:T(8,128)(2,1)S(1)}, u32[]{:S(2)}, u32[]{:S(2)}) %collective-permute-start.12) | collective-permute-done | bytes 131104 | tf_op jit(solution)/shard_map/ppermute | solution.py:64
  100.4 0.8 collective-permute-start.17
  101.1 0.1 collective-permute-start.18
  101.2 0.7 copy-done.6
  101.9 5.8 %predict.1 = (bf16[128,1024]{1,0:T(8,128)(2,1)}, bf16[4,128,1024]{2,1,0:T(8,128)(2,1)}) custom-call(bf16[8,128,128]{2,1,0:T(8,128)(2,1)} %copy-done.6, bf16[4,1024,1024]{2,1,0:T(8,128)(2,1)} %w.1), custom_call_target="tpu_custom_call" | custom-call | flops 1073741824 | bytes 8388608 | tf_op jit(solution)/shard_map/predict/pallas_call | solution.py:291
  107.9 0.6 copy-done.17
  108.4 0.1 copy-done.18
  108.6 0.1 copy-done.19
  108.6 0.0 copy-done.22
  108.7 0.0 copy-done.23
  108.7 4.3 %shard_map.91 = f32[4,128]{1,0:T(4,128)} custom-call(bf16[4,128,1024]{2,1,0:T(8,128)(2,1)} %get-tuple-element.31.refs_0_, bf16[384,1024]{1,0:T(8,128)(2,1)} %get-tuple-element.32.refs_1_, bf16[2064,128]{1,0:T(8,128)(2,1)} %copy-done.12, f32[8,128]{1,0:T(8,128)} %get-tuple-element.22.refs_14_.refs_3_, bf16[1024,128]{1,0:T(8,128)(2,1)} %bitcast.10, ...), custom_call_target="tpu_custom_call" | custom-call | flops 268435456 | bytes 4466688 | tf_op jit(solution)/shard_map/pallas_call | solution.py:36
  (59 shorter events, 0.2 us)
Async XLA Ops:
  2.8 34.2 %all-to-all-start = ((bf16[8,144,384]{2,1,0:T(8,128)(2,1)}), bf16[8,144,384]{2,1,0:T(8,128)(2,1)S(1)}, u32[]{:S(2)}, u32[]{:S(2)}) async-start(bf16[8,144,384]{2,1,0:T(8,128)(2,1)} %shard_map.86), calls=%async_computation | async-start | bytes 1769472 | tf_op jit(solution)/shard_map/all_to_all | solution.py:56
  9.5 18.8 %collective-permute-start = (bf16[1024,128]{1,0:T(8,128)(2,1)}, bf16[1024,128]{1,0:T(8,128)(2,1)S(1)}, u32[]{:S(2)}, u32[]{:S(2)}) collective-permute-start(bf16[1024,128]{1,0:T(8,128)(2,1)} %refs_1_.5), channel_id=1, source_target_pairs={{0,2},{1,3},{2,4},{3,5},{4,6},{5,7},{6,0},{7,1},{8,10},{9,11},{10,... | collective-permute-start | bytes 786440 | tf_op jit(solution)/shard_map/ppermute | solution.py:64
  10.9 18.4 %collective-permute-start.1 = (bf16[1024,128]{1,0:T(8,128)(2,1)}, bf16[1024,128]{1,0:T(8,128)(2,1)S(1)}, u32[]{:S(2)}, u32[]{:S(2)}) collective-permute-start(bf16[1024,128]{1,0:T(8,128)(2,1)} %refs_1_.5), channel_id=1, source_target_pairs={{0,6},{1,7},{2,0},{3,1},{4,2},{5,3},{6,4},{7,5},{8,14},{9,15},{10,... | collective-permute-start | bytes 786440 | tf_op jit(solution)/shard_map/ppermute | solution.py:64
  12.2 23.8 %collective-permute-start.4 = (bf16[1024,128]{1,0:T(8,128)(2,1)}, bf16[1024,128]{1,0:T(8,128)(2,1)S(1)}, u32[]{:S(2)}, u32[]{:S(2)}) collective-permute-start(bf16[1024,128]{1,0:T(8,128)(2,1)} %refs_1_.5), channel_id=1, source_target_pairs={{0,1},{1,0},{2,3},{3,2},{4,5},{5,4},{6,7},{7,6},{8,9},{9,8},{10,11... | collective-permute-start | bytes 786440 | tf_op jit(solution)/shard_map/ppermute | solution.py:64
  28.3 8.7 %copy-start.2 = (bf16[1024,128]{1,0:T(8,128)(2,1)}, bf16[1024,128]{1,0:T(8,128)(2,1)S(1)}, u32[]{:S(2)}) copy-start(bf16[1024,128]{1,0:T(8,128)(2,1)S(1)} %collective-permute-done.refs_2_) | copy-start | bytes 786436
  28.3 5.6 %collective-permute-start.2 = (bf16[512,128]{1,0:T(8,128)(2,1)S(1)}, bf16[512,128]{1,0:T(8,128)(2,1)S(1)}, u32[]{:S(2)}, u32[]{:S(2)}) collective-permute-start(bf16[512,128]{1,0:T(8,128)(2,1)S(1)} %slice.20), channel_id=1, source_target_pairs={{0,2},{1,3},{2,4},{3,5},{4,6},{5,7},{6,0},{7,1},{8,10},{9,11},{10,... | collective-permute-start | bytes 393224 | tf_op jit(solution)/shard_map/ppermute | solution.py:64
  28.4 7.6 %collective-permute-start.5 = (bf16[1024,128]{1,0:T(8,128)(2,1)S(1)}, bf16[1024,128]{1,0:T(8,128)(2,1)S(1)}, u32[]{:S(2)}, u32[]{:S(2)}) collective-permute-start(bf16[1024,128]{1,0:T(8,128)(2,1)S(1)} %collective-permute-done.refs_2_), channel_id=1, source_target_pairs={{0,1},{1,0},{2,3},{3,2},{4,5},{5,4},{6,7},{7,6},{8,9},{9,8},{10,11... | collective-permute-start | bytes 786440 | tf_op jit(solution)/shard_map/ppermute | solution.py:64
  29.2 7.8 %copy-start.3 = (bf16[1024,128]{1,0:T(8,128)(2,1)}, bf16[1024,128]{1,0:T(8,128)(2,1)S(1)}, u32[]{:S(2)}) copy-start(bf16[1024,128]{1,0:T(8,128)(2,1)S(1)} %collective-permute-done.1.refs_3_) | copy-start | bytes 786436
  29.3 6.8 %collective-permute-start.6 = (bf16[1024,128]{1,0:T(8,128)(2,1)S(1)}, bf16[1024,128]{1,0:T(8,128)(2,1)S(1)}, u32[]{:S(2)}, u32[]{:S(2)}) collective-permute-start(bf16[1024,128]{1,0:T(8,128)(2,1)S(1)} %collective-permute-done.1.refs_3_), channel_id=1, source_target_pairs={{0,1},{1,0},{2,3},{3,2},{4,5},{5,4},{6,7},{7,6},{8,9},{9,8},{10,11... | collective-permute-start | bytes 786440 | tf_op jit(solution)/shard_map/ppermute | solution.py:64
  29.4 6.1 %collective-permute-start.3 = (bf16[512,128]{1,0:T(8,128)(2,1)S(1)}, bf16[512,128]{1,0:T(8,128)(2,1)S(1)}, u32[]{:S(2)}, u32[]{:S(2)}) collective-permute-start(bf16[512,128]{1,0:T(8,128)(2,1)S(1)} %slice.21), channel_id=1, source_target_pairs={{0,6},{1,7},{2,0},{3,1},{4,2},{5,3},{6,4},{7,5},{8,14},{9,15},{10,... | collective-permute-start | bytes 393224 | tf_op jit(solution)/shard_map/ppermute | solution.py:64
  33.9 3.1 %copy-start.13 = (bf16[512,128]{1,0:T(8,128)(2,1)}, bf16[512,128]{1,0:T(8,128)(2,1)S(1)}, u32[]{:S(2)}) copy-start(bf16[512,128]{1,0:T(8,128)(2,1)S(1)} %collective-permute-done.2.refs_4_) | copy-start | bytes 393220
  33.9 2.6 %collective-permute-start.7 = (bf16[512,128]{1,0:T(8,128)(2,1)S(1)}, bf16[512,128]{1,0:T(8,128)(2,1)S(1)}, u32[]{:S(2)}, u32[]{:S(2)}) collective-permute-start(bf16[512,128]{1,0:T(8,128)(2,1)S(1)} %collective-permute-done.2.refs_4_), channel_id=1, source_target_pairs={{0,1},{1,0},{2,3},{3,2},{4,5},{5,4},{6,7},{7,6},{8,9},{9,8},{10,11... | collective-permute-start | bytes 393224 | tf_op jit(solution)/shard_map/ppermute | solution.py:64
  35.5 1.5 %copy-start.14 = (bf16[512,128]{1,0:T(8,128)(2,1)}, bf16[512,128]{1,0:T(8,128)(2,1)S(1)}, u32[]{:S(2)}) copy-start(bf16[512,128]{1,0:T(8,128)(2,1)S(1)} %collective-permute-done.3.refs_5_) | copy-start | bytes 393220
  35.5 1.5 %collective-permute-start.8 = (bf16[512,128]{1,0:T(8,128)(2,1)S(1)}, bf16[512,128]{1,0:T(8,128)(2,1)S(1)}, u32[]{:S(2)}, u32[]{:S(2)}) collective-permute-start(bf16[512,128]{1,0:T(8,128)(2,1)S(1)} %collective-permute-done.3.refs_5_), channel_id=1, source_target_pairs={{0,1},{1,0},{2,3},{3,2},{4,5},{5,4},{6,7},{7,6},{8,9},{9,8},{10,11... | collective-permute-start | bytes 393224 | tf_op jit(solution)/shard_map/ppermute | solution.py:64
  36.0 1.0 copy-start.7
  36.0 1.0 copy-start.8
  36.0 1.0 copy-start.9
  36.5 0.6 copy-start.15
  37.0 0.6 copy-start.16
  37.6 0.9 copy-start
  43.1 21.9 %all-to-all-start.1 = ((bf16[8,176,128]{2,1,0:T(8,128)(2,1)}), bf16[8,176,128]{2,1,0:T(8,128)(2,1)S(1)}, u32[]{:S(2)}, u32[]{:S(2)}) async-start(bf16[8,176,128]{2,1,0:T(8,128)(2,1)} %get-tuple-element.18), calls=%async_computation.1 | async-start | bytes 720896 | tf_op jit(solution)/shard_map/all_to_all | solution.py:56
  65.0 0.7 copy-start.4
  67.6 11.3 %all-to-all-start.2 = ((bf16[4,400,128]{2,1,0:T(8,128)(2,1)}), bf16[4,400,128]{2,1,0:T(8,128)(2,1)S(1)}, u32[]{:S(2)}, u32[]{:S(2)}) async-start(bf16[4,400,128]{2,1,0:T(8,128)(2,1)} %get-tuple-element.26), calls=%async_computation.2 | async-start | bytes 819200 | tf_op jit(solution)/shard_map/all_to_all | solution.py:56
  71.6 21.9 %collective-permute-start.9 = (bf16[2064,128]{1,0:T(8,128)(2,1)}, bf16[2064,128]{1,0:T(8,128)(2,1)S(1)}, u32[]{:S(2)}, u32[]{:S(2)}) collective-permute-start(bf16[2064,128]{1,0:T(8,128)(2,1)} %get-tuple-element.33), channel_id=1, source_target_pairs={{14,6},{15,7},{22,14},{23,15},{30,22},{31,23},{38,30},{39,31},{46,... | collective-permute-start | bytes 1585160 | tf_op jit(solution)/shard_map/ppermute | solution.py:388
  78.9 3.9 %copy-start.1 = (bf16[4,400,128]{2,1,0:T(8,128)(2,1)}, bf16[4,400,128]{2,1,0:T(8,128)(2,1)S(1)}, u32[]{:S(2)}) copy-start(bf16[4,400,128]{2,1,0:T(8,128)(2,1)S(1)} %all-to-all-done.2.refs_0_) | copy-start | bytes 1228804
  79.0 28.9 %copy-start.5 = (bf16[32,4,8,128]{3,2,0,1:T(8,128)(2,1)}, bf16[32,4,8,128]{3,2,0,1:T(8,128)(2,1)S(1)}, u32[]{:S(2)}) copy-start(bf16[32,4,8,128]{3,2,0,1:T(8,128)(2,1)S(1)} %copy.9) | copy-start | bytes 786436
  79.0 12.3 %collective-permute-start.10 = (bf16[1024,128]{1,0:T(8,128)(2,1)S(1)}, bf16[1024,128]{1,0:T(8,128)(2,1)S(1)}, u32[]{:S(2)}, u32[]{:S(2)}) collective-permute-start(bf16[1024,128]{1,0:T(8,128)(2,1)S(1)} %bitcast.7), channel_id=1, source_target_pairs={{0,2},{1,3},{2,4},{3,5},{4,6},{5,7},{6,0},{7,1},{8,10},{9,11},{10,... | collective-permute-start | bytes 786440 | tf_op jit(solution)/shard_map/ppermute | solution.py:64
  79.1 14.3 %collective-permute-start.11 = (bf16[1024,128]{1,0:T(8,128)(2,1)S(1)}, bf16[1024,128]{1,0:T(8,128)(2,1)S(1)}, u32[]{:S(2)}, u32[]{:S(2)}) collective-permute-start(bf16[1024,128]{1,0:T(8,128)(2,1)S(1)} %bitcast.8), channel_id=1, source_target_pairs={{0,6},{1,7},{2,0},{3,1},{4,2},{5,3},{6,4},{7,5},{8,14},{9,15},{10,... | collective-permute-start | bytes 786440 | tf_op jit(solution)/shard_map/ppermute | solution.py:64
  85.5 15.7 %all-to-all-start.3 = ((bf16[8,128,128]{2,1,0:T(8,128)(2,1)}), bf16[8,128,128]{2,1,0:T(8,128)(2,1)S(1)}, u32[]{:S(2)}, u32[]{:S(2)}) async-start(bf16[8,128,128]{2,1,0:T(8,128)(2,1)} %shard_map.90), calls=%async_computation.3 | async-start | bytes 524288 | tf_op jit(solution)/shard_map/all_to_all | solution.py:56
  91.1 16.7 %collective-permute-start.14 = (bf16[1024,128]{1,0:T(8,128)(2,1)S(1)}, bf16[1024,128]{1,0:T(8,128)(2,1)S(1)}, u32[]{:S(2)}, u32[]{:S(2)}) collective-permute-start(bf16[1024,128]{1,0:T(8,128)(2,1)S(1)} %bitcast.9), channel_id=1, source_target_pairs={{0,1},{1,0},{2,3},{3,2},{4,5},{5,4},{6,7},{7,6},{8,9},{9,8},{10,11... | collective-permute-start | bytes 786440 | tf_op jit(solution)/shard_map/ppermute | solution.py:64
  91.3 16.6 %copy-start.10 = (bf16[1024,128]{1,0:T(8,128)(2,1)}, bf16[1024,128]{1,0:T(8,128)(2,1)S(1)}, u32[]{:S(2)}) copy-start(bf16[1024,128]{1,0:T(8,128)(2,1)S(1)} %collective-permute-done.10.refs_5_) | copy-start | bytes 786436
  91.3 9.1 %collective-permute-start.12 = (bf16[512,128]{1,0:T(8,128)(2,1)S(1)}, bf16[512,128]{1,0:T(8,128)(2,1)S(1)}, u32[]{:S(2)}, u32[]{:S(2)}) collective-permute-start(bf16[512,128]{1,0:T(8,128)(2,1)S(1)} %slice.23), channel_id=1, source_target_pairs={{0,2},{1,3},{2,4},{3,5},{4,6},{5,7},{6,0},{7,1},{8,10},{9,11},{10,... | collective-permute-start | bytes 393224 | tf_op jit(solution)/shard_map/ppermute | solution.py:64
  92.9 14.8 %collective-permute-start.15 = (bf16[1024,128]{1,0:T(8,128)(2,1)S(1)}, bf16[1024,128]{1,0:T(8,128)(2,1)S(1)}, u32[]{:S(2)}, u32[]{:S(2)}) collective-permute-start(bf16[1024,128]{1,0:T(8,128)(2,1)S(1)} %collective-permute-done.10.refs_5_), channel_id=1, source_target_pairs={{0,1},{1,0},{2,3},{3,2},{4,5},{5,4},{6,7},{7,6},{8,9},{9,8},{10,11... | collective-permute-start | bytes 786440 | tf_op jit(solution)/shard_map/ppermute | solution.py:64
  93.3 14.5 %copy-start.11 = (bf16[1024,128]{1,0:T(8,128)(2,1)}, bf16[1024,128]{1,0:T(8,128)(2,1)S(1)}, u32[]{:S(2)}) copy-start(bf16[1024,128]{1,0:T(8,128)(2,1)S(1)} %collective-permute-done.11.refs_6_) | copy-start | bytes 786436
  93.3 14.4 %collective-permute-start.16 = (bf16[1024,128]{1,0:T(8,128)(2,1)S(1)}, bf16[1024,128]{1,0:T(8,128)(2,1)S(1)}, u32[]{:S(2)}, u32[]{:S(2)}) collective-permute-start(bf16[1024,128]{1,0:T(8,128)(2,1)S(1)} %collective-permute-done.11.refs_6_), channel_id=1, source_target_pairs={{0,1},{1,0},{2,3},{3,2},{4,5},{5,4},{6,7},{7,6},{8,9},{9,8},{10,11... | collective-permute-start | bytes 786440 | tf_op jit(solution)/shard_map/ppermute | solution.py:64
  93.5 14.3 %copy-start.12 = (bf16[2064,128]{1,0:T(8,128)(2,1)}, bf16[2064,128]{1,0:T(8,128)(2,1)S(1)}, u32[]{:S(2)}) copy-start(bf16[2064,128]{1,0:T(8,128)(2,1)S(1)} %collective-permute-done.9.refs_2_) | copy-start | bytes 1585156
  93.5 7.6 %collective-permute-start.13 = (bf16[512,128]{1,0:T(8,128)(2,1)S(1)}, bf16[512,128]{1,0:T(8,128)(2,1)S(1)}, u32[]{:S(2)}, u32[]{:S(2)}) collective-permute-start(bf16[512,128]{1,0:T(8,128)(2,1)S(1)} %slice.24), channel_id=1, source_target_pairs={{0,6},{1,7},{2,0},{3,1},{4,2},{5,3},{6,4},{7,5},{8,14},{9,15},{10,... | collective-permute-start | bytes 393224 | tf_op jit(solution)/shard_map/ppermute | solution.py:64
  100.4 7.5 %copy-start.20 = (bf16[512,128]{1,0:T(8,128)(2,1)}, bf16[512,128]{1,0:T(8,128)(2,1)S(1)}, u32[]{:S(2)}) copy-start(bf16[512,128]{1,0:T(8,128)(2,1)S(1)} %collective-permute-done.12.refs_7_) | copy-start | bytes 393220
  100.4 7.4 %collective-permute-start.17 = (bf16[512,128]{1,0:T(8,128)(2,1)S(1)}, bf16[512,128]{1,0:T(8,128)(2,1)S(1)}, u32[]{:S(2)}, u32[]{:S(2)}) collective-permute-start(bf16[512,128]{1,0:T(8,128)(2,1)S(1)} %collective-permute-done.12.refs_7_), channel_id=1, source_target_pairs={{0,1},{1,0},{2,3},{3,2},{4,5},{5,4},{6,7},{7,6},{8,9},{9,8},{10,11... | collective-permute-start | bytes 393224 | tf_op jit(solution)/shard_map/ppermute | solution.py:64
  101.1 6.7 %copy-start.21 = (bf16[512,128]{1,0:T(8,128)(2,1)}, bf16[512,128]{1,0:T(8,128)(2,1)S(1)}, u32[]{:S(2)}) copy-start(bf16[512,128]{1,0:T(8,128)(2,1)S(1)} %collective-permute-done.13.refs_8_) | copy-start | bytes 393220
  101.1 6.7 %collective-permute-start.18 = (bf16[512,128]{1,0:T(8,128)(2,1)S(1)}, bf16[512,128]{1,0:T(8,128)(2,1)S(1)}, u32[]{:S(2)}, u32[]{:S(2)}) collective-permute-start(bf16[512,128]{1,0:T(8,128)(2,1)S(1)} %collective-permute-done.13.refs_8_), channel_id=1, source_target_pairs={{0,1},{1,0},{2,3},{3,2},{4,5},{5,4},{6,7},{7,6},{8,9},{9,8},{10,11... | collective-permute-start | bytes 393224 | tf_op jit(solution)/shard_map/ppermute | solution.py:64
  101.2 0.7 copy-start.6
  107.7 0.7 copy-start.17
  107.8 0.8 copy-start.18
  107.8 0.9 copy-start.19
  107.8 0.9 copy-start.22
  107.8 0.9 copy-start.23

commit v3 on v2

--- a/solution.py
+++ b/solution.py
@@ -21,25 +21,46 @@
 BOTH = ("seq", "ch")
 ALONG_Z = [[x * ZS + z for z in range(ZS)] for x in range(XS)]
 ALONG_X = [[x * ZS + z for x in range(XS)] for z in range(ZS)]
+GRANT = 20 * 1024 * 1024
 SCORE_SCALE = 4.0 * CIN ** (-0.5)
 
 VMEM = pl.BlockSpec(memory_space=pltpu.VMEM)
-
-
-def call(body, out, ins, flops=0, scratch=(), after=()):
-    n = len(ins)
+HBM = pl.BlockSpec(memory_space=pltpu.HBM)
+
+
+def call(body, out, ins, flops=0, scratch=(), after=(), held=(), grant=True):
+    n, m = len(ins), len(ins) + len(after) + len(out) + len(scratch)
 
     def kernel(*refs):
-        body(*refs[:n], *refs[n + len(after) :])
+        given, rest = list(refs[:n]), refs[n + len(after) : m]
+        if not held:
+            return body(*given, *rest)
+        copies = []
+        for k, i in enumerate(held):
+            copies.append(pltpu.make_async_copy(given[i], refs[m + k], refs[m + len(held) + k]))
+            given[i] = refs[m + k]
+        for copy in copies:
+            copy.start()
+
+        def wait():
+            for copy in copies:
+                copy.wait()
+
+        body(wait, *given, *rest)
 
     moved = sum(a.size * a.dtype.itemsize for a in ins) + sum(o.size * o.dtype.itemsize for o in out)
     return pl.pallas_call(
         kernel,
         out_shape=out,
-        in_specs=[VMEM] * n + [pl.BlockSpec(memory_space=pl.ANY)] * len(after),
+        in_specs=[HBM if i in held else VMEM for i in range(n)] + [pl.BlockSpec(memory_space=pl.ANY)] * len(after),
         out_specs=[VMEM] * len(out),
-        scratch_shapes=list(scratch),
+        scratch_shapes=[
+            *scratch,
+            *[pltpu.VMEM(ins[i].shape, ins[i].dtype) for i in held],
+            *[pltpu.SemaphoreType.DMA for _ in held],
+        ],
         cost_estimate=pl.CostEstimate(flops=flops, bytes_accessed=moved, transcendentals=0),
+        compiler_params=pltpu.CompilerParams(vmem_limit_bytes=GRANT) if grant else None,
     )(*ins, *after)
 
 
@@ -128,10 +149,10 @@
     return acc
 
 
-def project_kernel(part, *refs):
+def project_kernel(wait, part, *refs):
     mine, theirs = refs[0:5], refs[5:10]
-    k_out, v_out, packet, cum_out, mask_out = refs[10:15]
-    gates, places = refs[15:17]
+    packet, cum_out, mask_out = refs[10:13]
+    gates, places = refs[13:15]
     for c in range(NCH):
         info = part[c, PART : PART + 16, :].astype(F32)
         for p in range(3):
@@ -153,15 +174,14 @@
     tail_t = jnp.exp(total - cum).T
     mask_t = mask_out[...].T
     pairs = paired(part, D, 3 * D)
+    wait()
     state = jnp.zeros((D, D), F32)
     size = 256
     for r in range(BLOCK // size):
         lo = r * size
         acc = encoded_dot(mine, theirs, pairs, lo, size)
         keys = acc[:, 0:D].astype(BF16)
-        k_out[lo : lo + size] = keys
         values = (acc[:, D:].astype(BF16).astype(F32) * column(mask_t, r)).astype(BF16)
-        v_out[lo : lo + size] = values
         scaled = (keys.astype(F32) * column(tail_t, r)).astype(BF16)
         state += lax.dot_general(scaled, values, (((0,), (0,)), ((), ())), preferred_element_type=F32)
     hot = (places[:, 0:1].astype(jnp.int32) == lax.broadcasted_iota(jnp.int32, (K * NCH, BLOCK), 1)).astype(F32)
@@ -179,18 +199,24 @@
 FAR = K * ROW
 
 
-def intra_kernel(part, *refs):
+def intra_kernel(wait, part, *refs):
     mine, theirs = refs[0:5], refs[5:10]
-    k, v, cum, masks = refs[10:14]
-    q, out, window, halo = refs[14:18]
-    pairs = paired(part, 0, D)
+    cum, masks = refs[10:12]
+    q, out, window, halo = refs[12:16]
+    pairs = paired(part, 0, 3 * D)
+    mask_t = masks[...].T
+    wait()
+    k, v = [], []
     size = 256
     cum_rows = cum[...]
     cum_t = cum_rows.T
     lower = lax.broadcasted_iota(jnp.int32, (size, size), 0) >= lax.broadcasted_iota(jnp.int32, (size, size), 1)
     for r in range(BLOCK // size):
         here = column(cum_t, r)
-        queries = encoded_dot(mine, theirs, pairs, r * size, size).astype(BF16)
+        acc = encoded_dot(mine, theirs, pairs, r * size, size)
+        queries = acc[:, 0:D].astype(BF16)
+        k.append(acc[:, D : 2 * D].astype(BF16))
+        v.append((acc[:, 2 * D :].astype(BF16).astype(F32) * column(mask_t, r)).astype(BF16))
         q[r * size : (r + 1) * size] = queries
         acc = jnp.zeros((size, D), F32)
         for s in range(r + 1):
@@ -198,9 +224,9 @@
             if s == r:
                 diff = jnp.where(lower, diff, -jnp.inf)
             scores = lax.dot_general(
-                queries, k[s * size : (s + 1) * size], (((1,), (1,)), ((), ())), preferred_element_type=F32
+                queries, k[s], (((1,), (1,)), ((), ())), preferred_element_type=F32
             )
-            acc += jnp.dot((scores * jnp.exp(diff)).astype(BF16), v[s * size : (s + 1) * size], preferred_element_type=F32)
+            acc += jnp.dot((scores * jnp.exp(diff)).astype(BF16), v[s], preferred_element_type=F32)
         out[r * size : (r + 1) * size] = acc
     _, _, y_at, core = place()
     ys = homes(y_at)
@@ -256,13 +282,14 @@
             packet[x, D + 16 + z * n : D + 16 + (z + 1) * n, :] = z_in[z, D + 16 : D + 16 + n, :]
 
 
-def finish_kernel(x_in, here, before, q, intra, cum, gain, out):
+def finish_kernel(wait, x_in, here, before, q, intra, cum, gain, out):
     x_at = place()[0]
     state = jnp.zeros((D, D), F32)
     for x in range(XS):
         log = log_of(x_in[x, D : D + 16, :])
         state = jnp.where(x < x_at, state * jnp.exp(log) + x_in[x, 0:D, :].astype(F32), state)
     incoming = (state * jnp.exp(before[0:1]) + here[...]).astype(BF16)
+    wait()
     grow_t = jnp.exp(cum[...]).T
     scale = gain[:, pl.ds(pl.multiple_of(lax.axis_index("ch") * D, D), D)]
     size = 256
@@ -276,25 +303,26 @@
         out[2 * r + 1] = context[LEN:]
 
 
-def predict_kernel(ctx, w, context, predicted):
-    j = pl.program_id(0)
+def predict_kernel(ctx, w, context, predicted, held, sems):
+    copies = [pltpu.make_async_copy(w.at[j], held.at[j], sems.at[j]) for j in range(K)]
+    for copy in copies:
+        copy.start()
     whole = jnp.concatenate([ctx[h] for h in range(HEADS)], axis=1)
-
-    @pl.when(j == 0)
-    def _():
-        context[...] = whole
-
-    predicted[0] = jnp.dot(whole, w[0], preferred_element_type=F32).astype(BF16)
+    context[...] = whole
+    for j in range(K):
+        copies[j].wait()
+        predicted[j] = jnp.dot(whole, held[j], preferred_element_type=F32).astype(BF16)
 
 
 def predict(ctx, w_pred):
     return pl.pallas_call(
         predict_kernel,
-        grid=(K,),
         out_shape=[shape((LEN, CIN), BF16), shape((K, LEN, CIN), BF16)],
-        in_specs=[pl.BlockSpec((HEADS, LEN, D), lambda j: (0, 0, 0)), pl.BlockSpec((1, CIN, CIN), lambda j: (j, 0, 0))],
-        out_specs=[pl.BlockSpec((LEN, CIN), lambda j: (0, 0)), pl.BlockSpec((1, LEN, CIN), lambda j: (j, 0, 0))],
+        in_specs=[VMEM, HBM],
+        out_specs=[VMEM, VMEM],
+        scratch_shapes=[pltpu.VMEM((K, CIN, CIN), BF16), pltpu.SemaphoreType.DMA((K,))],
         name="predict",
+        compiler_params=pltpu.CompilerParams(vmem_limit_bytes=GRANT),
         cost_estimate=pl.CostEstimate(flops=K * 2 * LEN * CIN * CIN, bytes_accessed=K * 2 * CIN * CIN, transcendentals=0),
     )(ctx, w_pred)
 
@@ -358,16 +386,16 @@
     mine, theirs = spread(features)
     (packed,) = call(
         pack_kernel, [shape((HEADS, PART + 16, 3 * D), BF16)],
-        [w_qkv, log_gate, patch_mask.reshape(1, -1), neg_index.T],
+        [w_qkv, log_gate, patch_mask.reshape(1, -1), neg_index.T], grant=False,
     )
     w_part = exchange(packed, "ch")
     pieces = [w_part, *mine, *theirs]
     whole = shape((BLOCK, D), BF16)
     n = K * NCH
-    keys, values, packet, cumul, masks = call(
+    packet, cumul, masks = call(
         project_kernel,
-        [whole, whole, shape((ZS, D + 16 + n, D), BF16), shape((NCH, LEN), F32), shape((NCH, LEN), F32)],
-        pieces,
+        [shape((ZS, D + 16 + n, D), BF16), shape((NCH, LEN), F32), shape((NCH, LEN), F32)],
+        pieces, held=(1,),
         flops=2 * BLOCK * CIN * 2 * D,
         scratch=[pltpu.VMEM((3, NCH, LEN), F32), pltpu.VMEM((n, D), F32)],
     )
@@ -375,7 +403,7 @@
     queries, intra, window, halo = call(
         intra_kernel,
         [whole, shape((BLOCK, D), F32), shape((LEN + FAR, CIN), BF16), shape((NCH * FAR + 16, D), BF16)],
-        [*pieces, keys, values, cumul, masks],
+        [*pieces, cumul, masks], held=(1,),
         flops=2 * BLOCK * (BLOCK + CIN) * D,
     )
     x_packet, here, before = call(
@@ -388,7 +416,7 @@
     halo = lax.ppermute(halo, BOTH, pairs)
     (context,) = call(
         finish_kernel, [shape((NCH, LEN, D), BF16)],
-        [x_in, here, before, queries, intra, cumul, norm_gain.reshape(1, -1)], flops=2 * BLOCK * D * D,
+        [x_in, here, before, queries, intra, cumul, norm_gain.reshape(1, -1)], held=(3, 4, 6), flops=2 * BLOCK * D * D,
     )
     bank = x_in[:, D + 16 :].reshape(XS * ZS, K, NCH, D).transpose(1, 0, 2, 3).reshape(K * NSEQ * NCH, D)
     context = exchange(context, "ch")

time: 114 us -> 107 us (0.939)
  Pallas kernels: 27.2 us -> 16.8 us
  local copies, waits for them, and re-layouts: 3.94 us -> 9.68 us
  waiting for transfers between devices: 38.7 us -> 36.3 us
    pallas_call x7, Pallas kernels: 27.2 us -> 16.8 us  [the longest x6 14.1 us: call(): pl.pallas_call(kernel, out_shape=out, in_specs=[HBM if i in held else VME...]
    unnamed x48 -> x22, local copies, waits for them, and re-layouts: 3.84 us -> 9.57 us
    all_to_all x4, waiting for transfers between devices: 15.3 us -> 12.9 us  [exchange(): lax.all_to_all(x, axis, split_axis=0, concat_axis=0, axis_index_groups=gr...]
  transfers between devices with their start and end apart: 23 -> 23, of which waited for: 7 -> 7; matrix products, arithmetic and copies ran while one was open for 0% -> 0% of each run, Pallas kernels for 13% -> 7%
where the time goes in v3:
time: 107 us
  starting transfers between devices  43 us (40%)
  waiting for transfers between devices  36.3 us (34%)
  Pallas kernels  16.8 us (16%)
  local copies, waits for them, and re-layouts  9.68 us (9%)
    all_to_all x4, starting transfers between devices, exchange(): lax.all_to_all(x, axis, split_axis=0, concat_axis=0, axis_index_groups=gr...  23.7 us
    ppermute x18, waiting for transfers between devices, hop(): return lax.ppermute(x, 'ch', pairs)  23.4 us
    ppermute x18, starting transfers between devices, hop(): return lax.ppermute(x, 'ch', pairs)  17.8 us
    pallas_call x6, Pallas kernels, call(): pl.pallas_call(kernel, out_shape=out, in_specs=[HBM if i in held else VME...  14.1 us
    all_to_all x4, waiting for transfers between devices, exchange(): lax.all_to_all(x, axis, split_axis=0, concat_axis=0, axis_index_groups=gr...  12.9 us
    unnamed x22, local copies, waits for them, and re-layouts  9.57 us
    pallas_call x1, Pallas kernels, predict(): pl.pallas_call(predict_kernel, out_shape=[shape((LEN, CIN), BF16), shape(...  2.67 us
  transfers between devices with their start and end apart: 23, of which 7 were waited for; matrix products, arithmetic and copies ran while one was open for 0% of the time, Pallas kernels for 7%

profile of v3, /device:TPU:1, one launch (start us, length us, event | category | flops | bytes accessed | tf_op | source)
XLA Modules:
  0.0 106.5 jit_solution(13708377278784701251)
XLA Ops:
  0.6 2.2 %shard_map.86 = bf16[8,144,384]{2,1,0:T(8,128)(2,1)} custom-call(bf16[128,3072]{1,0:T(8,128)(2,1)} %refs_0_.1, f32[8,128]{1,0:T(8,128)} %refs_1_.3, s32[1,128]{1,0:T(1,128)} %bitcast.13, s32[1,4]{1,0:T(1,128)} %bitcast.14), custom_call_target="tpu_custom_call" | custom-call | bytes 1675792 | tf_op jit(solution)/shard_map/pallas_call | solution.py:52
  2.9 6.7 %all-to-all-start = ((bf16[8,144,384]{2,1,0:T(8,128)(2,1)}), bf16[8,144,384]{2,1,0:T(8,128)(2,1)S(1)}, u32[]{:S(2)}, u32[]{:S(2)}) async-start(bf16[8,144,384]{2,1,0:T(8,128)(2,1)} %shard_map.86), calls=%async_computation | async-start | bytes 1769472 | tf_op jit(solution)/shard_map/all_to_all | solution.py:77
  9.5 1.4 %collective-permute-start = (bf16[1024,128]{1,0:T(8,128)(2,1)}, bf16[1024,128]{1,0:T(8,128)(2,1)S(1)}, u32[]{:S(2)}, u32[]{:S(2)}) collective-permute-start(bf16[1024,128]{1,0:T(8,128)(2,1)} %refs_1_.5), channel_id=1, source_target_pairs={{0,2},{1,3},{2,4},{3,5},{4,6},{5,7},{6,0},{7,1},{8,10},{9,11},{10,... | collective-permute-start | bytes 786440 | tf_op jit(solution)/shard_map/ppermute | solution.py:85
  10.9 1.3 %collective-permute-start.1 = (bf16[1024,128]{1,0:T(8,128)(2,1)}, bf16[1024,128]{1,0:T(8,128)(2,1)S(1)}, u32[]{:S(2)}, u32[]{:S(2)}) collective-permute-start(bf16[1024,128]{1,0:T(8,128)(2,1)} %refs_1_.5), channel_id=1, source_target_pairs={{0,6},{1,7},{2,0},{3,1},{4,2},{5,3},{6,4},{7,5},{8,14},{9,15},{10,... | collective-permute-start | bytes 786440 | tf_op jit(solution)/shard_map/ppermute | solution.py:85
  12.2 0.7 collective-permute-start.4
  12.9 15.4 %collective-permute-done.refs_2_ = bf16[1024,128]{1,0:T(8,128)(2,1)S(1)} collective-permute-done((bf16[1024,128]{1,0:T(8,128)(2,1)}, bf16[1024,128]{1,0:T(8,128)(2,1)S(1)}, u32[]{:S(2)}, u32[]{:S(2)}) %collective-permute-start) | collective-permute-done | bytes 262176 | tf_op jit(solution)/shard_map/ppermute | solution.py:85
  28.3 0.1 collective-permute-start.2
  28.4 0.9 collective-permute-start.5
  29.3 0.1 collective-permute-start.6
  29.4 2.9 %collective-permute-start.3 = (bf16[512,128]{1,0:T(8,128)(2,1)S(1)}, bf16[512,128]{1,0:T(8,128)(2,1)S(1)}, u32[]{:S(2)}, u32[]{:S(2)}) collective-permute-start(bf16[512,128]{1,0:T(8,128)(2,1)S(1)} %slice.21), channel_id=1, source_target_pairs={{0,6},{1,7},{2,0},{3,1},{4,2},{5,3},{6,4},{7,5},{8,14},{9,15},{10,... | collective-permute-start | bytes 393224 | tf_op jit(solution)/shard_map/ppermute | solution.py:85
  32.3 1.6 %collective-permute-done.2.refs_4_ = bf16[512,128]{1,0:T(8,128)(2,1)S(1)} collective-permute-done((bf16[512,128]{1,0:T(8,128)(2,1)S(1)}, bf16[512,128]{1,0:T(8,128)(2,1)S(1)}, u32[]{:S(2)}, u32[]{:S(2)}) %collective-permute-start.2) | collective-permute-done | bytes 131104 | tf_op jit(solution)/shard_map/ppermute | solution.py:85
  33.9 1.6 %collective-permute-start.7 = (bf16[512,128]{1,0:T(8,128)(2,1)S(1)}, bf16[512,128]{1,0:T(8,128)(2,1)S(1)}, u32[]{:S(2)}, u32[]{:S(2)}) collective-permute-start(bf16[512,128]{1,0:T(8,128)(2,1)S(1)} %collective-permute-done.2.refs_4_), channel_id=1, source_target_pairs={{0,1},{1,0},{2,3},{3,2},{4,5},{5,4},{6,7},{7,6},{8,9},{9,8},{10,11... | collective-permute-start | bytes 393224 | tf_op jit(solution)/shard_map/ppermute | solution.py:85
  35.5 0.0 collective-permute-done.3.refs_5_
  35.5 0.5 collective-permute-start.8
  36.0 0.5 collective-permute-done.7.refs_9_
  36.5 0.5 collective-permute-done.8.refs_10_
  37.0 1.0 copy-done.1
  38.0 3.1 %shard_map.87 = (bf16[8,176,128]{2,1,0:T(8,128)(2,1)}, f32[8,128]{1,0:T(8,128)S(1)}, f32[8,128]{1,0:T(8,128)S(1)}) custom-call(bf16[8,144,384]{2,1,0:T(8,128)(2,1)S(1)} %all-to-all-done.refs_0_, bf16[1024,128]{1,0:T(8,128)(2,1)S(1)} %copy-done.1, bf16[1024,128]{1,0:T(8,128)(2,1)S(1)} %collective-permute-done.refs_2_, ...), custom_call_target="tpu_custom_call" | custom-call | flops 536870912 | bytes 3350528 | tf_op jit(solution)/shard_map/pallas_call | solution.py:52
  41.1 7.5 %all-to-all-start.1 = ((bf16[8,176,128]{2,1,0:T(8,128)(2,1)}), bf16[8,176,128]{2,1,0:T(8,128)(2,1)S(1)}, u32[]{:S(2)}, u32[]{:S(2)}) async-start(bf16[8,176,128]{2,1,0:T(8,128)(2,1)} %get-tuple-element.16), calls=%async_computation.1 | async-start | bytes 720896 | tf_op jit(solution)/shard_map/all_to_all | solution.py:77
  48.6 0.0 copy-start.2
  48.6 0.9 copy-done.2
  49.5 0.9 copy-done.6
  50.4 3.1 %shard_map.88 = (bf16[1024,128]{1,0:T(8,128)(2,1)S(1)}, f32[1024,128]{1,0:T(8,128)S(1)}, bf16[384,1024]{1,0:T(8,128)(2,1)S(1)}, bf16[2064,128]{1,0:T(8,128)(2,1)S(1)}) custom-call(bf16[8,144,384]{2,1,0:T(8,128)(2,1)S(1)} %all-to-all-done.refs_0_, bf16[1024,128]{1,0:T(8,128)(2,1)S(1)} %copy-done.2, bf16[1024,128]{1,0:T(8,128)(2,1)S(1)} %collective-permute-done.refs_2_, ...), custom_call_target="tpu_custom_call" | custom-call | flops 536870912 | bytes 5091328 | tf_op jit(solution)/shard_map/pallas_call | solution.py:52
  53.5 0.9 copy-done.3
  54.4 0.7 copy-done.7
  55.1 0.8 copy-done.10
  55.9 7.1 %all-to-all-done.1.refs_0_ = bf16[8,176,128]{2,1,0:T(8,128)(2,1)S(1)} async-done(((bf16[8,176,128]{2,1,0:T(8,128)(2,1)}), bf16[8,176,128]{2,1,0:T(8,128)(2,1)S(1)}, u32[]{:S(2)}, u32[]{:S(2)}) %all-to-all-start.1) | async-done | bytes 360480 | tf_op jit(solution)/shard_map/all_to_all | solution.py:77
  63.0 0.8 shard_map.89
  63.8 4.0 %all-to-all-start.2 = ((bf16[4,400,128]{2,1,0:T(8,128)(2,1)}), bf16[4,400,128]{2,1,0:T(8,128)(2,1)S(1)}, u32[]{:S(2)}, u32[]{:S(2)}) async-start(bf16[4,400,128]{2,1,0:T(8,128)(2,1)} %get-tuple-element.22), calls=%async_computation.2 | async-start | bytes 819200 | tf_op jit(solution)/shard_map/all_to_all | solution.py:77
  67.9 1.5 %collective-permute-start.9 = (bf16[2064,128]{1,0:T(8,128)(2,1)}, bf16[2064,128]{1,0:T(8,128)(2,1)}, u32[]{:S(2)}, u32[]{:S(2)}) collective-permute-start(bf16[2064,128]{1,0:T(8,128)(2,1)} %copy-done.10), channel_id=1, source_target_pairs={{14,6},{15,7},{22,14},{23,15},{30,22},{31,23},{38,30},{39,31},{46,... | collective-permute-start | bytes 1585160 | tf_op jit(solution)/shard_map/ppermute | solution.py:416
  69.3 5.8 %all-to-all-done.2.refs_0_ = bf16[4,400,128]{2,1,0:T(8,128)(2,1)S(1)} async-done(((bf16[4,400,128]{2,1,0:T(8,128)(2,1)}), bf16[4,400,128]{2,1,0:T(8,128)(2,1)S(1)}, u32[]{:S(2)}, u32[]{:S(2)}) %all-to-all-start.2) | async-done | bytes 409632 | tf_op jit(solution)/shard_map/all_to_all | solution.py:77
  75.2 0.1 collective-permute-start.10
  75.3 3.7 %collective-permute-start.11 = (bf16[1024,128]{1,0:T(8,128)(2,1)S(1)}, bf16[1024,128]{1,0:T(8,128)(2,1)S(1)}, u32[]{:S(2)}, u32[]{:S(2)}) collective-permute-start(bf16[1024,128]{1,0:T(8,128)(2,1)S(1)} %bitcast.8), channel_id=1, source_target_pairs={{0,6},{1,7},{2,0},{3,1},{4,2},{5,3},{6,4},{7,5},{8,14},{9,15},{10,... | collective-permute-start | bytes 786440 | tf_op jit(solution)/shard_map/ppermute | solution.py:85
  78.9 0.9 copy-done.8
  79.9 1.7 %shard_map.90 = bf16[8,128,128]{2,1,0:T(8,128)(2,1)} custom-call(bf16[4,400,128]{2,1,0:T(8,128)(2,1)S(1)} %all-to-all-done.2.refs_0_, f32[128,128]{1,0:T(8,128)S(1)} %get-tuple-element.23.refs_1_, f32[8,128]{1,0:T(8,128)S(1)} %get-tuple-element.24.refs_2_, bf16[1024,128]{1,0:T(8,128)(2,1)S(1)} %copy-done.8, ...), custom_call_target="tpu_custom_call" | custom-call | flops 33554432 | bytes 1536000 | tf_op jit(solution)/shard_map/pallas_call | solution.py:52
  81.6 5.6 %all-to-all-start.3 = ((bf16[8,128,128]{2,1,0:T(8,128)(2,1)}), bf16[8,128,128]{2,1,0:T(8,128)(2,1)S(1)}, u32[]{:S(2)}, u32[]{:S(2)}) async-start(bf16[8,128,128]{2,1,0:T(8,128)(2,1)} %shard_map.90), calls=%async_computation.3 | async-start | bytes 524288 | tf_op jit(solution)/shard_map/all_to_all | solution.py:77
  87.2 0.2 collective-permute-start.14
  87.4 1.6 %collective-permute-start.12 = (bf16[512,128]{1,0:T(8,128)(2,1)S(1)}, bf16[512,128]{1,0:T(8,128)(2,1)S(1)}, u32[]{:S(2)}, u32[]{:S(2)}) collective-permute-start(bf16[512,128]{1,0:T(8,128)(2,1)S(1)} %slice.23), channel_id=1, source_target_pairs={{0,2},{1,3},{2,4},{3,5},{4,6},{5,7},{6,0},{7,1},{8,10},{9,11},{10,... | collective-permute-start | bytes 393224 | tf_op jit(solution)/shard_map/ppermute | solution.py:85
  89.0 0.4 collective-permute-start.15
  89.4 0.2 collective-permute-start.16
  89.6 1.3 %collective-permute-start.13 = (bf16[512,128]{1,0:T(8,128)(2,1)S(1)}, bf16[512,128]{1,0:T(8,128)(2,1)S(1)}, u32[]{:S(2)}, u32[]{:S(2)}) collective-permute-start(bf16[512,128]{1,0:T(8,128)(2,1)S(1)} %slice.24), channel_id=1, source_target_pairs={{0,6},{1,7},{2,0},{3,1},{4,2},{5,3},{6,4},{7,5},{8,14},{9,15},{10,... | collective-permute-start | bytes 393224 | tf_op jit(solution)/shard_map/ppermute | solution.py:85
  91.0 5.5 %collective-permute-done.12.refs_7_ = bf16[512,128]{1,0:T(8,128)(2,1)S(1)} collective-permute-done((bf16[512,128]{1,0:T(8,128)(2,1)S(1)}, bf16[512,128]{1,0:T(8,128)(2,1)S(1)}, u32[]{:S(2)}, u32[]{:S(2)}) %collective-permute-start.12) | collective-permute-done | bytes 131104 | tf_op jit(solution)/shard_map/ppermute | solution.py:85
  96.4 0.8 collective-permute-start.17
  97.2 0.0 collective-permute-start.18
  97.2 0.0 copy-start
  97.2 3.4 %copy-done = bf16[4,1024,1024]{2,1,0:T(8,128)(2,1)S(1)} copy-done((bf16[4,1024,1024]{2,1,0:T(8,128)(2,1)S(1)}, bf16[4,1024,1024]{2,1,0:T(8,128)(2,1)}, u32[]{:S(2)}) %copy-start) | copy-done | bytes 8388632
  100.6 2.7 %predict.1 = (bf16[128,1024]{1,0:T(8,128)(2,1)}, bf16[4,128,1024]{2,1,0:T(8,128)(2,1)S(1)}) custom-call(bf16[8,128,128]{2,1,0:T(8,128)(2,1)S(1)} %all-to-all-done.3.ctx, bf16[4,1024,1024]{2,1,0:T(8,128)(2,1)S(1)} %copy-done), custom_call_target="tpu_custom_call" | custom-call | flops 1073741824 | bytes 8388608 | tf_op jit(solution)/shard_map/predict/pallas_call | solution.py:318
  103.4 3.2 %shard_map.91 = f32[4,128]{1,0:T(4,128)} custom-call(bf16[4,128,1024]{2,1,0:T(8,128)(2,1)S(1)} %get-tuple-element.27.refs_0_, bf16[384,1024]{1,0:T(8,128)(2,1)S(1)} %copy-done.4, bf16[2064,128]{1,0:T(8,128)(2,1)} %collective-permute-done.9.refs_2_, f32[8,128]{1,0:T(8,128)S(1)} %get-tuple-element.18.refs_12_.refs_3_, bf16[1024,128]{1,0:T(8,128)(2,1)S(1)} %bitcast.10, ...), custom_call_target="tpu_custom_call" | custom-call | flops 268435456 | bytes 4466688 | tf_op jit(solution)/shard_map/pallas_call | solution.py:52
  (33 shorter events, 0.2 us)
Async XLA Ops:
  0.6 78.3 %copy-start.9 = (f32[1024]{0:T(1024)S(1)}, f32[1024]{0:T(1024)}, u32[]{:S(2)}) copy-start(f32[1024]{0:T(1024)} %param.10) | copy-start | bytes 12292
  2.9 34.1 %all-to-all-start = ((bf16[8,144,384]{2,1,0:T(8,128)(2,1)}), bf16[8,144,384]{2,1,0:T(8,128)(2,1)S(1)}, u32[]{:S(2)}, u32[]{:S(2)}) async-start(bf16[8,144,384]{2,1,0:T(8,128)(2,1)} %shard_map.86), calls=%async_computation | async-start | bytes 1769472 | tf_op jit(solution)/shard_map/all_to_all | solution.py:77
  9.5 18.8 %collective-permute-start = (bf16[1024,128]{1,0:T(8,128)(2,1)}, bf16[1024,128]{1,0:T(8,128)(2,1)S(1)}, u32[]{:S(2)}, u32[]{:S(2)}) collective-permute-start(bf16[1024,128]{1,0:T(8,128)(2,1)} %refs_1_.5), channel_id=1, source_target_pairs={{0,2},{1,3},{2,4},{3,5},{4,6},{5,7},{6,0},{7,1},{8,10},{9,11},{10,... | collective-permute-start | bytes 786440 | tf_op jit(solution)/shard_map/ppermute | solution.py:85
  10.9 18.4 %collective-permute-start.1 = (bf16[1024,128]{1,0:T(8,128)(2,1)}, bf16[1024,128]{1,0:T(8,128)(2,1)S(1)}, u32[]{:S(2)}, u32[]{:S(2)}) collective-permute-start(bf16[1024,128]{1,0:T(8,128)(2,1)} %refs_1_.5), channel_id=1, source_target_pairs={{0,6},{1,7},{2,0},{3,1},{4,2},{5,3},{6,4},{7,5},{8,14},{9,15},{10,... | collective-permute-start | bytes 786440 | tf_op jit(solution)/shard_map/ppermute | solution.py:85
  12.2 23.8 %collective-permute-start.4 = (bf16[1024,128]{1,0:T(8,128)(2,1)}, bf16[1024,128]{1,0:T(8,128)(2,1)S(1)}, u32[]{:S(2)}, u32[]{:S(2)}) collective-permute-start(bf16[1024,128]{1,0:T(8,128)(2,1)} %refs_1_.5), channel_id=1, source_target_pairs={{0,1},{1,0},{2,3},{3,2},{4,5},{5,4},{6,7},{7,6},{8,9},{9,8},{10,11... | collective-permute-start | bytes 786440 | tf_op jit(solution)/shard_map/ppermute | solution.py:85
  28.3 5.6 %collective-permute-start.2 = (bf16[512,128]{1,0:T(8,128)(2,1)S(1)}, bf16[512,128]{1,0:T(8,128)(2,1)S(1)}, u32[]{:S(2)}, u32[]{:S(2)}) collective-permute-start(bf16[512,128]{1,0:T(8,128)(2,1)S(1)} %slice.20), channel_id=1, source_target_pairs={{0,2},{1,3},{2,4},{3,5},{4,6},{5,7},{6,0},{7,1},{8,10},{9,11},{10,... | collective-permute-start | bytes 393224 | tf_op jit(solution)/shard_map/ppermute | solution.py:85
  28.4 7.6 %collective-permute-start.5 = (bf16[1024,128]{1,0:T(8,128)(2,1)S(1)}, bf16[1024,128]{1,0:T(8,128)(2,1)S(1)}, u32[]{:S(2)}, u32[]{:S(2)}) collective-permute-start(bf16[1024,128]{1,0:T(8,128)(2,1)S(1)} %collective-permute-done.refs_2_), channel_id=1, source_target_pairs={{0,1},{1,0},{2,3},{3,2},{4,5},{5,4},{6,7},{7,6},{8,9},{9,8},{10,11... | collective-permute-start | bytes 786440 | tf_op jit(solution)/shard_map/ppermute | solution.py:85
  29.3 6.8 %collective-permute-start.6 = (bf16[1024,128]{1,0:T(8,128)(2,1)S(1)}, bf16[1024,128]{1,0:T(8,128)(2,1)S(1)}, u32[]{:S(2)}, u32[]{:S(2)}) collective-permute-start(bf16[1024,128]{1,0:T(8,128)(2,1)S(1)} %collective-permute-done.1.refs_3_), channel_id=1, source_target_pairs={{0,1},{1,0},{2,3},{3,2},{4,5},{5,4},{6,7},{7,6},{8,9},{9,8},{10,11... | collective-permute-start | bytes 786440 | tf_op jit(solution)/shard_map/ppermute | solution.py:85
  29.4 6.1 %collective-permute-start.3 = (bf16[512,128]{1,0:T(8,128)(2,1)S(1)}, bf16[512,128]{1,0:T(8,128)(2,1)S(1)}, u32[]{:S(2)}, u32[]{:S(2)}) collective-permute-start(bf16[512,128]{1,0:T(8,128)(2,1)S(1)} %slice.21), channel_id=1, source_target_pairs={{0,6},{1,7},{2,0},{3,1},{4,2},{5,3},{6,4},{7,5},{8,14},{9,15},{10,... | collective-permute-start | bytes 393224 | tf_op jit(solution)/shard_map/ppermute | solution.py:85
  33.9 2.6 %collective-permute-start.7 = (bf16[512,128]{1,0:T(8,128)(2,1)S(1)}, bf16[512,128]{1,0:T(8,128)(2,1)S(1)}, u32[]{:S(2)}, u32[]{:S(2)}) collective-permute-start(bf16[512,128]{1,0:T(8,128)(2,1)S(1)} %collective-permute-done.2.refs_4_), channel_id=1, source_target_pairs={{0,1},{1,0},{2,3},{3,2},{4,5},{5,4},{6,7},{7,6},{8,9},{9,8},{10,11... | collective-permute-start | bytes 393224 | tf_op jit(solution)/shard_map/ppermute | solution.py:85
  35.5 1.5 %collective-permute-start.8 = (bf16[512,128]{1,0:T(8,128)(2,1)S(1)}, bf16[512,128]{1,0:T(8,128)(2,1)S(1)}, u32[]{:S(2)}, u32[]{:S(2)}) collective-permute-start(bf16[512,128]{1,0:T(8,128)(2,1)S(1)} %collective-permute-done.3.refs_5_), channel_id=1, source_target_pairs={{0,1},{1,0},{2,3},{3,2},{4,5},{5,4},{6,7},{7,6},{8,9},{9,8},{10,11... | collective-permute-start | bytes 393224 | tf_op jit(solution)/shard_map/ppermute | solution.py:85
  37.0 11.6 %copy-start.5 = (bf16[512,128]{1,0:T(8,128)(2,1)}, bf16[512,128]{1,0:T(8,128)(2,1)S(1)}, u32[]{:S(2)}) copy-start(bf16[512,128]{1,0:T(8,128)(2,1)S(1)} %collective-permute-done.8.refs_10_) | copy-start | bytes 393220
  37.0 1.0 copy-start.1
  41.1 21.9 %all-to-all-start.1 = ((bf16[8,176,128]{2,1,0:T(8,128)(2,1)}), bf16[8,176,128]{2,1,0:T(8,128)(2,1)S(1)}, u32[]{:S(2)}, u32[]{:S(2)}) async-start(bf16[8,176,128]{2,1,0:T(8,128)(2,1)} %get-tuple-element.16), calls=%async_computation.1 | async-start | bytes 720896 | tf_op jit(solution)/shard_map/all_to_all | solution.py:77
  48.6 1.0 copy-start.2
  49.5 0.9 copy-start.6
  53.5 0.9 copy-start.3
  54.4 0.7 copy-start.7
  55.1 0.8 copy-start.10
  63.0 40.4 %copy-start.4 = (bf16[384,1024]{1,0:T(8,128)(2,1)S(1)}, bf16[384,1024]{1,0:T(8,128)(2,1)}, u32[]{:S(2)}) copy-start(bf16[384,1024]{1,0:T(8,128)(2,1)} %copy-done.3) | copy-start | bytes 2359300
  63.8 11.3 %all-to-all-start.2 = ((bf16[4,400,128]{2,1,0:T(8,128)(2,1)}), bf16[4,400,128]{2,1,0:T(8,128)(2,1)S(1)}, u32[]{:S(2)}, u32[]{:S(2)}) async-start(bf16[4,400,128]{2,1,0:T(8,128)(2,1)} %get-tuple-element.22), calls=%async_computation.2 | async-start | bytes 819200 | tf_op jit(solution)/shard_map/all_to_all | solution.py:77
  67.9 21.8 %collective-permute-start.9 = (bf16[2064,128]{1,0:T(8,128)(2,1)}, bf16[2064,128]{1,0:T(8,128)(2,1)}, u32[]{:S(2)}, u32[]{:S(2)}) collective-permute-start(bf16[2064,128]{1,0:T(8,128)(2,1)} %copy-done.10), channel_id=1, source_target_pairs={{14,6},{15,7},{22,14},{23,15},{30,22},{31,23},{38,30},{39,31},{46,... | collective-permute-start | bytes 1585160 | tf_op jit(solution)/shard_map/ppermute | solution.py:416
  75.2 12.2 %collective-permute-start.10 = (bf16[1024,128]{1,0:T(8,128)(2,1)S(1)}, bf16[1024,128]{1,0:T(8,128)(2,1)S(1)}, u32[]{:S(2)}, u32[]{:S(2)}) collective-permute-start(bf16[1024,128]{1,0:T(8,128)(2,1)S(1)} %bitcast.7), channel_id=1, source_target_pairs={{0,2},{1,3},{2,4},{3,5},{4,6},{5,7},{6,0},{7,1},{8,10},{9,11},{10,... | collective-permute-start | bytes 786440 | tf_op jit(solution)/shard_map/ppermute | solution.py:85
  75.3 14.1 %collective-permute-start.11 = (bf16[1024,128]{1,0:T(8,128)(2,1)S(1)}, bf16[1024,128]{1,0:T(8,128)(2,1)S(1)}, u32[]{:S(2)}, u32[]{:S(2)}) collective-permute-start(bf16[1024,128]{1,0:T(8,128)(2,1)S(1)} %bitcast.8), channel_id=1, source_target_pairs={{0,6},{1,7},{2,0},{3,1},{4,2},{5,3},{6,4},{7,5},{8,14},{9,15},{10,... | collective-permute-start | bytes 786440 | tf_op jit(solution)/shard_map/ppermute | solution.py:85
  78.9 1.0 copy-start.8
  81.6 15.6 %all-to-all-start.3 = ((bf16[8,128,128]{2,1,0:T(8,128)(2,1)}), bf16[8,128,128]{2,1,0:T(8,128)(2,1)S(1)}, u32[]{:S(2)}, u32[]{:S(2)}) async-start(bf16[8,128,128]{2,1,0:T(8,128)(2,1)} %shard_map.90), calls=%async_computation.3 | async-start | bytes 524288 | tf_op jit(solution)/shard_map/all_to_all | solution.py:77
  87.2 16.1 %collective-permute-start.14 = (bf16[1024,128]{1,0:T(8,128)(2,1)S(1)}, bf16[1024,128]{1,0:T(8,128)(2,1)S(1)}, u32[]{:S(2)}, u32[]{:S(2)}) collective-permute-start(bf16[1024,128]{1,0:T(8,128)(2,1)S(1)} %bitcast.9), channel_id=1, source_target_pairs={{0,1},{1,0},{2,3},{3,2},{4,5},{5,4},{6,7},{7,6},{8,9},{9,8},{10,11... | collective-permute-start | bytes 786440 | tf_op jit(solution)/shard_map/ppermute | solution.py:85
  87.4 9.1 %collective-permute-start.12 = (bf16[512,128]{1,0:T(8,128)(2,1)S(1)}, bf16[512,128]{1,0:T(8,128)(2,1)S(1)}, u32[]{:S(2)}, u32[]{:S(2)}) collective-permute-start(bf16[512,128]{1,0:T(8,128)(2,1)S(1)} %slice.23), channel_id=1, source_target_pairs={{0,2},{1,3},{2,4},{3,5},{4,6},{5,7},{6,0},{7,1},{8,10},{9,11},{10,... | collective-permute-start | bytes 393224 | tf_op jit(solution)/shard_map/ppermute | solution.py:85
  89.0 14.3 %collective-permute-start.15 = (bf16[1024,128]{1,0:T(8,128)(2,1)S(1)}, bf16[1024,128]{1,0:T(8,128)(2,1)S(1)}, u32[]{:S(2)}, u32[]{:S(2)}) collective-permute-start(bf16[1024,128]{1,0:T(8,128)(2,1)S(1)} %collective-permute-done.10.refs_5_), channel_id=1, source_target_pairs={{0,1},{1,0},{2,3},{3,2},{4,5},{5,4},{6,7},{7,6},{8,9},{9,8},{10,11... | collective-permute-start | bytes 786440 | tf_op jit(solution)/shard_map/ppermute | solution.py:85
  89.4 13.9 %collective-permute-start.16 = (bf16[1024,128]{1,0:T(8,128)(2,1)S(1)}, bf16[1024,128]{1,0:T(8,128)(2,1)S(1)}, u32[]{:S(2)}, u32[]{:S(2)}) collective-permute-start(bf16[1024,128]{1,0:T(8,128)(2,1)S(1)} %collective-permute-done.11.refs_6_), channel_id=1, source_target_pairs={{0,1},{1,0},{2,3},{3,2},{4,5},{5,4},{6,7},{7,6},{8,9},{9,8},{10,11... | collective-permute-start | bytes 786440 | tf_op jit(solution)/shard_map/ppermute | solution.py:85
  89.6 7.6 %collective-permute-start.13 = (bf16[512,128]{1,0:T(8,128)(2,1)S(1)}, bf16[512,128]{1,0:T(8,128)(2,1)S(1)}, u32[]{:S(2)}, u32[]{:S(2)}) collective-permute-start(bf16[512,128]{1,0:T(8,128)(2,1)S(1)} %slice.24), channel_id=1, source_target_pairs={{0,6},{1,7},{2,0},{3,1},{4,2},{5,3},{6,4},{7,5},{8,14},{9,15},{10,... | collective-permute-start | bytes 393224 | tf_op jit(solution)/shard_map/ppermute | solution.py:85
  96.4 6.9 %collective-permute-start.17 = (bf16[512,128]{1,0:T(8,128)(2,1)S(1)}, bf16[512,128]{1,0:T(8,128)(2,1)S(1)}, u32[]{:S(2)}, u32[]{:S(2)}) collective-permute-start(bf16[512,128]{1,0:T(8,128)(2,1)S(1)} %collective-permute-done.12.refs_7_), channel_id=1, source_target_pairs={{0,1},{1,0},{2,3},{3,2},{4,5},{5,4},{6,7},{7,6},{8,9},{9,8},{10,11... | collective-permute-start | bytes 393224 | tf_op jit(solution)/shard_map/ppermute | solution.py:85
  97.2 6.1 %collective-permute-start.18 = (bf16[512,128]{1,0:T(8,128)(2,1)S(1)}, bf16[512,128]{1,0:T(8,128)(2,1)S(1)}, u32[]{:S(2)}, u32[]{:S(2)}) collective-permute-start(bf16[512,128]{1,0:T(8,128)(2,1)S(1)} %collective-permute-done.13.refs_8_), channel_id=1, source_target_pairs={{0,1},{1,0},{2,3},{3,2},{4,5},{5,4},{6,7},{7,6},{8,9},{9,8},{10,11... | collective-permute-start | bytes 393224 | tf_op jit(solution)/shard_map/ppermute | solution.py:85
  97.2 3.4 %copy-start = (bf16[4,1024,1024]{2,1,0:T(8,128)(2,1)S(1)}, bf16[4,1024,1024]{2,1,0:T(8,128)(2,1)}, u32[]{:S(2)}) copy-start(bf16[4,1024,1024]{2,1,0:T(8,128)(2,1)} %w.1) | copy-start | bytes 25165828

commit v4 on v2

--- a/solution.py
+++ b/solution.py
@@ -21,13 +21,13 @@
 BOTH = ("seq", "ch")
 ALONG_Z = [[x * ZS + z for z in range(ZS)] for x in range(XS)]
 ALONG_X = [[x * ZS + z for x in range(XS)] for z in range(ZS)]
+GRANT = 24 * 1024 * 1024
 SCORE_SCALE = 4.0 * CIN ** (-0.5)
 
-VMEM = pl.BlockSpec(memory_space=pltpu.VMEM)
-
-
-def call(body, out, ins, flops=0, scratch=(), after=()):
+
+def call(body, out, ins, flops=0, scratch=(), after=(), away=(), grant=True):
     n = len(ins)
+    away = (*away, *range(n, n + len(after)))
 
     def kernel(*refs):
         body(*refs[:n], *refs[n + len(after) :])
@@ -36,10 +36,11 @@
     return pl.pallas_call(
         kernel,
         out_shape=out,
-        in_specs=[VMEM] * n + [pl.BlockSpec(memory_space=pl.ANY)] * len(after),
-        out_specs=[VMEM] * len(out),
+        in_specs=[pl.BlockSpec(memory_space=pl.ANY) if i in away else pl.BlockSpec() for i in range(n + len(after))],
+        out_specs=[pl.BlockSpec()] * len(out),
         scratch_shapes=list(scratch),
         cost_estimate=pl.CostEstimate(flops=flops, bytes_accessed=moved, transcendentals=0),
+        compiler_params=pltpu.CompilerParams(vmem_limit_bytes=GRANT) if grant else None,
     )(*ins, *after)
 
 
@@ -130,8 +131,8 @@
 
 def project_kernel(part, *refs):
     mine, theirs = refs[0:5], refs[5:10]
-    k_out, v_out, packet, cum_out, mask_out = refs[10:15]
-    gates, places = refs[15:17]
+    packet, cum_out, mask_out = refs[10:13]
+    gates, places = refs[13:15]
     for c in range(NCH):
         info = part[c, PART : PART + 16, :].astype(F32)
         for p in range(3):
@@ -159,9 +160,7 @@
         lo = r * size
         acc = encoded_dot(mine, theirs, pairs, lo, size)
         keys = acc[:, 0:D].astype(BF16)
-        k_out[lo : lo + size] = keys
         values = (acc[:, D:].astype(BF16).astype(F32) * column(mask_t, r)).astype(BF16)
-        v_out[lo : lo + size] = values
         scaled = (keys.astype(F32) * column(tail_t, r)).astype(BF16)
         state += lax.dot_general(scaled, values, (((0,), (0,)), ((), ())), preferred_element_type=F32)
     hot = (places[:, 0:1].astype(jnp.int32) == lax.broadcasted_iota(jnp.int32, (K * NCH, BLOCK), 1)).astype(F32)
@@ -181,16 +180,21 @@
 
 def intra_kernel(part, *refs):
     mine, theirs = refs[0:5], refs[5:10]
-    k, v, cum, masks = refs[10:14]
-    q, out, window, halo = refs[14:18]
-    pairs = paired(part, 0, D)
+    cum, masks = refs[10:12]
+    q, out, window, halo = refs[12:16]
+    pairs = paired(part, 0, 3 * D)
+    mask_t = masks[...].T
+    k, v = [], []
     size = 256
     cum_rows = cum[...]
     cum_t = cum_rows.T
     lower = lax.broadcasted_iota(jnp.int32, (size, size), 0) >= lax.broadcasted_iota(jnp.int32, (size, size), 1)
     for r in range(BLOCK // size):
         here = column(cum_t, r)
-        queries = encoded_dot(mine, theirs, pairs, r * size, size).astype(BF16)
+        acc = encoded_dot(mine, theirs, pairs, r * size, size)
+        queries = acc[:, 0:D].astype(BF16)
+        k.append(acc[:, D : 2 * D].astype(BF16))
+        v.append((acc[:, 2 * D :].astype(BF16).astype(F32) * column(mask_t, r)).astype(BF16))
         q[r * size : (r + 1) * size] = queries
         acc = jnp.zeros((size, D), F32)
         for s in range(r + 1):
@@ -198,9 +202,9 @@
             if s == r:
                 diff = jnp.where(lower, diff, -jnp.inf)
             scores = lax.dot_general(
-                queries, k[s * size : (s + 1) * size], (((1,), (1,)), ((), ())), preferred_element_type=F32
+                queries, k[s], (((1,), (1,)), ((), ())), preferred_element_type=F32
             )
-            acc += jnp.dot((scores * jnp.exp(diff)).astype(BF16), v[s * size : (s + 1) * size], preferred_element_type=F32)
+            acc += jnp.dot((scores * jnp.exp(diff)).astype(BF16), v[s], preferred_element_type=F32)
         out[r * size : (r + 1) * size] = acc
     _, _, y_at, core = place()
     ys = homes(y_at)
@@ -277,42 +281,31 @@
 
 
 def predict_kernel(ctx, w, context, predicted):
-    j = pl.program_id(0)
     whole = jnp.concatenate([ctx[h] for h in range(HEADS)], axis=1)
-
-    @pl.when(j == 0)
-    def _():
-        context[...] = whole
-
-    predicted[0] = jnp.dot(whole, w[0], preferred_element_type=F32).astype(BF16)
-
-
-def predict(ctx, w_pred):
-    return pl.pallas_call(
-        predict_kernel,
-        grid=(K,),
-        out_shape=[shape((LEN, CIN), BF16), shape((K, LEN, CIN), BF16)],
-        in_specs=[pl.BlockSpec((HEADS, LEN, D), lambda j: (0, 0, 0)), pl.BlockSpec((1, CIN, CIN), lambda j: (j, 0, 0))],
-        out_specs=[pl.BlockSpec((LEN, CIN), lambda j: (0, 0)), pl.BlockSpec((1, LEN, CIN), lambda j: (j, 0, 0))],
-        name="predict",
-        cost_estimate=pl.CostEstimate(flops=K * 2 * LEN * CIN * CIN, bytes_accessed=K * 2 * CIN * CIN, transcendentals=0),
-    )(ctx, w_pred)
-
-
-def loss_kernel(predicted, window, halo, masks, *refs):
+    context[...] = whole
+    for j in range(K):
+        predicted[j] = jnp.dot(whole, w[j], preferred_element_type=F32).astype(BF16)
+
+
+def loss_kernel(predicted, window, halo_far, masks, *refs):
     mine, theirs = refs[0:5], refs[5:10]
-    loss, bank, ahead = refs[10:13]
+    loss, ahead, halo, sem = refs[10:14]
+    arrival = pltpu.make_async_copy(halo_far, halo, sem)
+    arrival.start()
     _, _, y_at, core = place()
-    half = BLOCK // 2
-    for i, y in enumerate(homes(y_at)):
-        for who, group in ((core, mine), (1 - core, theirs)):
-            lanes = pl.ds(pl.multiple_of((2 * y + who) * D, D), D)
-            if i < 3:
-                bank[:, lanes] = group[i][...]
-            else:
-                bank[0:half, lanes] = group[3][...]
-                bank[half:, lanes] = group[4][...]
+    n = NSEQ * NCH
+    negsums = []
+    for j in range(K):
+        logits = jnp.zeros((n, LEN), F32)
+        for i, y in enumerate(homes(y_at)):
+            k, lo = (i, j * n) if i < 3 else (3, j * n) if j < K // 2 else (4, (j - K // 2) * n)
+            both = jnp.concatenate([mine[k][lo : lo + n], theirs[k][lo : lo + n]], axis=1)
+            lanes = [pl.ds(pl.multiple_of((2 * y + who) * D, D), D) for who in (core, 1 - core)]
+            part = jnp.concatenate([predicted[j, :, lanes[0]], predicted[j, :, lanes[1]]], axis=1)
+            logits += lax.dot_general(both, part, (((1,), (1,)), ((), ())), preferred_element_type=F32)
+        negsums.append(jnp.sum(jnp.exp(logits * SCORE_SCALE), axis=0, keepdims=True))
     me = 2 * y_at + core
+    arrival.wait()
     next_rows = halo[NCH * FAR : NCH * FAR + 16, :].astype(F32)
     ahead[0:LEN, :] = window[0:LEN, :]
     flags = [masks[pl.ds(me, 1), :]]
@@ -338,35 +331,29 @@
         m0 * jnp.concatenate([m1[:, ROW:], m2[:, :ROW]], axis=1),
         m0 * m2,
     ]
-    n = NSEQ * NCH
     for j in range(K):
         part = predicted[j]
-        logits = (
-            lax.dot_general(bank[j * n : (j + 1) * n, :], part, (((1,), (1,)), ((), ())), preferred_element_type=F32)
-            * SCORE_SCALE
-        )
-        negsum = jnp.sum(jnp.exp(logits), axis=0, keepdims=True)
         acc = jnp.zeros((LEN, D), F32)
         for c in range(NCH):
             target = ahead[(j + 1) * ROW : (j + 1) * ROW + LEN, c * D : (c + 1) * D]
             acc += part[:, c * D : (c + 1) * D].astype(F32) * target.astype(F32)
         positive = jnp.sum(acc.T, axis=0, keepdims=True) * SCORE_SCALE
-        loss[j : j + 1, :] = valid[j] * (jnp.log(jnp.exp(positive) + negsum) - positive)
+        loss[j : j + 1, :] = valid[j] * (jnp.log(jnp.exp(positive) + negsums[j]) - positive)
 
 
 def step(features, w_qkv, log_gate, norm_gain, w_pred, patch_mask, neg_index):
     mine, theirs = spread(features)
     (packed,) = call(
         pack_kernel, [shape((HEADS, PART + 16, 3 * D), BF16)],
-        [w_qkv, log_gate, patch_mask.reshape(1, -1), neg_index.T],
+        [w_qkv, log_gate, patch_mask.reshape(1, -1), neg_index.T], grant=False,
     )
     w_part = exchange(packed, "ch")
     pieces = [w_part, *mine, *theirs]
     whole = shape((BLOCK, D), BF16)
     n = K * NCH
-    keys, values, packet, cumul, masks = call(
+    packet, cumul, masks = call(
         project_kernel,
-        [whole, whole, shape((ZS, D + 16 + n, D), BF16), shape((NCH, LEN), F32), shape((NCH, LEN), F32)],
+        [shape((ZS, D + 16 + n, D), BF16), shape((NCH, LEN), F32), shape((NCH, LEN), F32)],
         pieces,
         flops=2 * BLOCK * CIN * 2 * D,
         scratch=[pltpu.VMEM((3, NCH, LEN), F32), pltpu.VMEM((n, D), F32)],
@@ -375,12 +362,12 @@
     queries, intra, window, halo = call(
         intra_kernel,
         [whole, shape((BLOCK, D), F32), shape((LEN + FAR, CIN), BF16), shape((NCH * FAR + 16, D), BF16)],
-        [*pieces, keys, values, cumul, masks],
+        [*pieces, cumul, masks],
         flops=2 * BLOCK * (BLOCK + CIN) * D,
     )
     x_packet, here, before = call(
         row_kernel, [shape((XS, D + 16 + ZS * n, D), BF16), shape((D, D), F32), shape((8, D), F32)], [z_in],
-        after=[intra],
+        after=[intra, queries],
     )
     x_packet, halo = lax.optimization_barrier((x_packet, halo))
     x_in = exchange(x_packet, "seq", ALONG_X)
@@ -393,11 +380,15 @@
     bank = x_in[:, D + 16 :].reshape(XS * ZS, K, NCH, D).transpose(1, 0, 2, 3).reshape(K * NSEQ * NCH, D)
     context = exchange(context, "ch")
     bank_mine, bank_theirs = spread(bank)
-    context, predicted = predict(context, w_pred)
+    context, predicted = call(
+        predict_kernel, [shape((LEN, CIN), BF16), shape((K, LEN, CIN), BF16)], [context, w_pred],
+        flops=K * 2 * LEN * CIN * CIN,
+    )
     (loss,) = call(
         loss_kernel, [shape((K, LEN), F32)], [predicted, window, halo, masks, *bank_mine, *bank_theirs],
+        away=(2,),
         flops=K * 2 * LEN * CIN * 256,
-        scratch=[pltpu.VMEM((K * NSEQ * NCH, CIN), BF16), pltpu.VMEM((LEN + FAR, CIN), BF16)],
+        scratch=[pltpu.VMEM((LEN + FAR, CIN), BF16), pltpu.VMEM(halo.shape, BF16), pltpu.SemaphoreType.DMA],
     )
     return context, loss
 

time: 114 us -> 104 us (0.912)
  Pallas kernels: 27.2 us -> 14.3 us
  local copies, waits for them, and re-layouts: 3.94 us -> 9.85 us
  waiting for transfers between devices: 38.7 us -> 35.2 us
    pallas_call x7, Pallas kernels: 27.2 us -> 14.3 us  [call(): pl.pallas_call(kernel, out_shape=out, in_specs=[pl.BlockSpec(memory_space...]
    unnamed x48 -> x26, local copies, waits for them, and re-layouts: 3.84 us -> 9.74 us
    all_to_all x4, waiting for transfers between devices: 15.3 us -> 11.8 us  [exchange(): lax.all_to_all(x, axis, split_axis=0, concat_axis=0, axis_index_groups=gr...]
  transfers between devices with their start and end apart: 23 -> 23, of which waited for: 7 -> 7; matrix products, arithmetic and copies ran while one was open for 0% -> 0% of each run, Pallas kernels for 13% -> 6%
where the time goes in v4:
time: 104 us; the launch traced here: 103 us
  starting transfers between devices  42.9 us (41%)
  waiting for transfers between devices  35.2 us (34%)
  Pallas kernels  14.3 us (14%)
  local copies, waits for them, and re-layouts  9.85 us (9%)
    all_to_all x4, starting transfers between devices, exchange(): lax.all_to_all(x, axis, split_axis=0, concat_axis=0, axis_index_groups=gr...  23.7 us
    ppermute x18, waiting for transfers between devices, hop(): return lax.ppermute(x, 'ch', pairs)  23.4 us
    ppermute x18, starting transfers between devices, hop(): return lax.ppermute(x, 'ch', pairs)  17.8 us
    pallas_call x7, Pallas kernels, call(): pl.pallas_call(kernel, out_shape=out, in_specs=[pl.BlockSpec(memory_space...  14.3 us
    all_to_all x4, waiting for transfers between devices, exchange(): lax.all_to_all(x, axis, split_axis=0, concat_axis=0, axis_index_groups=gr...  11.8 us
    unnamed x26, local copies, waits for them, and re-layouts  9.74 us
  transfers between devices with their start and end apart: 23, of which 7 were waited for; matrix products, arithmetic and copies ran while one was open for 0% of the time, Pallas kernels for 6%

profile of v4, /device:TPU:1, one launch (start us, length us, event | category | flops | bytes accessed | tf_op | source)
XLA Modules:
  0.0 103.3 jit_solution(16186084802142827358)
XLA Ops:
  0.6 2.2 %shard_map.86 = bf16[8,144,384]{2,1,0:T(8,128)(2,1)} custom-call(bf16[128,3072]{1,0:T(8,128)(2,1)} %refs_0_.1, f32[8,128]{1,0:T(8,128)} %refs_1_.4, s32[1,128]{1,0:T(1,128)} %bitcast.13, s32[1,4]{1,0:T(1,128)} %bitcast.14), custom_call_target="tpu_custom_call" | custom-call | bytes 1675792 | tf_op jit(solution)/shard_map/pallas_call | solution.py:36
  2.8 6.7 %all-to-all-start = ((bf16[8,144,384]{2,1,0:T(8,128)(2,1)}), bf16[8,144,384]{2,1,0:T(8,128)(2,1)S(1)}, u32[]{:S(2)}, u32[]{:S(2)}) async-start(bf16[8,144,384]{2,1,0:T(8,128)(2,1)} %shard_map.86), calls=%async_computation | async-start | bytes 1769472 | tf_op jit(solution)/shard_map/all_to_all | solution.py:57
  9.5 1.4 %collective-permute-start = (bf16[1024,128]{1,0:T(8,128)(2,1)}, bf16[1024,128]{1,0:T(8,128)(2,1)S(1)}, u32[]{:S(2)}, u32[]{:S(2)}) collective-permute-start(bf16[1024,128]{1,0:T(8,128)(2,1)} %refs_1_.6), channel_id=1, source_target_pairs={{0,2},{1,3},{2,4},{3,5},{4,6},{5,7},{6,0},{7,1},{8,10},{9,11},{10,... | collective-permute-start | bytes 786440 | tf_op jit(solution)/shard_map/ppermute | solution.py:65
  10.9 1.3 %collective-permute-start.1 = (bf16[1024,128]{1,0:T(8,128)(2,1)}, bf16[1024,128]{1,0:T(8,128)(2,1)S(1)}, u32[]{:S(2)}, u32[]{:S(2)}) collective-permute-start(bf16[1024,128]{1,0:T(8,128)(2,1)} %refs_1_.6), channel_id=1, source_target_pairs={{0,6},{1,7},{2,0},{3,1},{4,2},{5,3},{6,4},{7,5},{8,14},{9,15},{10,... | collective-permute-start | bytes 786440 | tf_op jit(solution)/shard_map/ppermute | solution.py:65
  12.2 0.7 collective-permute-start.4
  12.9 15.4 %collective-permute-done.refs_2_ = bf16[1024,128]{1,0:T(8,128)(2,1)S(1)} collective-permute-done((bf16[1024,128]{1,0:T(8,128)(2,1)}, bf16[1024,128]{1,0:T(8,128)(2,1)S(1)}, u32[]{:S(2)}, u32[]{:S(2)}) %collective-permute-start) | collective-permute-done | bytes 262176 | tf_op jit(solution)/shard_map/ppermute | solution.py:65
  28.3 0.1 collective-permute-start.2
  28.4 0.9 collective-permute-start.5
  29.3 0.1 collective-permute-start.6
  29.4 2.9 %collective-permute-start.3 = (bf16[512,128]{1,0:T(8,128)(2,1)S(1)}, bf16[512,128]{1,0:T(8,128)(2,1)S(1)}, u32[]{:S(2)}, u32[]{:S(2)}) collective-permute-start(bf16[512,128]{1,0:T(8,128)(2,1)S(1)} %slice.21), channel_id=1, source_target_pairs={{0,6},{1,7},{2,0},{3,1},{4,2},{5,3},{6,4},{7,5},{8,14},{9,15},{10,... | collective-permute-start | bytes 393224 | tf_op jit(solution)/shard_map/ppermute | solution.py:65
  32.3 1.6 %collective-permute-done.2.refs_4_ = bf16[512,128]{1,0:T(8,128)(2,1)S(1)} collective-permute-done((bf16[512,128]{1,0:T(8,128)(2,1)S(1)}, bf16[512,128]{1,0:T(8,128)(2,1)S(1)}, u32[]{:S(2)}, u32[]{:S(2)}) %collective-permute-start.2) | collective-permute-done | bytes 131104 | tf_op jit(solution)/shard_map/ppermute | solution.py:65
  33.9 1.6 %collective-permute-start.7 = (bf16[512,128]{1,0:T(8,128)(2,1)S(1)}, bf16[512,128]{1,0:T(8,128)(2,1)S(1)}, u32[]{:S(2)}, u32[]{:S(2)}) collective-permute-start(bf16[512,128]{1,0:T(8,128)(2,1)S(1)} %collective-permute-done.2.refs_4_), channel_id=1, source_target_pairs={{0,1},{1,0},{2,3},{3,2},{4,5},{5,4},{6,7},{7,6},{8,9},{9,8},{10,11... | collective-permute-start | bytes 393224 | tf_op jit(solution)/shard_map/ppermute | solution.py:65
  35.5 0.0 collective-permute-done.3.refs_5_
  35.5 0.5 collective-permute-start.8
  36.0 0.5 collective-permute-done.7.refs_9_
  36.5 0.5 collective-permute-done.8.refs_10_
  37.0 1.0 copy-done.1
  38.0 2.8 %shard_map.87 = (bf16[8,176,128]{2,1,0:T(8,128)(2,1)}, f32[8,128]{1,0:T(8,128)S(1)}, f32[8,128]{1,0:T(8,128)S(1)}) custom-call(bf16[8,144,384]{2,1,0:T(8,128)(2,1)S(1)} %all-to-all-done.refs_0_, bf16[1024,128]{1,0:T(8,128)(2,1)S(1)} %copy-done.1, bf16[1024,128]{1,0:T(8,128)(2,1)S(1)} %collective-permute-done.refs_2_, ...), custom_call_target="tpu_custom_call" | custom-call | flops 536870912 | bytes 3350528 | tf_op jit(solution)/shard_map/pallas_call | solution.py:36
  40.8 7.5 %all-to-all-start.1 = ((bf16[8,176,128]{2,1,0:T(8,128)(2,1)}), bf16[8,176,128]{2,1,0:T(8,128)(2,1)S(1)}, u32[]{:S(2)}, u32[]{:S(2)}) async-start(bf16[8,176,128]{2,1,0:T(8,128)(2,1)} %get-tuple-element.16), calls=%async_computation.1 | async-start | bytes 720896 | tf_op jit(solution)/shard_map/all_to_all | solution.py:57
  48.3 0.0 copy-start.2
  48.3 0.9 copy-done.2
  49.3 0.9 copy-done.6
  50.2 0.9 copy-done.8
  51.1 0.9 copy-done.10
  52.0 3.1 %shard_map.88 = (bf16[1024,128]{1,0:T(8,128)(2,1)S(1)}, f32[1024,128]{1,0:T(8,128)S(1)}, bf16[384,1024]{1,0:T(8,128)(2,1)S(1)}, bf16[2064,128]{1,0:T(8,128)(2,1)S(1)}) custom-call(bf16[8,144,384]{2,1,0:T(8,128)(2,1)S(1)} %all-to-all-done.refs_0_, bf16[1024,128]{1,0:T(8,128)(2,1)S(1)} %copy-done.2, bf16[1024,128]{1,0:T(8,128)(2,1)S(1)} %collective-permute-done.refs_2_, ...), custom_call_target="tpu_custom_call" | custom-call | flops 536870912 | bytes 5091328 | tf_op jit(solution)/shard_map/pallas_call | solution.py:36
  55.1 0.9 copy-done.3
  56.0 0.8 copy-done.12
  56.8 6.0 %all-to-all-done.1.refs_0_ = bf16[8,176,128]{2,1,0:T(8,128)(2,1)S(1)} async-done(((bf16[8,176,128]{2,1,0:T(8,128)(2,1)}), bf16[8,176,128]{2,1,0:T(8,128)(2,1)S(1)}, u32[]{:S(2)}, u32[]{:S(2)}) %all-to-all-start.1) | async-done | bytes 360480 | tf_op jit(solution)/shard_map/all_to_all | solution.py:57
  62.7 0.9 shard_map.89
  63.6 4.0 %all-to-all-start.2 = ((bf16[4,400,128]{2,1,0:T(8,128)(2,1)}), bf16[4,400,128]{2,1,0:T(8,128)(2,1)S(1)}, u32[]{:S(2)}, u32[]{:S(2)}) async-start(bf16[4,400,128]{2,1,0:T(8,128)(2,1)} %get-tuple-element.23), calls=%async_computation.2 | async-start | bytes 819200 | tf_op jit(solution)/shard_map/all_to_all | solution.py:57
  67.6 1.4 %collective-permute-start.9 = (bf16[2064,128]{1,0:T(8,128)(2,1)}, bf16[2064,128]{1,0:T(8,128)(2,1)}, u32[]{:S(2)}, u32[]{:S(2)}) collective-permute-start(bf16[2064,128]{1,0:T(8,128)(2,1)} %copy-done.12), channel_id=1, source_target_pairs={{14,6},{15,7},{22,14},{23,15},{30,22},{31,23},{38,30},{39,31},{46,... | collective-permute-start | bytes 1585160 | tf_op jit(solution)/shard_map/ppermute | solution.py:375
  69.0 5.8 %all-to-all-done.2.refs_0_ = bf16[4,400,128]{2,1,0:T(8,128)(2,1)S(1)} async-done(((bf16[4,400,128]{2,1,0:T(8,128)(2,1)}), bf16[4,400,128]{2,1,0:T(8,128)(2,1)S(1)}, u32[]{:S(2)}, u32[]{:S(2)}) %all-to-all-start.2) | async-done | bytes 409632 | tf_op jit(solution)/shard_map/all_to_all | solution.py:57
  74.9 0.1 collective-permute-start.10
  75.0 3.7 %collective-permute-start.11 = (bf16[1024,128]{1,0:T(8,128)(2,1)S(1)}, bf16[1024,128]{1,0:T(8,128)(2,1)S(1)}, u32[]{:S(2)}, u32[]{:S(2)}) collective-permute-start(bf16[1024,128]{1,0:T(8,128)(2,1)S(1)} %bitcast.8), channel_id=1, source_target_pairs={{0,6},{1,7},{2,0},{3,1},{4,2},{5,3},{6,4},{7,5},{8,14},{9,15},{10,... | collective-permute-start | bytes 786440 | tf_op jit(solution)/shard_map/ppermute | solution.py:65
  78.7 1.5 %shard_map.90 = bf16[8,128,128]{2,1,0:T(8,128)(2,1)} custom-call(bf16[4,400,128]{2,1,0:T(8,128)(2,1)S(1)} %all-to-all-done.2.refs_0_, f32[128,128]{1,0:T(8,128)S(1)} %get-tuple-element.24.refs_1_, f32[8,128]{1,0:T(8,128)S(1)} %get-tuple-element.25.refs_2_, bf16[1024,128]{1,0:T(8,128)(2,1)S(1)} %get-tuple-element.20.refs_2_.refs_3_, ...), custom_call_target="tpu_custom_call" | custom-call | flops 33554432 | bytes 1536000 | tf_op jit(solution)/shard_map/pallas_call | solution.py:36
  80.2 5.5 %all-to-all-start.3 = ((bf16[8,128,128]{2,1,0:T(8,128)(2,1)}), bf16[8,128,128]{2,1,0:T(8,128)(2,1)S(1)}, u32[]{:S(2)}, u32[]{:S(2)}) async-start(bf16[8,128,128]{2,1,0:T(8,128)(2,1)} %shard_map.90), calls=%async_computation.3 | async-start | bytes 524288 | tf_op jit(solution)/shard_map/all_to_all | solution.py:57
  85.7 0.2 collective-permute-start.14
  85.9 1.6 %collective-permute-start.12 = (bf16[512,128]{1,0:T(8,128)(2,1)S(1)}, bf16[512,128]{1,0:T(8,128)(2,1)S(1)}, u32[]{:S(2)}, u32[]{:S(2)}) collective-permute-start(bf16[512,128]{1,0:T(8,128)(2,1)S(1)} %slice.23), channel_id=1, source_target_pairs={{0,2},{1,3},{2,4},{3,5},{4,6},{5,7},{6,0},{7,1},{8,10},{9,11},{10,... | collective-permute-start | bytes 393224 | tf_op jit(solution)/shard_map/ppermute | solution.py:65
  87.5 0.4 collective-permute-start.15
  88.0 0.2 collective-permute-start.16
  88.2 1.3 %collective-permute-start.13 = (bf16[512,128]{1,0:T(8,128)(2,1)S(1)}, bf16[512,128]{1,0:T(8,128)(2,1)S(1)}, u32[]{:S(2)}, u32[]{:S(2)}) collective-permute-start(bf16[512,128]{1,0:T(8,128)(2,1)S(1)} %slice.24), channel_id=1, source_target_pairs={{0,6},{1,7},{2,0},{3,1},{4,2},{5,3},{6,4},{7,5},{8,14},{9,15},{10,... | collective-permute-start | bytes 393224 | tf_op jit(solution)/shard_map/ppermute | solution.py:65
  89.5 5.5 %collective-permute-done.12.refs_7_ = bf16[512,128]{1,0:T(8,128)(2,1)S(1)} collective-permute-done((bf16[512,128]{1,0:T(8,128)(2,1)S(1)}, bf16[512,128]{1,0:T(8,128)(2,1)S(1)}, u32[]{:S(2)}, u32[]{:S(2)}) %collective-permute-start.12) | collective-permute-done | bytes 131104 | tf_op jit(solution)/shard_map/ppermute | solution.py:65
  95.0 0.8 collective-permute-start.17
  95.8 0.0 collective-permute-start.18
  95.8 0.0 copy-start
  95.8 3.4 %copy-done = bf16[4,1024,1024]{2,1,0:T(8,128)(2,1)S(1)} copy-done((bf16[4,1024,1024]{2,1,0:T(8,128)(2,1)S(1)}, bf16[4,1024,1024]{2,1,0:T(8,128)(2,1)}, u32[]{:S(2)}) %copy-start) | copy-done | bytes 8388632
  99.2 1.3 %shard_map.91 = (bf16[128,1024]{1,0:T(8,128)(2,1)}, bf16[4,128,1024]{2,1,0:T(8,128)(2,1)S(1)}) custom-call(bf16[8,128,128]{2,1,0:T(8,128)(2,1)S(1)} %all-to-all-done.3.refs_0_, bf16[4,1024,1024]{2,1,0:T(8,128)(2,1)S(1)} %copy-done), custom_call_target="tpu_custom_call" | custom-call | flops 1073741824 | bytes 9961472 | tf_op jit(solution)/shard_map/pallas_call | solution.py:36
  100.5 2.6 %shard_map.92 = f32[4,128]{1,0:T(4,128)} custom-call(bf16[4,128,1024]{2,1,0:T(8,128)(2,1)S(1)} %get-tuple-element.27.refs_0_, bf16[384,1024]{1,0:T(8,128)(2,1)S(1)} %copy-done.4, bf16[2064,128]{1,0:T(8,128)(2,1)} %collective-permute-done.9.refs_2_, f32[8,128]{1,0:T(8,128)S(1)} %get-tuple-element.18.refs_12_.refs_3_, bf16[1024,128]{1,0:T(8,128)(2,1)S(1)} %bitcast.10, ...), custom_call_target="tpu_custom_call" | custom-call | flops 268435456 | bytes 4466688 | tf_op jit(solution)/shard_map/pallas_call | solution.py:36
  (37 shorter events, 0.2 us)
Async XLA Ops:
  0.6 78.0 %copy-start.11 = (f32[1024]{0:T(1024)S(1)}, f32[1024]{0:T(1024)}, u32[]{:S(2)}) copy-start(f32[1024]{0:T(1024)} %param.10) | copy-start | bytes 12292
  2.8 34.1 %all-to-all-start = ((bf16[8,144,384]{2,1,0:T(8,128)(2,1)}), bf16[8,144,384]{2,1,0:T(8,128)(2,1)S(1)}, u32[]{:S(2)}, u32[]{:S(2)}) async-start(bf16[8,144,384]{2,1,0:T(8,128)(2,1)} %shard_map.86), calls=%async_computation | async-start | bytes 1769472 | tf_op jit(solution)/shard_map/all_to_all | solution.py:57
  9.5 18.8 %collective-permute-start = (bf16[1024,128]{1,0:T(8,128)(2,1)}, bf16[1024,128]{1,0:T(8,128)(2,1)S(1)}, u32[]{:S(2)}, u32[]{:S(2)}) collective-permute-start(bf16[1024,128]{1,0:T(8,128)(2,1)} %refs_1_.6), channel_id=1, source_target_pairs={{0,2},{1,3},{2,4},{3,5},{4,6},{5,7},{6,0},{7,1},{8,10},{9,11},{10,... | collective-permute-start | bytes 786440 | tf_op jit(solution)/shard_map/ppermute | solution.py:65
  10.9 18.4 %collective-permute-start.1 = (bf16[1024,128]{1,0:T(8,128)(2,1)}, bf16[1024,128]{1,0:T(8,128)(2,1)S(1)}, u32[]{:S(2)}, u32[]{:S(2)}) collective-permute-start(bf16[1024,128]{1,0:T(8,128)(2,1)} %refs_1_.6), channel_id=1, source_target_pairs={{0,6},{1,7},{2,0},{3,1},{4,2},{5,3},{6,4},{7,5},{8,14},{9,15},{10,... | collective-permute-start | bytes 786440 | tf_op jit(solution)/shard_map/ppermute | solution.py:65
  12.2 23.8 %collective-permute-start.4 = (bf16[1024,128]{1,0:T(8,128)(2,1)}, bf16[1024,128]{1,0:T(8,128)(2,1)S(1)}, u32[]{:S(2)}, u32[]{:S(2)}) collective-permute-start(bf16[1024,128]{1,0:T(8,128)(2,1)} %refs_1_.6), channel_id=1, source_target_pairs={{0,1},{1,0},{2,3},{3,2},{4,5},{5,4},{6,7},{7,6},{8,9},{9,8},{10,11... | collective-permute-start | bytes 786440 | tf_op jit(solution)/shard_map/ppermute | solution.py:65
  28.3 5.6 %collective-permute-start.2 = (bf16[512,128]{1,0:T(8,128)(2,1)S(1)}, bf16[512,128]{1,0:T(8,128)(2,1)S(1)}, u32[]{:S(2)}, u32[]{:S(2)}) collective-permute-start(bf16[512,128]{1,0:T(8,128)(2,1)S(1)} %slice.20), channel_id=1, source_target_pairs={{0,2},{1,3},{2,4},{3,5},{4,6},{5,7},{6,0},{7,1},{8,10},{9,11},{10,... | collective-permute-start | bytes 393224 | tf_op jit(solution)/shard_map/ppermute | solution.py:65
  28.4 7.6 %collective-permute-start.5 = (bf16[1024,128]{1,0:T(8,128)(2,1)S(1)}, bf16[1024,128]{1,0:T(8,128)(2,1)S(1)}, u32[]{:S(2)}, u32[]{:S(2)}) collective-permute-start(bf16[1024,128]{1,0:T(8,128)(2,1)S(1)} %collective-permute-done.refs_2_), channel_id=1, source_target_pairs={{0,1},{1,0},{2,3},{3,2},{4,5},{5,4},{6,7},{7,6},{8,9},{9,8},{10,11... | collective-permute-start | bytes 786440 | tf_op jit(solution)/shard_map/ppermute | solution.py:65
  29.3 6.8 %collective-permute-start.6 = (bf16[1024,128]{1,0:T(8,128)(2,1)S(1)}, bf16[1024,128]{1,0:T(8,128)(2,1)S(1)}, u32[]{:S(2)}, u32[]{:S(2)}) collective-permute-start(bf16[1024,128]{1,0:T(8,128)(2,1)S(1)} %collective-permute-done.1.refs_3_), channel_id=1, source_target_pairs={{0,1},{1,0},{2,3},{3,2},{4,5},{5,4},{6,7},{7,6},{8,9},{9,8},{10,11... | collective-permute-start | bytes 786440 | tf_op jit(solution)/shard_map/ppermute | solution.py:65
  29.4 6.1 %collective-permute-start.3 = (bf16[512,128]{1,0:T(8,128)(2,1)S(1)}, bf16[512,128]{1,0:T(8,128)(2,1)S(1)}, u32[]{:S(2)}, u32[]{:S(2)}) collective-permute-start(bf16[512,128]{1,0:T(8,128)(2,1)S(1)} %slice.21), channel_id=1, source_target_pairs={{0,6},{1,7},{2,0},{3,1},{4,2},{5,3},{6,4},{7,5},{8,14},{9,15},{10,... | collective-permute-start | bytes 393224 | tf_op jit(solution)/shard_map/ppermute | solution.py:65
  33.9 2.6 %collective-permute-start.7 = (bf16[512,128]{1,0:T(8,128)(2,1)S(1)}, bf16[512,128]{1,0:T(8,128)(2,1)S(1)}, u32[]{:S(2)}, u32[]{:S(2)}) collective-permute-start(bf16[512,128]{1,0:T(8,128)(2,1)S(1)} %collective-permute-done.2.refs_4_), channel_id=1, source_target_pairs={{0,1},{1,0},{2,3},{3,2},{4,5},{5,4},{6,7},{7,6},{8,9},{9,8},{10,11... | collective-permute-start | bytes 393224 | tf_op jit(solution)/shard_map/ppermute | solution.py:65
  35.5 12.8 %copy-start.5 = (bf16[512,128]{1,0:T(8,128)(2,1)}, bf16[512,128]{1,0:T(8,128)(2,1)S(1)}, u32[]{:S(2)}) copy-start(bf16[512,128]{1,0:T(8,128)(2,1)S(1)} %collective-permute-done.3.refs_5_) | copy-start | bytes 393220
  35.5 1.5 %collective-permute-start.8 = (bf16[512,128]{1,0:T(8,128)(2,1)S(1)}, bf16[512,128]{1,0:T(8,128)(2,1)S(1)}, u32[]{:S(2)}, u32[]{:S(2)}) collective-permute-start(bf16[512,128]{1,0:T(8,128)(2,1)S(1)} %collective-permute-done.3.refs_5_), channel_id=1, source_target_pairs={{0,1},{1,0},{2,3},{3,2},{4,5},{5,4},{6,7},{7,6},{8,9},{9,8},{10,11... | collective-permute-start | bytes 393224 | tf_op jit(solution)/shard_map/ppermute | solution.py:65
  36.5 11.8 %copy-start.7 = (bf16[512,128]{1,0:T(8,128)(2,1)}, bf16[512,128]{1,0:T(8,128)(2,1)S(1)}, u32[]{:S(2)}) copy-start(bf16[512,128]{1,0:T(8,128)(2,1)S(1)} %collective-permute-done.7.refs_9_) | copy-start | bytes 393220
  37.0 11.3 %copy-start.9 = (bf16[512,128]{1,0:T(8,128)(2,1)}, bf16[512,128]{1,0:T(8,128)(2,1)S(1)}, u32[]{:S(2)}) copy-start(bf16[512,128]{1,0:T(8,128)(2,1)S(1)} %collective-permute-done.8.refs_10_) | copy-start | bytes 393220
  37.0 1.0 copy-start.1
  40.8 21.9 %all-to-all-start.1 = ((bf16[8,176,128]{2,1,0:T(8,128)(2,1)}), bf16[8,176,128]{2,1,0:T(8,128)(2,1)S(1)}, u32[]{:S(2)}, u32[]{:S(2)}) async-start(bf16[8,176,128]{2,1,0:T(8,128)(2,1)} %get-tuple-element.16), calls=%async_computation.1 | async-start | bytes 720896 | tf_op jit(solution)/shard_map/all_to_all | solution.py:57
  48.3 1.0 copy-start.2
  49.3 0.9 copy-start.6
  50.2 0.9 copy-start.8
  51.1 0.9 copy-start.10
  55.1 0.9 copy-start.3
  56.0 0.8 copy-start.12
  62.7 37.8 %copy-start.4 = (bf16[384,1024]{1,0:T(8,128)(2,1)S(1)}, bf16[384,1024]{1,0:T(8,128)(2,1)}, u32[]{:S(2)}) copy-start(bf16[384,1024]{1,0:T(8,128)(2,1)} %copy-done.3) | copy-start | bytes 2359300
  63.6 11.3 %all-to-all-start.2 = ((bf16[4,400,128]{2,1,0:T(8,128)(2,1)}), bf16[4,400,128]{2,1,0:T(8,128)(2,1)S(1)}, u32[]{:S(2)}, u32[]{:S(2)}) async-start(bf16[4,400,128]{2,1,0:T(8,128)(2,1)} %get-tuple-element.23), calls=%async_computation.2 | async-start | bytes 819200 | tf_op jit(solution)/shard_map/all_to_all | solution.py:57
  67.6 20.6 %collective-permute-start.9 = (bf16[2064,128]{1,0:T(8,128)(2,1)}, bf16[2064,128]{1,0:T(8,128)(2,1)}, u32[]{:S(2)}, u32[]{:S(2)}) collective-permute-start(bf16[2064,128]{1,0:T(8,128)(2,1)} %copy-done.12), channel_id=1, source_target_pairs={{14,6},{15,7},{22,14},{23,15},{30,22},{31,23},{38,30},{39,31},{46,... | collective-permute-start | bytes 1585160 | tf_op jit(solution)/shard_map/ppermute | solution.py:375
  74.9 11.0 %collective-permute-start.10 = (bf16[1024,128]{1,0:T(8,128)(2,1)S(1)}, bf16[1024,128]{1,0:T(8,128)(2,1)S(1)}, u32[]{:S(2)}, u32[]{:S(2)}) collective-permute-start(bf16[1024,128]{1,0:T(8,128)(2,1)S(1)} %bitcast.7), channel_id=1, source_target_pairs={{0,2},{1,3},{2,4},{3,5},{4,6},{5,7},{6,0},{7,1},{8,10},{9,11},{10,... | collective-permute-start | bytes 786440 | tf_op jit(solution)/shard_map/ppermute | solution.py:65
  75.0 13.0 %collective-permute-start.11 = (bf16[1024,128]{1,0:T(8,128)(2,1)S(1)}, bf16[1024,128]{1,0:T(8,128)(2,1)S(1)}, u32[]{:S(2)}, u32[]{:S(2)}) collective-permute-start(bf16[1024,128]{1,0:T(8,128)(2,1)S(1)} %bitcast.8), channel_id=1, source_target_pairs={{0,6},{1,7},{2,0},{3,1},{4,2},{5,3},{6,4},{7,5},{8,14},{9,15},{10,... | collective-permute-start | bytes 786440 | tf_op jit(solution)/shard_map/ppermute | solution.py:65
  80.2 15.6 %all-to-all-start.3 = ((bf16[8,128,128]{2,1,0:T(8,128)(2,1)}), bf16[8,128,128]{2,1,0:T(8,128)(2,1)S(1)}, u32[]{:S(2)}, u32[]{:S(2)}) async-start(bf16[8,128,128]{2,1,0:T(8,128)(2,1)} %shard_map.90), calls=%async_computation.3 | async-start | bytes 524288 | tf_op jit(solution)/shard_map/all_to_all | solution.py:57
  85.7 14.7 %collective-permute-start.14 = (bf16[1024,128]{1,0:T(8,128)(2,1)S(1)}, bf16[1024,128]{1,0:T(8,128)(2,1)S(1)}, u32[]{:S(2)}, u32[]{:S(2)}) collective-permute-start(bf16[1024,128]{1,0:T(8,128)(2,1)S(1)} %bitcast.9), channel_id=1, source_target_pairs={{0,1},{1,0},{2,3},{3,2},{4,5},{5,4},{6,7},{7,6},{8,9},{9,8},{10,11... | collective-permute-start | bytes 786440 | tf_op jit(solution)/shard_map/ppermute | solution.py:65
  85.9 9.1 %collective-permute-start.12 = (bf16[512,128]{1,0:T(8,128)(2,1)S(1)}, bf16[512,128]{1,0:T(8,128)(2,1)S(1)}, u32[]{:S(2)}, u32[]{:S(2)}) collective-permute-start(bf16[512,128]{1,0:T(8,128)(2,1)S(1)} %slice.23), channel_id=1, source_target_pairs={{0,2},{1,3},{2,4},{3,5},{4,6},{5,7},{6,0},{7,1},{8,10},{9,11},{10,... | collective-permute-start | bytes 393224 | tf_op jit(solution)/shard_map/ppermute | solution.py:65
  87.5 12.9 %collective-permute-start.15 = (bf16[1024,128]{1,0:T(8,128)(2,1)S(1)}, bf16[1024,128]{1,0:T(8,128)(2,1)S(1)}, u32[]{:S(2)}, u32[]{:S(2)}) collective-permute-start(bf16[1024,128]{1,0:T(8,128)(2,1)S(1)} %collective-permute-done.10.refs_5_), channel_id=1, source_target_pairs={{0,1},{1,0},{2,3},{3,2},{4,5},{5,4},{6,7},{7,6},{8,9},{9,8},{10,11... | collective-permute-start | bytes 786440 | tf_op jit(solution)/shard_map/ppermute | solution.py:65
  88.0 12.5 %collective-permute-start.16 = (bf16[1024,128]{1,0:T(8,128)(2,1)S(1)}, bf16[1024,128]{1,0:T(8,128)(2,1)S(1)}, u32[]{:S(2)}, u32[]{:S(2)}) collective-permute-start(bf16[1024,128]{1,0:T(8,128)(2,1)S(1)} %collective-permute-done.11.refs_6_), channel_id=1, source_target_pairs={{0,1},{1,0},{2,3},{3,2},{4,5},{5,4},{6,7},{7,6},{8,9},{9,8},{10,11... | collective-permute-start | bytes 786440 | tf_op jit(solution)/shard_map/ppermute | solution.py:65
  88.2 7.6 %collective-permute-start.13 = (bf16[512,128]{1,0:T(8,128)(2,1)S(1)}, bf16[512,128]{1,0:T(8,128)(2,1)S(1)}, u32[]{:S(2)}, u32[]{:S(2)}) collective-permute-start(bf16[512,128]{1,0:T(8,128)(2,1)S(1)} %slice.24), channel_id=1, source_target_pairs={{0,6},{1,7},{2,0},{3,1},{4,2},{5,3},{6,4},{7,5},{8,14},{9,15},{10,... | collective-permute-start | bytes 393224 | tf_op jit(solution)/shard_map/ppermute | solution.py:65
  95.0 5.5 %collective-permute-start.17 = (bf16[512,128]{1,0:T(8,128)(2,1)S(1)}, bf16[512,128]{1,0:T(8,128)(2,1)S(1)}, u32[]{:S(2)}, u32[]{:S(2)}) collective-permute-start(bf16[512,128]{1,0:T(8,128)(2,1)S(1)} %collective-permute-done.12.refs_7_), channel_id=1, source_target_pairs={{0,1},{1,0},{2,3},{3,2},{4,5},{5,4},{6,7},{7,6},{8,9},{9,8},{10,11... | collective-permute-start | bytes 393224 | tf_op jit(solution)/shard_map/ppermute | solution.py:65
  95.8 4.7 %collective-permute-start.18 = (bf16[512,128]{1,0:T(8,128)(2,1)S(1)}, bf16[512,128]{1,0:T(8,128)(2,1)S(1)}, u32[]{:S(2)}, u32[]{:S(2)}) collective-permute-start(bf16[512,128]{1,0:T(8,128)(2,1)S(1)} %collective-permute-done.13.refs_8_), channel_id=1, source_target_pairs={{0,1},{1,0},{2,3},{3,2},{4,5},{5,4},{6,7},{7,6},{8,9},{9,8},{10,11... | collective-permute-start | bytes 393224 | tf_op jit(solution)/shard_map/ppermute | solution.py:65
  95.8 3.4 %copy-start = (bf16[4,1024,1024]{2,1,0:T(8,128)(2,1)S(1)}, bf16[4,1024,1024]{2,1,0:T(8,128)(2,1)}, u32[]{:S(2)}) copy-start(bf16[4,1024,1024]{2,1,0:T(8,128)(2,1)} %refs_1_.7) | copy-start | bytes 25165828

commit v5 on v4

--- a/solution.py
+++ b/solution.py
@@ -65,11 +65,10 @@
     return lax.ppermute(x, "ch", pairs)
 
 
-def spread(x):
-    half = x.shape[0] // 2
+def spread(x, cut):
     up, dn = hop(x, 1), hop(x, -1)
     other = hop(x, 0, True)
-    far_a, far_b = hop(up[:half], 1), hop(dn[half:], -1)
+    far_a, far_b = hop(up[:cut], 1), hop(dn[cut:], -1)
     return [x, up, dn, far_a, far_b], [other] + [hop(a, 0, True) for a in (up, dn, far_a, far_b)]
 
 
@@ -298,7 +297,7 @@
     for j in range(K):
         logits = jnp.zeros((n, LEN), F32)
         for i, y in enumerate(homes(y_at)):
-            k, lo = (i, j * n) if i < 3 else (3, j * n) if j < K // 2 else (4, (j - K // 2) * n)
+            k, lo = (i, j * n) if i < 3 else (3, 0) if j == 0 else (4, (j - 1) * n)
             both = jnp.concatenate([mine[k][lo : lo + n], theirs[k][lo : lo + n]], axis=1)
             lanes = [pl.ds(pl.multiple_of((2 * y + who) * D, D), D) for who in (core, 1 - core)]
             part = jnp.concatenate([predicted[j, :, lanes[0]], predicted[j, :, lanes[1]]], axis=1)
@@ -342,7 +341,7 @@
 
 
 def step(features, w_qkv, log_gate, norm_gain, w_pred, patch_mask, neg_index):
-    mine, theirs = spread(features)
+    mine, theirs = spread(features, BLOCK // 2)
     (packed,) = call(
         pack_kernel, [shape((HEADS, PART + 16, 3 * D), BF16)],
         [w_qkv, log_gate, patch_mask.reshape(1, -1), neg_index.T], grant=False,
@@ -379,7 +378,7 @@
     )
     bank = x_in[:, D + 16 :].reshape(XS * ZS, K, NCH, D).transpose(1, 0, 2, 3).reshape(K * NSEQ * NCH, D)
     context = exchange(context, "ch")
-    bank_mine, bank_theirs = spread(bank)
+    bank_mine, bank_theirs = spread(bank, NSEQ * NCH)
     context, predicted = call(
         predict_kernel, [shape((LEN, CIN), BF16), shape((K, LEN, CIN), BF16)], [context, w_pred],
         flops=K * 2 * LEN * CIN * CIN,

time: 104 us -> 111 us (1.067)
  waiting for transfers between devices: 35.2 us -> 38.8 us
  starting transfers between devices: 42.9 us -> 44.9 us
  local copies, waits for them, and re-layouts: 9.85 us -> 11.5 us
    ppermute x18, waiting for transfers between devices: 23.4 us -> 26.3 us  [hop(): return lax.ppermute(x, 'ch', pairs)]
    ppermute x18, starting transfers between devices: 17.8 us -> 19.7 us  [hop(): return lax.ppermute(x, 'ch', pairs)]
    unnamed x26 -> x30, local copies, waits for them, and re-layouts: 9.74 us -> 10.6 us
  transfers between devices with their start and end apart: 23 -> 23, of which waited for: 7 -> 8; matrix products, arithmetic and copies ran while one was open for 0% -> 1% of each run, Pallas kernels for 6% -> 5%
where the time goes in v5:
time: 111 us
  starting transfers between devices  44.9 us (40%)
  waiting for transfers between devices  38.8 us (35%)
  Pallas kernels  14.5 us (13%)
  local copies, waits for them, and re-layouts  11.5 us (10%)
    ppermute x18, waiting for transfers between devices, hop(): return lax.ppermute(x, 'ch', pairs)  26.3 us
    all_to_all x4, starting transfers between devices, exchange(): lax.all_to_all(x, axis, split_axis=0, concat_axis=0, axis_index_groups=gr...  24.5 us
    ppermute x18, starting transfers between devices, hop(): return lax.ppermute(x, 'ch', pairs)  19.7 us
    pallas_call x7, Pallas kernels, call(): pl.pallas_call(kernel, out_shape=out, in_specs=[pl.BlockSpec(memory_space...  14.5 us
    all_to_all x4, waiting for transfers between devices, exchange(): lax.all_to_all(x, axis, split_axis=0, concat_axis=0, axis_index_groups=gr...  12.5 us
    unnamed x30, local copies, waits for them, and re-layouts  10.6 us
  transfers between devices with their start and end apart: 23, of which 8 were waited for; matrix products, arithmetic and copies ran while one was open for 1% of the time, Pallas kernels for 5%

profile of v5, /device:TPU:1, one launch (start us, length us, event | category | flops | bytes accessed | tf_op | source)
XLA Modules:
  0.0 110.7 jit_solution(6177433610764471113)
XLA Ops:
  0.6 2.2 %shard_map.86 = bf16[8,144,384]{2,1,0:T(8,128)(2,1)} custom-call(bf16[128,3072]{1,0:T(8,128)(2,1)} %refs_0_.1, f32[8,128]{1,0:T(8,128)} %refs_1_.4, s32[1,128]{1,0:T(1,128)} %bitcast.13, s32[1,4]{1,0:T(1,128)} %bitcast.14), custom_call_target="tpu_custom_call" | custom-call | bytes 1675792 | tf_op jit(solution)/shard_map/pallas_call | solution.py:36
  2.8 6.7 %all-to-all-start = ((bf16[8,144,384]{2,1,0:T(8,128)(2,1)}), bf16[8,144,384]{2,1,0:T(8,128)(2,1)S(1)}, u32[]{:S(2)}, u32[]{:S(2)}) async-start(bf16[8,144,384]{2,1,0:T(8,128)(2,1)} %shard_map.86), calls=%async_computation | async-start | bytes 1769472 | tf_op jit(solution)/shard_map/all_to_all | solution.py:57
  9.5 1.4 %collective-permute-start = (bf16[1024,128]{1,0:T(8,128)(2,1)}, bf16[1024,128]{1,0:T(8,128)(2,1)S(1)}, u32[]{:S(2)}, u32[]{:S(2)}) collective-permute-start(bf16[1024,128]{1,0:T(8,128)(2,1)} %refs_1_.6), channel_id=1, source_target_pairs={{0,2},{1,3},{2,4},{3,5},{4,6},{5,7},{6,0},{7,1},{8,10},{9,11},{10,... | collective-permute-start | bytes 786440 | tf_op jit(solution)/shard_map/ppermute | solution.py:65
  10.9 1.3 %collective-permute-start.1 = (bf16[1024,128]{1,0:T(8,128)(2,1)}, bf16[1024,128]{1,0:T(8,128)(2,1)S(1)}, u32[]{:S(2)}, u32[]{:S(2)}) collective-permute-start(bf16[1024,128]{1,0:T(8,128)(2,1)} %refs_1_.6), channel_id=1, source_target_pairs={{0,6},{1,7},{2,0},{3,1},{4,2},{5,3},{6,4},{7,5},{8,14},{9,15},{10,... | collective-permute-start | bytes 786440 | tf_op jit(solution)/shard_map/ppermute | solution.py:65
  12.2 0.7 collective-permute-start.4
  12.9 15.4 %collective-permute-done.refs_2_ = bf16[1024,128]{1,0:T(8,128)(2,1)S(1)} collective-permute-done((bf16[1024,128]{1,0:T(8,128)(2,1)}, bf16[1024,128]{1,0:T(8,128)(2,1)S(1)}, u32[]{:S(2)}, u32[]{:S(2)}) %collective-permute-start) | collective-permute-done | bytes 262176 | tf_op jit(solution)/shard_map/ppermute | solution.py:65
  28.3 0.1 collective-permute-start.2
  28.4 0.9 collective-permute-start.5
  29.3 0.1 collective-permute-start.6
  29.4 2.9 %collective-permute-start.3 = (bf16[512,128]{1,0:T(8,128)(2,1)S(1)}, bf16[512,128]{1,0:T(8,128)(2,1)S(1)}, u32[]{:S(2)}, u32[]{:S(2)}) collective-permute-start(bf16[512,128]{1,0:T(8,128)(2,1)S(1)} %slice.21), channel_id=1, source_target_pairs={{0,6},{1,7},{2,0},{3,1},{4,2},{5,3},{6,4},{7,5},{8,14},{9,15},{10,... | collective-permute-start | bytes 393224 | tf_op jit(solution)/shard_map/ppermute | solution.py:65
  32.3 1.6 %collective-permute-done.2.refs_4_ = bf16[512,128]{1,0:T(8,128)(2,1)S(1)} collective-permute-done((bf16[512,128]{1,0:T(8,128)(2,1)S(1)}, bf16[512,128]{1,0:T(8,128)(2,1)S(1)}, u32[]{:S(2)}, u32[]{:S(2)}) %collective-permute-start.2) | collective-permute-done | bytes 131104 | tf_op jit(solution)/shard_map/ppermute | solution.py:65
  33.9 1.6 %collective-permute-start.7 = (bf16[512,128]{1,0:T(8,128)(2,1)S(1)}, bf16[512,128]{1,0:T(8,128)(2,1)S(1)}, u32[]{:S(2)}, u32[]{:S(2)}) collective-permute-start(bf16[512,128]{1,0:T(8,128)(2,1)S(1)} %collective-permute-done.2.refs_4_), channel_id=1, source_target_pairs={{0,1},{1,0},{2,3},{3,2},{4,5},{5,4},{6,7},{7,6},{8,9},{9,8},{10,11... | collective-permute-start | bytes 393224 | tf_op jit(solution)/shard_map/ppermute | solution.py:65
  35.5 0.5 collective-permute-start.8
  36.0 0.5 collective-permute-done.7.refs_9_
  36.5 0.5 collective-permute-done.8.refs_10_
  37.0 1.0 copy-done.1
  38.0 2.9 %shard_map.87 = (bf16[8,176,128]{2,1,0:T(8,128)(2,1)}, f32[8,128]{1,0:T(8,128)S(1)}, f32[8,128]{1,0:T(8,128)S(1)}) custom-call(bf16[8,144,384]{2,1,0:T(8,128)(2,1)S(1)} %all-to-all-done.refs_0_, bf16[1024,128]{1,0:T(8,128)(2,1)S(1)} %copy-done.1, bf16[1024,128]{1,0:T(8,128)(2,1)S(1)} %collective-permute-done.refs_2_, ...), custom_call_target="tpu_custom_call" | custom-call | flops 536870912 | bytes 3350528 | tf_op jit(solution)/shard_map/pallas_call | solution.py:36
  40.8 7.5 %all-to-all-start.1 = ((bf16[8,176,128]{2,1,0:T(8,128)(2,1)}), bf16[8,176,128]{2,1,0:T(8,128)(2,1)S(1)}, u32[]{:S(2)}, u32[]{:S(2)}) async-start(bf16[8,176,128]{2,1,0:T(8,128)(2,1)} %get-tuple-element.16), calls=%async_computation.1 | async-start | bytes 720896 | tf_op jit(solution)/shard_map/all_to_all | solution.py:57
  48.3 0.0 copy-start.2
  48.3 0.9 copy-done.2
  49.3 0.9 copy-done.6
  50.2 0.9 copy-done.8
  51.1 0.9 copy-done.10
  52.0 3.1 %shard_map.88 = (bf16[1024,128]{1,0:T(8,128)(2,1)S(1)}, f32[1024,128]{1,0:T(8,128)S(1)}, bf16[384,1024]{1,0:T(8,128)(2,1)S(1)}, bf16[2064,128]{1,0:T(8,128)(2,1)S(1)}) custom-call(bf16[8,144,384]{2,1,0:T(8,128)(2,1)S(1)} %all-to-all-done.refs_0_, bf16[1024,128]{1,0:T(8,128)(2,1)S(1)} %copy-done.2, bf16[1024,128]{1,0:T(8,128)(2,1)S(1)} %collective-permute-done.refs_2_, ...), custom_call_target="tpu_custom_call" | custom-call | flops 536870912 | bytes 5091328 | tf_op jit(solution)/shard_map/pallas_call | solution.py:36
  55.1 0.9 copy-done.3
  56.0 0.8 copy-done.14
  56.8 6.0 %all-to-all-done.1.refs_0_ = bf16[8,176,128]{2,1,0:T(8,128)(2,1)S(1)} async-done(((bf16[8,176,128]{2,1,0:T(8,128)(2,1)}), bf16[8,176,128]{2,1,0:T(8,128)(2,1)S(1)}, u32[]{:S(2)}, u32[]{:S(2)}) %all-to-all-start.1) | async-done | bytes 360480 | tf_op jit(solution)/shard_map/all_to_all | solution.py:57
  62.7 0.9 shard_map.89
  63.6 4.0 %all-to-all-start.2 = ((bf16[4,400,128]{2,1,0:T(8,128)(2,1)}), bf16[4,400,128]{2,1,0:T(8,128)(2,1)S(1)}, u32[]{:S(2)}, u32[]{:S(2)}) async-start(bf16[4,400,128]{2,1,0:T(8,128)(2,1)} %get-tuple-element.23), calls=%async_computation.2 | async-start | bytes 819200 | tf_op jit(solution)/shard_map/all_to_all | solution.py:57
  67.6 0.7 collective-permute-start.9
  68.3 6.6 %all-to-all-done.2.refs_0_ = bf16[4,400,128]{2,1,0:T(8,128)(2,1)S(1)} async-done(((bf16[4,400,128]{2,1,0:T(8,128)(2,1)}), bf16[4,400,128]{2,1,0:T(8,128)(2,1)S(1)}, u32[]{:S(2)}, u32[]{:S(2)}) %all-to-all-start.2) | async-done | bytes 409632 | tf_op jit(solution)/shard_map/all_to_all | solution.py:57
  74.9 3.5 %collective-permute-start.11 = (bf16[1024,128]{1,0:T(8,128)(2,1)S(1)}, bf16[1024,128]{1,0:T(8,128)(2,1)S(1)}, u32[]{:S(2)}, u32[]{:S(2)}) collective-permute-start(bf16[1024,128]{1,0:T(8,128)(2,1)S(1)} %bitcast.7), channel_id=1, source_target_pairs={{0,6},{1,7},{2,0},{3,1},{4,2},{5,3},{6,4},{7,5},{8,14},{9,15},{10,... | collective-permute-start | bytes 786440 | tf_op jit(solution)/shard_map/ppermute | solution.py:65
  78.4 3.7 %collective-permute-done.11.refs_6_ = bf16[1024,128]{1,0:T(8,128)(2,1)S(1)} collective-permute-done((bf16[1024,128]{1,0:T(8,128)(2,1)S(1)}, bf16[1024,128]{1,0:T(8,128)(2,1)S(1)}, u32[]{:S(2)}, u32[]{:S(2)}) %collective-permute-start.11) | collective-permute-done | bytes 262176 | tf_op jit(solution)/shard_map/ppermute | solution.py:65
  82.1 3.5 %collective-permute-start.13 = (bf16[768,128]{1,0:T(8,128)(2,1)S(1)}, bf16[768,128]{1,0:T(8,128)(2,1)S(1)}, u32[]{:S(2)}, u32[]{:S(2)}) collective-permute-start(bf16[768,128]{1,0:T(8,128)(2,1)S(1)} %slice.24), channel_id=1, source_target_pairs={{0,6},{1,7},{2,0},{3,1},{4,2},{5,3},{6,4},{7,5},{8,14},{9,15},{10,... | collective-permute-start | bytes 589832 | tf_op jit(solution)/shard_map/ppermute | solution.py:65
  85.6 0.8 copy-done.12
  86.5 1.5 %shard_map.90 = bf16[8,128,128]{2,1,0:T(8,128)(2,1)} custom-call(bf16[4,400,128]{2,1,0:T(8,128)(2,1)S(1)} %all-to-all-done.2.refs_0_, f32[128,128]{1,0:T(8,128)S(1)} %copy-done.12, f32[8,128]{1,0:T(8,128)S(1)} %get-tuple-element.25.refs_2_, bf16[1024,128]{1,0:T(8,128)(2,1)S(1)} %get-tuple-element.20.refs_2_.refs_3_, ...), custom_call_target="tpu_custom_call" | custom-call | flops 33554432 | bytes 1536000 | tf_op jit(solution)/shard_map/pallas_call | solution.py:36
  88.0 6.4 %all-to-all-start.3 = ((bf16[8,128,128]{2,1,0:T(8,128)(2,1)}), bf16[8,128,128]{2,1,0:T(8,128)(2,1)S(1)}, u32[]{:S(2)}, u32[]{:S(2)}) async-start(bf16[8,128,128]{2,1,0:T(8,128)(2,1)} %shard_map.90), calls=%async_computation.3 | async-start | bytes 524288 | tf_op jit(solution)/shard_map/all_to_all | solution.py:57
  94.4 0.2 collective-permute-start.14
  94.6 0.3 collective-permute-start.15
  94.9 0.2 collective-permute-start.16
  95.1 0.3 collective-permute-start.18
  95.4 0.8 slice.23
  96.2 1.4 %collective-permute-start.12 = (bf16[256,128]{1,0:T(8,128)(2,1)S(1)}, bf16[256,128]{1,0:T(8,128)(2,1)S(1)}, u32[]{:S(2)}, u32[]{:S(2)}) collective-permute-start(bf16[256,128]{1,0:T(8,128)(2,1)S(1)} %slice.23), channel_id=1, source_target_pairs={{0,2},{1,3},{2,4},{3,5},{4,6},{5,7},{6,0},{7,1},{8,10},{9,11},{10,... | collective-permute-start | bytes 196616 | tf_op jit(solution)/shard_map/ppermute | solution.py:65
  97.6 4.6 %collective-permute-done.12.refs_7_ = bf16[256,128]{1,0:T(8,128)(2,1)S(1)} collective-permute-done((bf16[256,128]{1,0:T(8,128)(2,1)S(1)}, bf16[256,128]{1,0:T(8,128)(2,1)S(1)}, u32[]{:S(2)}, u32[]{:S(2)}) %collective-permute-start.12) | collective-permute-done | bytes 65568 | tf_op jit(solution)/shard_map/ppermute | solution.py:65
  102.3 0.8 collective-permute-start.17
  103.0 3.4 %copy-done = bf16[4,1024,1024]{2,1,0:T(8,128)(2,1)S(1)} copy-done((bf16[4,1024,1024]{2,1,0:T(8,128)(2,1)S(1)}, bf16[4,1024,1024]{2,1,0:T(8,128)(2,1)}, u32[]{:S(2)}) %copy-start) | copy-done | bytes 8388632
  106.4 1.3 %shard_map.91 = (bf16[128,1024]{1,0:T(8,128)(2,1)}, bf16[4,128,1024]{2,1,0:T(8,128)(2,1)S(1)}) custom-call(bf16[8,128,128]{2,1,0:T(8,128)(2,1)S(1)} %all-to-all-done.3.refs_0_, bf16[4,1024,1024]{2,1,0:T(8,128)(2,1)S(1)} %copy-done), custom_call_target="tpu_custom_call" | custom-call | flops 1073741824 | bytes 9961472 | tf_op jit(solution)/shard_map/pallas_call | solution.py:36
  107.8 2.8 %shard_map.92 = f32[4,128]{1,0:T(4,128)} custom-call(bf16[4,128,1024]{2,1,0:T(8,128)(2,1)S(1)} %get-tuple-element.27.refs_0_, bf16[384,1024]{1,0:T(8,128)(2,1)S(1)} %copy-done.4, bf16[2064,128]{1,0:T(8,128)(2,1)S(1)} %collective-permute-done.9.refs_2_, f32[8,128]{1,0:T(8,128)S(1)} %get-tuple-element.18.refs_12_.refs_3_, bf16[1024,128]{1,0:T(8,128)(2,1)S(1)} %bitcast.10, ...), custom_call_target="tpu_custom_call" | custom-call | flops 268435456 | bytes 4466688 | tf_op jit(solution)/shard_map/pallas_call | solution.py:36
  (41 shorter events, 0.2 us)
Async XLA Ops:
  0.6 85.0 %copy-start.13 = (f32[1024]{0:T(1024)S(1)}, f32[1024]{0:T(1024)}, u32[]{:S(2)}) copy-start(f32[1024]{0:T(1024)} %param.10) | copy-start | bytes 12292
  2.8 34.1 %all-to-all-start = ((bf16[8,144,384]{2,1,0:T(8,128)(2,1)}), bf16[8,144,384]{2,1,0:T(8,128)(2,1)S(1)}, u32[]{:S(2)}, u32[]{:S(2)}) async-start(bf16[8,144,384]{2,1,0:T(8,128)(2,1)} %shard_map.86), calls=%async_computation | async-start | bytes 1769472 | tf_op jit(solution)/shard_map/all_to_all | solution.py:57
  9.5 18.8 %collective-permute-start = (bf16[1024,128]{1,0:T(8,128)(2,1)}, bf16[1024,128]{1,0:T(8,128)(2,1)S(1)}, u32[]{:S(2)}, u32[]{:S(2)}) collective-permute-start(bf16[1024,128]{1,0:T(8,128)(2,1)} %refs_1_.6), channel_id=1, source_target_pairs={{0,2},{1,3},{2,4},{3,5},{4,6},{5,7},{6,0},{7,1},{8,10},{9,11},{10,... | collective-permute-start | bytes 786440 | tf_op jit(solution)/shard_map/ppermute | solution.py:65
  10.9 18.4 %collective-permute-start.1 = (bf16[1024,128]{1,0:T(8,128)(2,1)}, bf16[1024,128]{1,0:T(8,128)(2,1)S(1)}, u32[]{:S(2)}, u32[]{:S(2)}) collective-permute-start(bf16[1024,128]{1,0:T(8,128)(2,1)} %refs_1_.6), channel_id=1, source_target_pairs={{0,6},{1,7},{2,0},{3,1},{4,2},{5,3},{6,4},{7,5},{8,14},{9,15},{10,... | collective-permute-start | bytes 786440 | tf_op jit(solution)/shard_map/ppermute | solution.py:65
  12.2 23.8 %collective-permute-start.4 = (bf16[1024,128]{1,0:T(8,128)(2,1)}, bf16[1024,128]{1,0:T(8,128)(2,1)S(1)}, u32[]{:S(2)}, u32[]{:S(2)}) collective-permute-start(bf16[1024,128]{1,0:T(8,128)(2,1)} %refs_1_.6), channel_id=1, source_target_pairs={{0,1},{1,0},{2,3},{3,2},{4,5},{5,4},{6,7},{7,6},{8,9},{9,8},{10,11... | collective-permute-start | bytes 786440 | tf_op jit(solution)/shard_map/ppermute | solution.py:65
  28.3 5.6 %collective-permute-start.2 = (bf16[512,128]{1,0:T(8,128)(2,1)S(1)}, bf16[512,128]{1,0:T(8,128)(2,1)S(1)}, u32[]{:S(2)}, u32[]{:S(2)}) collective-permute-start(bf16[512,128]{1,0:T(8,128)(2,1)S(1)} %slice.20), channel_id=1, source_target_pairs={{0,2},{1,3},{2,4},{3,5},{4,6},{5,7},{6,0},{7,1},{8,10},{9,11},{10,... | collective-permute-start | bytes 393224 | tf_op jit(solution)/shard_map/ppermute | solution.py:65
  28.4 7.6 %collective-permute-start.5 = (bf16[1024,128]{1,0:T(8,128)(2,1)S(1)}, bf16[1024,128]{1,0:T(8,128)(2,1)S(1)}, u32[]{:S(2)}, u32[]{:S(2)}) collective-permute-start(bf16[1024,128]{1,0:T(8,128)(2,1)S(1)} %collective-permute-done.refs_2_), channel_id=1, source_target_pairs={{0,1},{1,0},{2,3},{3,2},{4,5},{5,4},{6,7},{7,6},{8,9},{9,8},{10,11... | collective-permute-start | bytes 786440 | tf_op jit(solution)/shard_map/ppermute | solution.py:65
  29.3 6.8 %collective-permute-start.6 = (bf16[1024,128]{1,0:T(8,128)(2,1)S(1)}, bf16[1024,128]{1,0:T(8,128)(2,1)S(1)}, u32[]{:S(2)}, u32[]{:S(2)}) collective-permute-start(bf16[1024,128]{1,0:T(8,128)(2,1)S(1)} %collective-permute-done.1.refs_3_), channel_id=1, source_target_pairs={{0,1},{1,0},{2,3},{3,2},{4,5},{5,4},{6,7},{7,6},{8,9},{9,8},{10,11... | collective-permute-start | bytes 786440 | tf_op jit(solution)/shard_map/ppermute | solution.py:65
  29.4 6.1 %collective-permute-start.3 = (bf16[512,128]{1,0:T(8,128)(2,1)S(1)}, bf16[512,128]{1,0:T(8,128)(2,1)S(1)}, u32[]{:S(2)}, u32[]{:S(2)}) collective-permute-start(bf16[512,128]{1,0:T(8,128)(2,1)S(1)} %slice.21), channel_id=1, source_target_pairs={{0,6},{1,7},{2,0},{3,1},{4,2},{5,3},{6,4},{7,5},{8,14},{9,15},{10,... | collective-permute-start | bytes 393224 | tf_op jit(solution)/shard_map/ppermute | solution.py:65
  33.9 2.6 %collective-permute-start.7 = (bf16[512,128]{1,0:T(8,128)(2,1)S(1)}, bf16[512,128]{1,0:T(8,128)(2,1)S(1)}, u32[]{:S(2)}, u32[]{:S(2)}) collective-permute-start(bf16[512,128]{1,0:T(8,128)(2,1)S(1)} %collective-permute-done.2.refs_4_), channel_id=1, source_target_pairs={{0,1},{1,0},{2,3},{3,2},{4,5},{5,4},{6,7},{7,6},{8,9},{9,8},{10,11... | collective-permute-start | bytes 393224 | tf_op jit(solution)/shard_map/ppermute | solution.py:65
  35.5 12.8 %copy-start.5 = (bf16[512,128]{1,0:T(8,128)(2,1)}, bf16[512,128]{1,0:T(8,128)(2,1)S(1)}, u32[]{:S(2)}) copy-start(bf16[512,128]{1,0:T(8,128)(2,1)S(1)} %collective-permute-done.3.refs_5_) | copy-start | bytes 393220
  35.5 1.5 %collective-permute-start.8 = (bf16[512,128]{1,0:T(8,128)(2,1)S(1)}, bf16[512,128]{1,0:T(8,128)(2,1)S(1)}, u32[]{:S(2)}, u32[]{:S(2)}) collective-permute-start(bf16[512,128]{1,0:T(8,128)(2,1)S(1)} %collective-permute-done.3.refs_5_), channel_id=1, source_target_pairs={{0,1},{1,0},{2,3},{3,2},{4,5},{5,4},{6,7},{7,6},{8,9},{9,8},{10,11... | collective-permute-start | bytes 393224 | tf_op jit(solution)/shard_map/ppermute | solution.py:65
  36.5 11.8 %copy-start.7 = (bf16[512,128]{1,0:T(8,128)(2,1)}, bf16[512,128]{1,0:T(8,128)(2,1)S(1)}, u32[]{:S(2)}) copy-start(bf16[512,128]{1,0:T(8,128)(2,1)S(1)} %collective-permute-done.7.refs_9_) | copy-start | bytes 393220
  37.0 11.3 %copy-start.9 = (bf16[512,128]{1,0:T(8,128)(2,1)}, bf16[512,128]{1,0:T(8,128)(2,1)S(1)}, u32[]{:S(2)}) copy-start(bf16[512,128]{1,0:T(8,128)(2,1)S(1)} %collective-permute-done.8.refs_10_) | copy-start | bytes 393220
  37.0 1.0 copy-start.1
  40.8 21.9 %all-to-all-start.1 = ((bf16[8,176,128]{2,1,0:T(8,128)(2,1)}), bf16[8,176,128]{2,1,0:T(8,128)(2,1)S(1)}, u32[]{:S(2)}, u32[]{:S(2)}) async-start(bf16[8,176,128]{2,1,0:T(8,128)(2,1)} %get-tuple-element.16), calls=%async_computation.1 | async-start | bytes 720896 | tf_op jit(solution)/shard_map/all_to_all | solution.py:57
  48.3 1.0 copy-start.2
  49.3 0.9 copy-start.6
  50.2 0.9 copy-start.8
  51.1 0.9 copy-start.10
  55.1 0.9 copy-start.3
  56.0 0.8 copy-start.14
  62.7 45.1 %copy-start.4 = (bf16[384,1024]{1,0:T(8,128)(2,1)S(1)}, bf16[384,1024]{1,0:T(8,128)(2,1)}, u32[]{:S(2)}) copy-start(bf16[384,1024]{1,0:T(8,128)(2,1)} %copy-done.3) | copy-start | bytes 2359300
  63.6 18.5 %copy-start.11 = (f32[128,128]{1,0:T(8,128)}, f32[128,128]{1,0:T(8,128)S(1)}, u32[]{:S(2)}) copy-start(f32[128,128]{1,0:T(8,128)S(1)} %get-tuple-element.24.refs_1_) | copy-start | bytes 196612
  63.6 11.3 %all-to-all-start.2 = ((bf16[4,400,128]{2,1,0:T(8,128)(2,1)}), bf16[4,400,128]{2,1,0:T(8,128)(2,1)S(1)}, u32[]{:S(2)}, u32[]{:S(2)}) async-start(bf16[4,400,128]{2,1,0:T(8,128)(2,1)} %get-tuple-element.23), calls=%async_computation.2 | async-start | bytes 819200 | tf_op jit(solution)/shard_map/all_to_all | solution.py:57
  67.6 28.6 %collective-permute-start.9 = (bf16[2064,128]{1,0:T(8,128)(2,1)}, bf16[2064,128]{1,0:T(8,128)(2,1)S(1)}, u32[]{:S(2)}, u32[]{:S(2)}) collective-permute-start(bf16[2064,128]{1,0:T(8,128)(2,1)} %copy-done.14), channel_id=1, source_target_pairs={{14,6},{15,7},{22,14},{23,15},{30,22},{31,23},{38,30},{39,31},{46,... | collective-permute-start | bytes 1585160 | tf_op jit(solution)/shard_map/ppermute | solution.py:374
  74.9 7.2 %collective-permute-start.11 = (bf16[1024,128]{1,0:T(8,128)(2,1)S(1)}, bf16[1024,128]{1,0:T(8,128)(2,1)S(1)}, u32[]{:S(2)}, u32[]{:S(2)}) collective-permute-start(bf16[1024,128]{1,0:T(8,128)(2,1)S(1)} %bitcast.7), channel_id=1, source_target_pairs={{0,6},{1,7},{2,0},{3,1},{4,2},{5,3},{6,4},{7,5},{8,14},{9,15},{10,... | collective-permute-start | bytes 786440 | tf_op jit(solution)/shard_map/ppermute | solution.py:65
  78.4 16.1 %collective-permute-start.10 = (bf16[1024,128]{1,0:T(8,128)(2,1)S(1)}, bf16[1024,128]{1,0:T(8,128)(2,1)}, u32[]{:S(2)}, u32[]{:S(2)}) collective-permute-start(bf16[1024,128]{1,0:T(8,128)(2,1)S(1)} %bitcast.8), channel_id=1, source_target_pairs={{0,2},{1,3},{2,4},{3,5},{4,6},{5,7},{6,0},{7,1},{8,10},{9,11},{10,... | collective-permute-start | bytes 786440 | tf_op jit(solution)/shard_map/ppermute | solution.py:65
  82.1 12.9 %collective-permute-start.13 = (bf16[768,128]{1,0:T(8,128)(2,1)S(1)}, bf16[768,128]{1,0:T(8,128)(2,1)S(1)}, u32[]{:S(2)}, u32[]{:S(2)}) collective-permute-start(bf16[768,128]{1,0:T(8,128)(2,1)S(1)} %slice.24), channel_id=1, source_target_pairs={{0,6},{1,7},{2,0},{3,1},{4,2},{5,3},{6,4},{7,5},{8,14},{9,15},{10,... | collective-permute-start | bytes 589832 | tf_op jit(solution)/shard_map/ppermute | solution.py:65
  85.6 0.8 copy-start.12
  88.0 15.1 %all-to-all-start.3 = ((bf16[8,128,128]{2,1,0:T(8,128)(2,1)}), bf16[8,128,128]{2,1,0:T(8,128)(2,1)S(1)}, u32[]{:S(2)}, u32[]{:S(2)}) async-start(bf16[8,128,128]{2,1,0:T(8,128)(2,1)} %shard_map.90), calls=%async_computation.3 | async-start | bytes 524288 | tf_op jit(solution)/shard_map/all_to_all | solution.py:57
  94.4 13.3 %collective-permute-start.14 = (bf16[1024,128]{1,0:T(8,128)(2,1)S(1)}, bf16[1024,128]{1,0:T(8,128)(2,1)S(1)}, u32[]{:S(2)}, u32[]{:S(2)}) collective-permute-start(bf16[1024,128]{1,0:T(8,128)(2,1)S(1)} %bitcast.9), channel_id=1, source_target_pairs={{0,1},{1,0},{2,3},{3,2},{4,5},{5,4},{6,7},{7,6},{8,9},{9,8},{10,11... | collective-permute-start | bytes 786440 | tf_op jit(solution)/shard_map/ppermute | solution.py:65
  94.6 13.2 %collective-permute-start.15 = (bf16[1024,128]{1,0:T(8,128)(2,1)}, bf16[1024,128]{1,0:T(8,128)(2,1)S(1)}, u32[]{:S(2)}, u32[]{:S(2)}) collective-permute-start(bf16[1024,128]{1,0:T(8,128)(2,1)} %collective-permute-done.10.refs_5_), channel_id=1, source_target_pairs={{0,1},{1,0},{2,3},{3,2},{4,5},{5,4},{6,7},{7,6},{8,9},{9,8},{10,11... | collective-permute-start | bytes 786440 | tf_op jit(solution)/shard_map/ppermute | solution.py:65
  94.9 12.9 %collective-permute-start.16 = (bf16[1024,128]{1,0:T(8,128)(2,1)S(1)}, bf16[1024,128]{1,0:T(8,128)(2,1)S(1)}, u32[]{:S(2)}, u32[]{:S(2)}) collective-permute-start(bf16[1024,128]{1,0:T(8,128)(2,1)S(1)} %collective-permute-done.11.refs_6_), channel_id=1, source_target_pairs={{0,1},{1,0},{2,3},{3,2},{4,5},{5,4},{6,7},{7,6},{8,9},{9,8},{10,11... | collective-permute-start | bytes 786440 | tf_op jit(solution)/shard_map/ppermute | solution.py:65
  95.1 12.7 %collective-permute-start.18 = (bf16[768,128]{1,0:T(8,128)(2,1)S(1)}, bf16[768,128]{1,0:T(8,128)(2,1)S(1)}, u32[]{:S(2)}, u32[]{:S(2)}) collective-permute-start(bf16[768,128]{1,0:T(8,128)(2,1)S(1)} %collective-permute-done.13.refs_8_), channel_id=1, source_target_pairs={{0,1},{1,0},{2,3},{3,2},{4,5},{5,4},{6,7},{7,6},{8,9},{9,8},{10,11... | collective-permute-start | bytes 589832 | tf_op jit(solution)/shard_map/ppermute | solution.py:65
  96.2 6.0 %collective-permute-start.12 = (bf16[256,128]{1,0:T(8,128)(2,1)S(1)}, bf16[256,128]{1,0:T(8,128)(2,1)S(1)}, u32[]{:S(2)}, u32[]{:S(2)}) collective-permute-start(bf16[256,128]{1,0:T(8,128)(2,1)S(1)} %slice.23), channel_id=1, source_target_pairs={{0,2},{1,3},{2,4},{3,5},{4,6},{5,7},{6,0},{7,1},{8,10},{9,11},{10,... | collective-permute-start | bytes 196616 | tf_op jit(solution)/shard_map/ppermute | solution.py:65
  102.3 5.5 %collective-permute-start.17 = (bf16[256,128]{1,0:T(8,128)(2,1)S(1)}, bf16[256,128]{1,0:T(8,128)(2,1)S(1)}, u32[]{:S(2)}, u32[]{:S(2)}) collective-permute-start(bf16[256,128]{1,0:T(8,128)(2,1)S(1)} %collective-permute-done.12.refs_7_), channel_id=1, source_target_pairs={{0,1},{1,0},{2,3},{3,2},{4,5},{5,4},{6,7},{7,6},{8,9},{9,8},{10,11... | collective-permute-start | bytes 196616 | tf_op jit(solution)/shard_map/ppermute | solution.py:65
  103.0 3.4 %copy-start = (bf16[4,1024,1024]{2,1,0:T(8,128)(2,1)S(1)}, bf16[4,1024,1024]{2,1,0:T(8,128)(2,1)}, u32[]{:S(2)}) copy-start(bf16[4,1024,1024]{2,1,0:T(8,128)(2,1)} %refs_1_.7) | copy-start | bytes 25165828

commit v6 on v5

--- a/solution.py
+++ b/solution.py
@@ -70,6 +70,12 @@
     other = hop(x, 0, True)
     far_a, far_b = hop(up[:cut], 1), hop(dn[cut:], -1)
     return [x, up, dn, far_a, far_b], [other] + [hop(a, 0, True) for a in (up, dn, far_a, far_b)]
+
+
+def spread_down(x):
+    up, dn = hop(x, 1), hop(x, -1)
+    far = hop(dn, -1)
+    return [x, up, dn, far], [hop(a, 0, True) for a in (x, up, dn, far)]
 
 
 def split3(x):
@@ -287,8 +293,8 @@
 
 
 def loss_kernel(predicted, window, halo_far, masks, *refs):
-    mine, theirs = refs[0:5], refs[5:10]
-    loss, ahead, halo, sem = refs[10:14]
+    mine, theirs = refs[0:4], refs[4:8]
+    loss, ahead, halo, sem = refs[8:12]
     arrival = pltpu.make_async_copy(halo_far, halo, sem)
     arrival.start()
     _, _, y_at, core = place()
@@ -297,7 +303,7 @@
     for j in range(K):
         logits = jnp.zeros((n, LEN), F32)
         for i, y in enumerate(homes(y_at)):
-            k, lo = (i, j * n) if i < 3 else (3, 0) if j == 0 else (4, (j - 1) * n)
+            k, lo = i, j * n
             both = jnp.concatenate([mine[k][lo : lo + n], theirs[k][lo : lo + n]], axis=1)
             lanes = [pl.ds(pl.multiple_of((2 * y + who) * D, D), D) for who in (core, 1 - core)]
             part = jnp.concatenate([predicted[j, :, lanes[0]], predicted[j, :, lanes[1]]], axis=1)
@@ -378,7 +384,7 @@
     )
     bank = x_in[:, D + 16 :].reshape(XS * ZS, K, NCH, D).transpose(1, 0, 2, 3).reshape(K * NSEQ * NCH, D)
     context = exchange(context, "ch")
-    bank_mine, bank_theirs = spread(bank, NSEQ * NCH)
+    bank_mine, bank_theirs = spread_down(bank)
     context, predicted = call(
         predict_kernel, [shape((LEN, CIN), BF16), shape((K, LEN, CIN), BF16)], [context, w_pred],
         flops=K * 2 * LEN * CIN * CIN,

time: 111 us -> 107 us (0.964)
  blocking collectives: 0 us -> 11.2 us
  waiting for transfers between devices: 38.8 us -> 32.1 us
  starting transfers between devices: 44.9 us -> 38.9 us
  local copies, waits for them, and re-layouts: 11.5 us -> 9.81 us
    all_to_all x0 -> x1, blocking collectives: none -> 11.2 us  [exchange(): lax.all_to_all(x, axis, split_axis=0, concat_axis=0, axis_index_groups=gr...]
    ppermute x18 -> x16, waiting for transfers between devices: 26.3 us -> 20.7 us  [hop(): return lax.ppermute(x, 'ch', pairs)]
    all_to_all x4 -> x3, starting transfers between devices: 24.5 us -> 20.5 us  [exchange(): lax.all_to_all(x, axis, split_axis=0, concat_axis=0, axis_index_groups=gr...]
    ppermute x18 -> x16, starting transfers between devices: 19.7 us -> 17.7 us  [hop(): return lax.ppermute(x, 'ch', pairs)]
    all_to_all x4 -> x3, waiting for transfers between devices: 12.5 us -> 11.5 us  [exchange(): lax.all_to_all(x, axis, split_axis=0, concat_axis=0, axis_index_groups=gr...]
    unnamed x30 -> x26, local copies, waits for them, and re-layouts: 10.6 us -> 9.73 us
  transfers between devices with their start and end apart: 23 -> 20, of which waited for: 8 -> 7; matrix products, arithmetic and copies ran while one was open for 1% -> 0% of each run, Pallas kernels for 5% -> 5%
where the time goes in v6:
time: 107 us
  starting transfers between devices  38.9 us (36%)
  waiting for transfers between devices  32.1 us (30%)
  Pallas kernels  13.8 us (13%)
  blocking collectives  11.2 us (10%)
  local copies, waits for them, and re-layouts  9.81 us (9%)
    ppermute x16, waiting for transfers between devices, hop(): return lax.ppermute(x, 'ch', pairs)  20.7 us
    all_to_all x3, starting transfers between devices, exchange(): lax.all_to_all(x, axis, split_axis=0, concat_axis=0, axis_index_groups=gr...  20.5 us
    ppermute x16, starting transfers between devices, hop(): return lax.ppermute(x, 'ch', pairs)  17.7 us
    pallas_call x7, Pallas kernels, call(): pl.pallas_call(kernel, out_shape=out, in_specs=[pl.BlockSpec(memory_space...  13.8 us
    all_to_all x3, waiting for transfers between devices, exchange(): lax.all_to_all(x, axis, split_axis=0, concat_axis=0, axis_index_groups=gr...  11.5 us
    all_to_all x1, blocking collectives, exchange(): lax.all_to_all(x, axis, split_axis=0, concat_axis=0, axis_index_groups=gr...  11.2 us
    unnamed x26, local copies, waits for them, and re-layouts  9.73 us
  transfers between devices with their start and end apart: 20, of which 7 were waited for; matrix products, arithmetic and copies ran while one was open for 0% of the time, Pallas kernels for 5%

profile of v6, /device:TPU:1, one launch (start us, length us, event | category | flops | bytes accessed | tf_op | source)
XLA Modules:
  0.0 106.8 jit_solution(10652478147369112714)
XLA Ops:
  0.6 2.2 %shard_map.86 = bf16[8,144,384]{2,1,0:T(8,128)(2,1)} custom-call(bf16[128,3072]{1,0:T(8,128)(2,1)} %refs_0_.1, f32[8,128]{1,0:T(8,128)} %refs_1_.4, s32[1,128]{1,0:T(1,128)} %bitcast.13, s32[1,4]{1,0:T(1,128)} %bitcast.14), custom_call_target="tpu_custom_call" | custom-call | bytes 1675792 | tf_op jit(solution)/shard_map/pallas_call | solution.py:36
  2.9 6.7 %all-to-all-start = ((bf16[8,144,384]{2,1,0:T(8,128)(2,1)}), bf16[8,144,384]{2,1,0:T(8,128)(2,1)S(1)}, u32[]{:S(2)}, u32[]{:S(2)}) async-start(bf16[8,144,384]{2,1,0:T(8,128)(2,1)} %shard_map.86), calls=%async_computation | async-start | bytes 1769472 | tf_op jit(solution)/shard_map/all_to_all | solution.py:57
  9.5 1.4 %collective-permute-start = (bf16[1024,128]{1,0:T(8,128)(2,1)}, bf16[1024,128]{1,0:T(8,128)(2,1)S(1)}, u32[]{:S(2)}, u32[]{:S(2)}) collective-permute-start(bf16[1024,128]{1,0:T(8,128)(2,1)} %refs_1_.6), channel_id=1, source_target_pairs={{0,2},{1,3},{2,4},{3,5},{4,6},{5,7},{6,0},{7,1},{8,10},{9,11},{10,... | collective-permute-start | bytes 786440 | tf_op jit(solution)/shard_map/ppermute | solution.py:65
  10.9 1.3 %collective-permute-start.1 = (bf16[1024,128]{1,0:T(8,128)(2,1)}, bf16[1024,128]{1,0:T(8,128)(2,1)S(1)}, u32[]{:S(2)}, u32[]{:S(2)}) collective-permute-start(bf16[1024,128]{1,0:T(8,128)(2,1)} %refs_1_.6), channel_id=1, source_target_pairs={{0,6},{1,7},{2,0},{3,1},{4,2},{5,3},{6,4},{7,5},{8,14},{9,15},{10,... | collective-permute-start | bytes 786440 | tf_op jit(solution)/shard_map/ppermute | solution.py:65
  12.2 0.7 collective-permute-start.4
  12.9 15.4 %collective-permute-done.refs_2_ = bf16[1024,128]{1,0:T(8,128)(2,1)S(1)} collective-permute-done((bf16[1024,128]{1,0:T(8,128)(2,1)}, bf16[1024,128]{1,0:T(8,128)(2,1)S(1)}, u32[]{:S(2)}, u32[]{:S(2)}) %collective-permute-start) | collective-permute-done | bytes 262176 | tf_op jit(solution)/shard_map/ppermute | solution.py:65
  28.3 0.1 collective-permute-start.2
  28.4 0.9 collective-permute-start.5
  29.3 0.1 collective-permute-start.6
  29.4 2.9 %collective-permute-start.3 = (bf16[512,128]{1,0:T(8,128)(2,1)S(1)}, bf16[512,128]{1,0:T(8,128)(2,1)S(1)}, u32[]{:S(2)}, u32[]{:S(2)}) collective-permute-start(bf16[512,128]{1,0:T(8,128)(2,1)S(1)} %slice.13), channel_id=1, source_target_pairs={{0,6},{1,7},{2,0},{3,1},{4,2},{5,3},{6,4},{7,5},{8,14},{9,15},{10,... | collective-permute-start | bytes 393224 | tf_op jit(solution)/shard_map/ppermute | solution.py:65
  32.3 1.6 %collective-permute-done.2.refs_4_ = bf16[512,128]{1,0:T(8,128)(2,1)S(1)} collective-permute-done((bf16[512,128]{1,0:T(8,128)(2,1)S(1)}, bf16[512,128]{1,0:T(8,128)(2,1)S(1)}, u32[]{:S(2)}, u32[]{:S(2)}) %collective-permute-start.2) | collective-permute-done | bytes 131104 | tf_op jit(solution)/shard_map/ppermute | solution.py:65
  33.9 1.6 %collective-permute-start.7 = (bf16[512,128]{1,0:T(8,128)(2,1)S(1)}, bf16[512,128]{1,0:T(8,128)(2,1)S(1)}, u32[]{:S(2)}, u32[]{:S(2)}) collective-permute-start(bf16[512,128]{1,0:T(8,128)(2,1)S(1)} %collective-permute-done.2.refs_4_), channel_id=1, source_target_pairs={{0,1},{1,0},{2,3},{3,2},{4,5},{5,4},{6,7},{7,6},{8,9},{9,8},{10,11... | collective-permute-start | bytes 393224 | tf_op jit(solution)/shard_map/ppermute | solution.py:65
  35.5 0.0 collective-permute-done.3.refs_5_
  35.5 0.5 collective-permute-start.8
  36.0 0.5 collective-permute-done.7.refs_9_
  36.5 0.5 collective-permute-done.8.refs_10_
  37.0 0.0 all-to-all-done.refs_0_
  37.0 1.0 copy-done.1
  38.0 2.8 %shard_map.87 = (bf16[8,176,128]{2,1,0:T(8,128)(2,1)}, f32[8,128]{1,0:T(8,128)S(1)}, f32[8,128]{1,0:T(8,128)S(1)}) custom-call(bf16[8,144,384]{2,1,0:T(8,128)(2,1)S(1)} %all-to-all-done.refs_0_, bf16[1024,128]{1,0:T(8,128)(2,1)S(1)} %copy-done.1, bf16[1024,128]{1,0:T(8,128)(2,1)S(1)} %collective-permute-done.refs_2_, ...), custom_call_target="tpu_custom_call" | custom-call | flops 536870912 | bytes 3350528 | tf_op jit(solution)/shard_map/pallas_call | solution.py:36
  40.8 7.5 %all-to-all-start.1 = ((bf16[8,176,128]{2,1,0:T(8,128)(2,1)}), bf16[8,176,128]{2,1,0:T(8,128)(2,1)S(1)}, u32[]{:S(2)}, u32[]{:S(2)}) async-start(bf16[8,176,128]{2,1,0:T(8,128)(2,1)} %get-tuple-element.16), calls=%async_computation.1 | async-start | bytes 720896 | tf_op jit(solution)/shard_map/all_to_all | solution.py:57
  48.3 0.0 copy-start.2
  48.3 0.9 copy-done.2
  49.3 0.9 copy-done.6
  50.2 0.9 copy-done.8
  51.1 0.9 copy-done.10
  52.0 3.0 %shard_map.88 = (bf16[1024,128]{1,0:T(8,128)(2,1)S(1)}, f32[1024,128]{1,0:T(8,128)S(1)}, bf16[384,1024]{1,0:T(8,128)(2,1)S(1)}, bf16[2064,128]{1,0:T(8,128)(2,1)S(1)}) custom-call(bf16[8,144,384]{2,1,0:T(8,128)(2,1)S(1)} %all-to-all-done.refs_0_, bf16[1024,128]{1,0:T(8,128)(2,1)S(1)} %copy-done.2, bf16[1024,128]{1,0:T(8,128)(2,1)S(1)} %collective-permute-done.refs_2_, ...), custom_call_target="tpu_custom_call" | custom-call | flops 536870912 | bytes 5091328 | tf_op jit(solution)/shard_map/pallas_call | solution.py:36
  55.0 0.9 copy-done.3
  55.9 0.8 copy-done.12
  56.7 6.0 %all-to-all-done.1.refs_0_ = bf16[8,176,128]{2,1,0:T(8,128)(2,1)S(1)} async-done(((bf16[8,176,128]{2,1,0:T(8,128)(2,1)}), bf16[8,176,128]{2,1,0:T(8,128)(2,1)S(1)}, u32[]{:S(2)}, u32[]{:S(2)}) %all-to-all-start.1) | async-done | bytes 360480 | tf_op jit(solution)/shard_map/all_to_all | solution.py:57
  62.7 0.1 shard_map.89
  62.8 11.2 %all_to_all.20.refs_0_ = bf16[4,400,128]{2,1,0:T(8,128)(2,1)S(1)} all-to-all(bf16[4,400,128]{2,1,0:T(8,128)(2,1)S(1)} %get-tuple-element.23), channel_id=1, replica_groups={{0,64,128,192},{8,72,136,200},{16,80,144,208},{24,88,152,216},{32,96,16..., dimensions={0} | all-to-all | bytes 819200 | tf_op jit(solution)/shard_map/all_to_all | solution.py:57
  74.1 3.5 %collective-permute-start.11 = (bf16[1024,128]{1,0:T(8,128)(2,1)S(1)}, bf16[1024,128]{1,0:T(8,128)(2,1)S(1)}, u32[]{:S(2)}, u32[]{:S(2)}) collective-permute-start(bf16[1024,128]{1,0:T(8,128)(2,1)S(1)} %bitcast.7), channel_id=1, source_target_pairs={{0,6},{1,7},{2,0},{3,1},{4,2},{5,3},{6,4},{7,5},{8,14},{9,15},{10,... | collective-permute-start | bytes 786440 | tf_op jit(solution)/shard_map/ppermute | solution.py:65
  77.6 0.7 collective-permute-start.9
  78.3 0.3 collective-permute-start.10
  78.6 2.8 %collective-permute-done.11.refs_6_ = bf16[1024,128]{1,0:T(8,128)(2,1)S(1)} collective-permute-done((bf16[1024,128]{1,0:T(8,128)(2,1)S(1)}, bf16[1024,128]{1,0:T(8,128)(2,1)S(1)}, u32[]{:S(2)}, u32[]{:S(2)}) %collective-permute-start.11) | collective-permute-done | bytes 262176 | tf_op jit(solution)/shard_map/ppermute | solution.py:65
  81.3 3.4 %collective-permute-start.12 = (bf16[1024,128]{1,0:T(8,128)(2,1)S(1)}, bf16[1024,128]{1,0:T(8,128)(2,1)}, u32[]{:S(2)}, u32[]{:S(2)}) collective-permute-start(bf16[1024,128]{1,0:T(8,128)(2,1)S(1)} %collective-permute-done.11.refs_6_), channel_id=1, source_target_pairs={{0,6},{1,7},{2,0},{3,1},{4,2},{5,3},{6,4},{7,5},{8,14},{9,15},{10,... | collective-permute-start | bytes 786440 | tf_op jit(solution)/shard_map/ppermute | solution.py:65
  84.7 1.5 %shard_map.90 = bf16[8,128,128]{2,1,0:T(8,128)(2,1)} custom-call(bf16[4,400,128]{2,1,0:T(8,128)(2,1)S(1)} %all_to_all.20.refs_0_, f32[128,128]{1,0:T(8,128)S(1)} %get-tuple-element.24.refs_1_, f32[8,128]{1,0:T(8,128)S(1)} %get-tuple-element.25.refs_2_, bf16[1024,128]{1,0:T(8,128)(2,1)S(1)} %get-tuple-element.20.refs_2_.refs_3_, ...), custom_call_target="tpu_custom_call" | custom-call | flops 33554432 | bytes 1536000 | tf_op jit(solution)/shard_map/pallas_call | solution.py:36
  86.2 6.4 %all-to-all-start.3 = ((bf16[8,128,128]{2,1,0:T(8,128)(2,1)}), bf16[8,128,128]{2,1,0:T(8,128)(2,1)S(1)}, u32[]{:S(2)}, u32[]{:S(2)}) async-start(bf16[8,128,128]{2,1,0:T(8,128)(2,1)} %shard_map.90), calls=%async_computation.3 | async-start | bytes 524288 | tf_op jit(solution)/shard_map/all_to_all | solution.py:57
  92.6 0.2 collective-permute-start.13
  92.8 0.3 collective-permute-start.15
  93.1 0.2 collective-permute-start.14
  93.3 0.3 collective-permute-start.16
  93.6 5.5 %all-to-all-done.3.refs_0_ = bf16[8,128,128]{2,1,0:T(8,128)(2,1)S(1)} async-done(((bf16[8,128,128]{2,1,0:T(8,128)(2,1)}), bf16[8,128,128]{2,1,0:T(8,128)(2,1)S(1)}, u32[]{:S(2)}, u32[]{:S(2)}) %all-to-all-start.3) | async-done | bytes 262176 | tf_op jit(solution)/shard_map/all_to_all | solution.py:57
  99.1 3.4 %copy-done = bf16[4,1024,1024]{2,1,0:T(8,128)(2,1)S(1)} copy-done((bf16[4,1024,1024]{2,1,0:T(8,128)(2,1)S(1)}, bf16[4,1024,1024]{2,1,0:T(8,128)(2,1)}, u32[]{:S(2)}) %copy-start) | copy-done | bytes 8388632
  102.5 1.3 %shard_map.91 = (bf16[128,1024]{1,0:T(8,128)(2,1)}, bf16[4,128,1024]{2,1,0:T(8,128)(2,1)S(1)}) custom-call(bf16[8,128,128]{2,1,0:T(8,128)(2,1)S(1)} %all-to-all-done.3.refs_0_, bf16[4,1024,1024]{2,1,0:T(8,128)(2,1)S(1)} %copy-done), custom_call_target="tpu_custom_call" | custom-call | flops 1073741824 | bytes 9961472 | tf_op jit(solution)/shard_map/pallas_call | solution.py:36
  103.8 0.0 collective-permute-done.9.refs_2_
  103.8 0.0 collective-permute-done.15.refs_10_
  103.8 2.8 %shard_map.92 = f32[4,128]{1,0:T(4,128)} custom-call(bf16[4,128,1024]{2,1,0:T(8,128)(2,1)S(1)} %get-tuple-element.27.refs_0_, bf16[384,1024]{1,0:T(8,128)(2,1)S(1)} %copy-done.4, bf16[2064,128]{1,0:T(8,128)(2,1)S(1)} %collective-permute-done.9.refs_2_, f32[8,128]{1,0:T(8,128)S(1)} %get-tuple-element.18.refs_12_.refs_3_, bf16[1024,128]{1,0:T(8,128)(2,1)S(1)} %bitcast.10, ...), custom_call_target="tpu_custom_call" | custom-call | flops 268435456 | bytes 4466688 | tf_op jit(solution)/shard_map/pallas_call | solution.py:36
  (30 shorter events, 0.1 us)
Async XLA Ops:
  0.6 84.1 %copy-start.11 = (f32[1024]{0:T(1024)S(1)}, f32[1024]{0:T(1024)}, u32[]{:S(2)}) copy-start(f32[1024]{0:T(1024)} %param.10) | copy-start | bytes 12292
  2.9 34.1 %all-to-all-start = ((bf16[8,144,384]{2,1,0:T(8,128)(2,1)}), bf16[8,144,384]{2,1,0:T(8,128)(2,1)S(1)}, u32[]{:S(2)}, u32[]{:S(2)}) async-start(bf16[8,144,384]{2,1,0:T(8,128)(2,1)} %shard_map.86), calls=%async_computation | async-start | bytes 1769472 | tf_op jit(solution)/shard_map/all_to_all | solution.py:57
  9.5 18.8 %collective-permute-start = (bf16[1024,128]{1,0:T(8,128)(2,1)}, bf16[1024,128]{1,0:T(8,128)(2,1)S(1)}, u32[]{:S(2)}, u32[]{:S(2)}) collective-permute-start(bf16[1024,128]{1,0:T(8,128)(2,1)} %refs_1_.6), channel_id=1, source_target_pairs={{0,2},{1,3},{2,4},{3,5},{4,6},{5,7},{6,0},{7,1},{8,10},{9,11},{10,... | collective-permute-start | bytes 786440 | tf_op jit(solution)/shard_map/ppermute | solution.py:65
  10.9 18.4 %collective-permute-start.1 = (bf16[1024,128]{1,0:T(8,128)(2,1)}, bf16[1024,128]{1,0:T(8,128)(2,1)S(1)}, u32[]{:S(2)}, u32[]{:S(2)}) collective-permute-start(bf16[1024,128]{1,0:T(8,128)(2,1)} %refs_1_.6), channel_id=1, source_target_pairs={{0,6},{1,7},{2,0},{3,1},{4,2},{5,3},{6,4},{7,5},{8,14},{9,15},{10,... | collective-permute-start | bytes 786440 | tf_op jit(solution)/shard_map/ppermute | solution.py:65
  12.2 23.8 %collective-permute-start.4 = (bf16[1024,128]{1,0:T(8,128)(2,1)}, bf16[1024,128]{1,0:T(8,128)(2,1)S(1)}, u32[]{:S(2)}, u32[]{:S(2)}) collective-permute-start(bf16[1024,128]{1,0:T(8,128)(2,1)} %refs_1_.6), channel_id=1, source_target_pairs={{0,1},{1,0},{2,3},{3,2},{4,5},{5,4},{6,7},{7,6},{8,9},{9,8},{10,11... | collective-permute-start | bytes 786440 | tf_op jit(solution)/shard_map/ppermute | solution.py:65
  28.3 5.6 %collective-permute-start.2 = (bf16[512,128]{1,0:T(8,128)(2,1)S(1)}, bf16[512,128]{1,0:T(8,128)(2,1)S(1)}, u32[]{:S(2)}, u32[]{:S(2)}) collective-permute-start(bf16[512,128]{1,0:T(8,128)(2,1)S(1)} %slice.12), channel_id=1, source_target_pairs={{0,2},{1,3},{2,4},{3,5},{4,6},{5,7},{6,0},{7,1},{8,10},{9,11},{10,... | collective-permute-start | bytes 393224 | tf_op jit(solution)/shard_map/ppermute | solution.py:65
  28.4 7.6 %collective-permute-start.5 = (bf16[1024,128]{1,0:T(8,128)(2,1)S(1)}, bf16[1024,128]{1,0:T(8,128)(2,1)S(1)}, u32[]{:S(2)}, u32[]{:S(2)}) collective-permute-start(bf16[1024,128]{1,0:T(8,128)(2,1)S(1)} %collective-permute-done.refs_2_), channel_id=1, source_target_pairs={{0,1},{1,0},{2,3},{3,2},{4,5},{5,4},{6,7},{7,6},{8,9},{9,8},{10,11... | collective-permute-start | bytes 786440 | tf_op jit(solution)/shard_map/ppermute | solution.py:65
  29.3 6.8 %collective-permute-start.6 = (bf16[1024,128]{1,0:T(8,128)(2,1)S(1)}, bf16[1024,128]{1,0:T(8,128)(2,1)S(1)}, u32[]{:S(2)}, u32[]{:S(2)}) collective-permute-start(bf16[1024,128]{1,0:T(8,128)(2,1)S(1)} %collective-permute-done.1.refs_3_), channel_id=1, source_target_pairs={{0,1},{1,0},{2,3},{3,2},{4,5},{5,4},{6,7},{7,6},{8,9},{9,8},{10,11... | collective-permute-start | bytes 786440 | tf_op jit(solution)/shard_map/ppermute | solution.py:65
  29.4 6.1 %collective-permute-start.3 = (bf16[512,128]{1,0:T(8,128)(2,1)S(1)}, bf16[512,128]{1,0:T(8,128)(2,1)S(1)}, u32[]{:S(2)}, u32[]{:S(2)}) collective-permute-start(bf16[512,128]{1,0:T(8,128)(2,1)S(1)} %slice.13), channel_id=1, source_target_pairs={{0,6},{1,7},{2,0},{3,1},{4,2},{5,3},{6,4},{7,5},{8,14},{9,15},{10,... | collective-permute-start | bytes 393224 | tf_op jit(solution)/shard_map/ppermute | solution.py:65
  33.9 2.6 %collective-permute-start.7 = (bf16[512,128]{1,0:T(8,128)(2,1)S(1)}, bf16[512,128]{1,0:T(8,128)(2,1)S(1)}, u32[]{:S(2)}, u32[]{:S(2)}) collective-permute-start(bf16[512,128]{1,0:T(8,128)(2,1)S(1)} %collective-permute-done.2.refs_4_), channel_id=1, source_target_pairs={{0,1},{1,0},{2,3},{3,2},{4,5},{5,4},{6,7},{7,6},{8,9},{9,8},{10,11... | collective-permute-start | bytes 393224 | tf_op jit(solution)/shard_map/ppermute | solution.py:65
  35.5 12.8 %copy-start.5 = (bf16[512,128]{1,0:T(8,128)(2,1)}, bf16[512,128]{1,0:T(8,128)(2,1)S(1)}, u32[]{:S(2)}) copy-start(bf16[512,128]{1,0:T(8,128)(2,1)S(1)} %collective-permute-done.3.refs_5_) | copy-start | bytes 393220
  35.5 1.5 %collective-permute-start.8 = (bf16[512,128]{1,0:T(8,128)(2,1)S(1)}, bf16[512,128]{1,0:T(8,128)(2,1)S(1)}, u32[]{:S(2)}, u32[]{:S(2)}) collective-permute-start(bf16[512,128]{1,0:T(8,128)(2,1)S(1)} %collective-permute-done.3.refs_5_), channel_id=1, source_target_pairs={{0,1},{1,0},{2,3},{3,2},{4,5},{5,4},{6,7},{7,6},{8,9},{9,8},{10,11... | collective-permute-start | bytes 393224 | tf_op jit(solution)/shard_map/ppermute | solution.py:65
  36.5 11.8 %copy-start.7 = (bf16[512,128]{1,0:T(8,128)(2,1)}, bf16[512,128]{1,0:T(8,128)(2,1)S(1)}, u32[]{:S(2)}) copy-start(bf16[512,128]{1,0:T(8,128)(2,1)S(1)} %collective-permute-done.7.refs_9_) | copy-start | bytes 393220
  37.0 11.3 %copy-start.9 = (bf16[512,128]{1,0:T(8,128)(2,1)}, bf16[512,128]{1,0:T(8,128)(2,1)S(1)}, u32[]{:S(2)}) copy-start(bf16[512,128]{1,0:T(8,128)(2,1)S(1)} %collective-permute-done.8.refs_10_) | copy-start | bytes 393220
  37.0 1.0 copy-start.1
  40.8 21.9 %all-to-all-start.1 = ((bf16[8,176,128]{2,1,0:T(8,128)(2,1)}), bf16[8,176,128]{2,1,0:T(8,128)(2,1)S(1)}, u32[]{:S(2)}, u32[]{:S(2)}) async-start(bf16[8,176,128]{2,1,0:T(8,128)(2,1)} %get-tuple-element.16), calls=%async_computation.1 | async-start | bytes 720896 | tf_op jit(solution)/shard_map/all_to_all | solution.py:57
  48.3 1.0 copy-start.2
  49.3 0.9 copy-start.6
  50.2 0.9 copy-start.8
  51.1 0.9 copy-start.10
  55.0 0.9 copy-start.3
  55.9 0.8 copy-start.12
  62.7 41.1 %copy-start.4 = (bf16[384,1024]{1,0:T(8,128)(2,1)S(1)}, bf16[384,1024]{1,0:T(8,128)(2,1)}, u32[]{:S(2)}) copy-start(bf16[384,1024]{1,0:T(8,128)(2,1)} %copy-done.3) | copy-start | bytes 2359300
  74.1 7.2 %collective-permute-start.11 = (bf16[1024,128]{1,0:T(8,128)(2,1)S(1)}, bf16[1024,128]{1,0:T(8,128)(2,1)S(1)}, u32[]{:S(2)}, u32[]{:S(2)}) collective-permute-start(bf16[1024,128]{1,0:T(8,128)(2,1)S(1)} %bitcast.7), channel_id=1, source_target_pairs={{0,6},{1,7},{2,0},{3,1},{4,2},{5,3},{6,4},{7,5},{8,14},{9,15},{10,... | collective-permute-start | bytes 786440 | tf_op jit(solution)/shard_map/ppermute | solution.py:65
  77.6 26.2 %collective-permute-start.9 = (bf16[2064,128]{1,0:T(8,128)(2,1)}, bf16[2064,128]{1,0:T(8,128)(2,1)S(1)}, u32[]{:S(2)}, u32[]{:S(2)}) collective-permute-start(bf16[2064,128]{1,0:T(8,128)(2,1)} %copy-done.12), channel_id=1, source_target_pairs={{14,6},{15,7},{22,14},{23,15},{30,22},{31,23},{38,30},{39,31},{46,... | collective-permute-start | bytes 1585160 | tf_op jit(solution)/shard_map/ppermute | solution.py:380
  78.3 14.8 %collective-permute-start.10 = (bf16[1024,128]{1,0:T(8,128)(2,1)S(1)}, bf16[1024,128]{1,0:T(8,128)(2,1)S(1)}, u32[]{:S(2)}, u32[]{:S(2)}) collective-permute-start(bf16[1024,128]{1,0:T(8,128)(2,1)S(1)} %bitcast.8), channel_id=1, source_target_pairs={{0,2},{1,3},{2,4},{3,5},{4,6},{5,7},{6,0},{7,1},{8,10},{9,11},{10,... | collective-permute-start | bytes 786440 | tf_op jit(solution)/shard_map/ppermute | solution.py:65
  81.3 12.0 %collective-permute-start.12 = (bf16[1024,128]{1,0:T(8,128)(2,1)S(1)}, bf16[1024,128]{1,0:T(8,128)(2,1)}, u32[]{:S(2)}, u32[]{:S(2)}) collective-permute-start(bf16[1024,128]{1,0:T(8,128)(2,1)S(1)} %collective-permute-done.11.refs_6_), channel_id=1, source_target_pairs={{0,6},{1,7},{2,0},{3,1},{4,2},{5,3},{6,4},{7,5},{8,14},{9,15},{10,... | collective-permute-start | bytes 786440 | tf_op jit(solution)/shard_map/ppermute | solution.py:65
  86.2 12.9 %all-to-all-start.3 = ((bf16[8,128,128]{2,1,0:T(8,128)(2,1)}), bf16[8,128,128]{2,1,0:T(8,128)(2,1)S(1)}, u32[]{:S(2)}, u32[]{:S(2)}) async-start(bf16[8,128,128]{2,1,0:T(8,128)(2,1)} %shard_map.90), calls=%async_computation.3 | async-start | bytes 524288 | tf_op jit(solution)/shard_map/all_to_all | solution.py:57
  92.6 11.2 %collective-permute-start.13 = (bf16[1024,128]{1,0:T(8,128)(2,1)S(1)}, bf16[1024,128]{1,0:T(8,128)(2,1)S(1)}, u32[]{:S(2)}, u32[]{:S(2)}) collective-permute-start(bf16[1024,128]{1,0:T(8,128)(2,1)S(1)} %bitcast.9), channel_id=1, source_target_pairs={{0,1},{1,0},{2,3},{3,2},{4,5},{5,4},{6,7},{7,6},{8,9},{9,8},{10,11... | collective-permute-start | bytes 786440 | tf_op jit(solution)/shard_map/ppermute | solution.py:65
  92.8 11.0 %collective-permute-start.15 = (bf16[1024,128]{1,0:T(8,128)(2,1)S(1)}, bf16[1024,128]{1,0:T(8,128)(2,1)S(1)}, u32[]{:S(2)}, u32[]{:S(2)}) collective-permute-start(bf16[1024,128]{1,0:T(8,128)(2,1)S(1)} %collective-permute-done.11.refs_6_), channel_id=1, source_target_pairs={{0,1},{1,0},{2,3},{3,2},{4,5},{5,4},{6,7},{7,6},{8,9},{9,8},{10,11... | collective-permute-start | bytes 786440 | tf_op jit(solution)/shard_map/ppermute | solution.py:65
  93.1 10.7 %collective-permute-start.14 = (bf16[1024,128]{1,0:T(8,128)(2,1)S(1)}, bf16[1024,128]{1,0:T(8,128)(2,1)S(1)}, u32[]{:S(2)}, u32[]{:S(2)}) collective-permute-start(bf16[1024,128]{1,0:T(8,128)(2,1)S(1)} %collective-permute-done.10.refs_5_), channel_id=1, source_target_pairs={{0,1},{1,0},{2,3},{3,2},{4,5},{5,4},{6,7},{7,6},{8,9},{9,8},{10,11... | collective-permute-start | bytes 786440 | tf_op jit(solution)/shard_map/ppermute | solution.py:65
  93.3 10.5 %collective-permute-start.16 = (bf16[1024,128]{1,0:T(8,128)(2,1)}, bf16[1024,128]{1,0:T(8,128)(2,1)}, u32[]{:S(2)}, u32[]{:S(2)}) collective-permute-start(bf16[1024,128]{1,0:T(8,128)(2,1)} %collective-permute-done.12.refs_7_), channel_id=1, source_target_pairs={{0,1},{1,0},{2,3},{3,2},{4,5},{5,4},{6,7},{7,6},{8,9},{9,8},{10,11... | collective-permute-start | bytes 786440 | tf_op jit(solution)/shard_map/ppermute | solution.py:65
  99.1 3.4 %copy-start = (bf16[4,1024,1024]{2,1,0:T(8,128)(2,1)S(1)}, bf16[4,1024,1024]{2,1,0:T(8,128)(2,1)}, u32[]{:S(2)}) copy-start(bf16[4,1024,1024]{2,1,0:T(8,128)(2,1)} %refs_1_.7) | copy-start | bytes 25165828
